TPU v7x, 32 devices: a whole 2x2x4 slice. The times are simulated.
32 devices in a mesh: dp: 8 (over z, y), seq: 4 (over x, core).
Axes of the slice: x: 2, y: 2, z: 4, core: 2. Of those that a mesh axis runs over, the one named last changes fastest.
Arguments:
- mel_frames: bfloat16 [8, 3072, 80], P('dp', 'seq'), may hold values from -6 to 6
- token_ids: int32 [8, 448], P('dp', 'seq'), may hold values from 0 to 26111
- token_counts: int32 [8], P('dp'), may hold values from 1 to 448, as said below
- conv1_weight: bfloat16 [3, 80, 768], P(None, 'seq', 'dp'), may hold values from -0.375 to 0.375
- conv2_weight: bfloat16 [3, 768, 768], P(None, 'dp', 'seq'), may hold values from -0.125 to 0.125
- encoder_attn_gain: bfloat16 [768], P(('dp', 'seq')), may hold values from 0.099609375 to 1.8984375
- encoder_attn_bias: bfloat16 [768], P(('dp', 'seq')), may hold values from -1.5 to 1.5
- encoder_query: bfloat16 [768, 768], P('dp', 'seq'), may hold values from -0.21875 to 0.21875
- encoder_key: bfloat16 [768, 768], P('dp', 'seq'), may hold values from -0.21875 to 0.21875
- encoder_value: bfloat16 [768, 768], P('dp', 'seq'), may hold values from -0.21875 to 0.21875
- encoder_output: bfloat16 [768, 768], P('dp', 'seq'), may hold values from -0.875 to 0.875
- encoder_mlp_gain: bfloat16 [768], P(('dp', 'seq')), may hold values from 0.099609375 to 1.8984375
- encoder_mlp_bias: bfloat16 [768], P(('dp', 'seq')), may hold values from -1.5 to 1.5
- encoder_expand: bfloat16 [768, 3072], P('dp', 'seq'), may hold values from -0.21875 to 0.21875
- encoder_contract: bfloat16 [3072, 768], P('dp', 'seq'), may hold values from -0.109375 to 0.109375
- encoder_final_gain: bfloat16 [768], P(('dp', 'seq')), may hold values from 0.099609375 to 1.8984375
- encoder_final_bias: bfloat16 [768], P(('dp', 'seq')), may hold values from -1.5 to 1.5
- token_table: bfloat16 [26112, 768], P('dp', 'seq'), may hold values from -5 to 5
- position_table: bfloat16 [448, 768], P('dp', 'seq'), may hold values from -2.5 to 2.5
- decoder_attn_gain: bfloat16 [768], P(('dp', 'seq')), may hold values from 0.099609375 to 1.8984375
- decoder_attn_bias: bfloat16 [768], P(('dp', 'seq')), may hold values from -1.5 to 1.5
- decoder_query: bfloat16 [768, 768], P('dp', 'seq'), may hold values from -0.21875 to 0.21875
- decoder_key: bfloat16 [768, 768], P('dp', 'seq'), may hold values from -0.21875 to 0.21875
- decoder_value: bfloat16 [768, 768], P('dp', 'seq'), may hold values from -0.21875 to 0.21875
- decoder_output: bfloat16 [768, 768], P('dp', 'seq'), may hold values from -0.625 to 0.625
- cross_attn_gain: bfloat16 [768], P(('dp', 'seq')), may hold values from 0.099609375 to 1.8984375
- cross_attn_bias: bfloat16 [768], P(('dp', 'seq')), may hold values from -1.5 to 1.5
- cross_query: bfloat16 [768, 768], P('dp', 'seq'), may hold values from -0.21875 to 0.21875
- cross_key: bfloat16 [768, 768], P('dp', 'seq'), may hold values from -0.21875 to 0.21875
- cross_value: bfloat16 [768, 768], P('dp', 'seq'), may hold values from -0.21875 to 0.21875
- cross_output: bfloat16 [768, 768], P('dp', 'seq'), may hold values from -0.875 to 0.875
- decoder_mlp_gain: bfloat16 [768], P(('dp', 'seq')), may hold values from 0.099609375 to 1.8984375
- decoder_mlp_bias: bfloat16 [768], P(('dp', 'seq')), may hold values from -1.5 to 1.5
- decoder_expand: bfloat16 [768, 3072], P('dp', 'seq'), may hold values from -0.21875 to 0.21875
- decoder_contract: bfloat16 [3072, 768], P('dp', 'seq'), may hold values from -0.109375 to 0.109375
- cotangent: bfloat16 [8, 448, 768], P('dp', 'seq'), may hold values from -6 to 6
Outputs:
- decoded: bfloat16 [8, 448, 768], P('dp', 'seq')
- mel_grad: float32 [8, 3072, 80], P('dp', 'seq')
- grad_conv1_weight: float32 [3, 80, 768], P(None, 'seq', 'dp')
- grad_conv2_weight: float32 [3, 768, 768], P(None, 'dp', 'seq')
- grad_encoder_attn_gain: float32 [768], P(('dp', 'seq'))
- grad_encoder_attn_bias: float32 [768], P(('dp', 'seq'))
- grad_encoder_query: float32 [768, 768], P('dp', 'seq')
- grad_encoder_key: float32 [768, 768], P('dp', 'seq')
- grad_encoder_value: float32 [768, 768], P('dp', 'seq')
- grad_encoder_output: float32 [768, 768], P('dp', 'seq')
- grad_encoder_mlp_gain: float32 [768], P(('dp', 'seq'))
- grad_encoder_mlp_bias: float32 [768], P(('dp', 'seq'))
- grad_encoder_expand: float32 [768, 3072], P('dp', 'seq')
- grad_encoder_contract: float32 [3072, 768], P('dp', 'seq')
- grad_encoder_final_gain: float32 [768], P(('dp', 'seq'))
- grad_encoder_final_bias: float32 [768], P(('dp', 'seq'))
- grad_token_table: float32 [26112, 768], P('dp', 'seq')
- grad_position_table: float32 [448, 768], P('dp', 'seq')
- grad_decoder_attn_gain: float32 [768], P(('dp', 'seq'))
- grad_decoder_attn_bias: float32 [768], P(('dp', 'seq'))
- grad_decoder_query: float32 [768, 768], P('dp', 'seq')
- grad_decoder_key: float32 [768, 768], P('dp', 'seq')
- grad_decoder_value: float32 [768, 768], P('dp', 'seq')
- grad_decoder_output: float32 [768, 768], P('dp', 'seq')
- grad_cross_attn_gain: float32 [768], P(('dp', 'seq'))
- grad_cross_attn_bias: float32 [768], P(('dp', 'seq'))
- grad_cross_query: float32 [768, 768], P('dp', 'seq')
- grad_cross_key: float32 [768, 768], P('dp', 'seq')
- grad_cross_value: float32 [768, 768], P('dp', 'seq')
- grad_cross_output: float32 [768, 768], P('dp', 'seq')
- grad_decoder_mlp_gain: float32 [768], P(('dp', 'seq'))
- grad_decoder_mlp_bias: float32 [768], P(('dp', 'seq'))
- grad_decoder_expand: float32 [768, 3072], P('dp', 'seq')
- grad_decoder_contract: float32 [3072, 768], P('dp', 'seq')
Inputs may be any that keep to these rules, and one draw needn't show every extreme that they name: `token_counts`: each clip's number of live decoder slots; in every draw some clip has 448.
All inputs are finite; a program needn't handle non-finite values.
Results may differ from a plain program's by a relative error of at most 0.03.
Values may be sent and summed in bfloat16 or wider, within the bound.
A program may use at most 576 MiB of HBM per device.

v0:
```python
import functools
import math

import jax
import jax.numpy as jnp
from jax import lax
from jax.experimental import pallas as pl
from jax.experimental.pallas import tpu as pltpu
from jax.sharding import PartitionSpec as P

D = 768
HEADS = 12
HEAD = 64
EPSILON = 1e-05
NEGATIVE = -1e30
SCALE = 1.0 / math.sqrt(HEAD)
BF = jnp.bfloat16
F32 = jnp.float32
BOTH = ("dp", "seq")

KINDS = "12vvmmmmvvmmvvtmvvmmmmvvmmmmvvmm"


def dot(a, b, ca, cb, out=F32):
    return lax.dot_general(a, b, (((ca,), (cb,)), ((), ())), preferred_element_type=F32).astype(out)


def mm(a, b, out=F32):
    return dot(a, b, 1, 0, out)


def mm_t(a, b, out=F32):
    return dot(a, b, 1, 1, out)


def outer(a, b, out=BF):
    return dot(a, b, 0, 0, out)


def norm_parts(values):
    center = values - jnp.mean(values, axis=-1, keepdims=True)
    spread = jnp.mean(center * center, axis=-1, keepdims=True)
    inv = lax.rsqrt(spread + EPSILON)
    return center * inv, inv


def norm(values, gain, bias):
    return (norm_parts(values)[0] * gain + bias).astype(BF)


def norm_back(values, gain, up):
    hat, inv = norm_parts(values)
    g = up * gain
    back = inv * (
        g - jnp.mean(g, axis=-1, keepdims=True) - hat * jnp.mean(g * hat, axis=-1, keepdims=True)
    )
    return back, jnp.sum(up * hat, axis=0), jnp.sum(up, axis=0)


def gelu(v):
    return v * (0.5 + 0.5 * lax.erf(v * math.sqrt(0.5)))


def gelu_slope(v):
    return (0.5 + 0.5 * lax.erf(v * math.sqrt(0.5))) + v * jnp.exp(-0.5 * v * v) * (
        1.0 / math.sqrt(2.0 * math.pi)
    )


def mlp(normed, expand, contract):
    wide = expand.shape[2]
    pre, hidden, out = [], [], 0.0
    for s in range(expand.shape[0]):
        pre.append(mm(normed, expand[s]))
        hidden.append(gelu(pre[s]).astype(BF))
        out = out + mm(hidden[s], contract[s * wide : (s + 1) * wide])
    return pre, hidden, out


def low(v):
    return lax.reduce_precision(v, 8, 7)


def heads(v):
    return v.reshape(v.shape[0], HEADS, HEAD)


def bdot(a, b, ca, cb, ba, bb):
    return lax.dot_general(a, b, (((ca,), (cb,)), ((ba,), (bb,))), preferred_element_type=F32)


def scores_of(q, k, allowed):
    s = bdot(heads(q), heads(k), 2, 2, 1, 1)
    return s if allowed is None else jnp.where(allowed, s, NEGATIVE)


def attend(q, k, v, allowed=None):
    s = scores_of(q, k, allowed)
    top = jnp.max(s, axis=-1, keepdims=True)
    e = jnp.exp(s - top)
    total = jnp.sum(e, axis=-1, keepdims=True)
    o = bdot((e / total).astype(BF), heads(v), 2, 0, 0, 1)
    o = o.transpose(1, 0, 2).reshape(q.shape)
    return o, (top + jnp.log(total))[..., 0].T


def attend_back(q, k, v, allowed, lse, up, total=lambda v: v):
    s = scores_of(q, k, allowed)
    p = jnp.exp(s - lse.T[:, :, None])
    dv = bdot(p.astype(BF), heads(up), 1, 0, 0, 1)
    dp = bdot(heads(up), heads(v), 2, 2, 1, 1)
    mass = total(jnp.sum(p, axis=-1, keepdims=True))
    inner = total(jnp.sum(p * dp, axis=-1, keepdims=True)) / mass
    ds = (p * (dp - inner)).astype(BF)
    dq = bdot(ds, heads(k), 2, 0, 0, 1)
    dk = bdot(ds, heads(q), 1, 0, 0, 1)
    flat = lambda a, like: a.transpose(1, 0, 2).reshape(like.shape)
    return flat(dq, q), flat(dk, k), flat(dv, v)


def pack(rows, extras):
    cols = [rows.astype(F32)] + extras
    wide = sum(c.shape[1] for c in cols)
    return jnp.concatenate(cols + [jnp.zeros((rows.shape[0], -wide % 128), F32)], axis=1)


def unpack(packed, count):
    return packed[..., :D], [
        packed[..., D + i * HEADS : D + (i + 1) * HEADS] for i in range(count)
    ]


def shift(v, axis, step):
    n = lax.axis_size(axis)
    return lax.ppermute(v, axis, [(i, i + step) for i in range(n) if 0 <= i + step < n])


def extended(x, width):
    before = shift(x[-width:], "seq", 1)
    after = shift(x[:width], "seq", -1)
    return jnp.concatenate([before, x, after], axis=0)


def exchange(v):
    n = lax.axis_size("seq")
    got = lax.all_to_all(v, "seq", split_axis=0, concat_axis=0, tiled=True)
    return got.reshape(n, v.shape[0] // n, v.shape[1])


def sinusoid(first_frame, frame_count):
    half = D // 2
    frequency = jnp.exp(jnp.arange(half).astype(F32) * (-math.log(10000.0) / (half - 1)))
    places = (first_frame + jnp.arange(frame_count)).astype(F32)
    angles = places[:, None] * frequency[None, :]
    return jnp.concatenate([jnp.sin(angles), jnp.cos(angles)], axis=1)


def to_whole(flat, shape, kind, dps, seqs):
    if kind == "v":
        return flat.reshape(-1)
    if kind == "1":
        t, i, o = shape
        return (
            flat.reshape(dps, seqs, t, i, o)
            .transpose(2, 1, 3, 0, 4)
            .reshape(t, seqs * i, dps * o)
        )
    if kind == "2":
        t, i, o = shape
        return (
            flat.reshape(dps, seqs, t, i, o)
            .transpose(2, 0, 3, 1, 4)
            .reshape(t, dps * i, seqs * o)
        )
    r, c = shape
    return flat.reshape(dps, seqs, r, c).transpose(0, 2, 1, 3).reshape(dps * r, seqs * c)


def to_owner(g, kind, dps, seqs):
    n = dps * seqs
    if kind == "v":
        return g.reshape(n, -1)
    if kind == "1":
        t, i, o = g.shape
        g = g.reshape(t, seqs, i // seqs, dps, o // dps).transpose(3, 1, 0, 2, 4)
    elif kind == "2":
        t, i, o = g.shape
        g = g.reshape(t, dps, i // dps, seqs, o // seqs).transpose(1, 3, 0, 2, 4)
    else:
        r, c = g.shape
        g = g.reshape(dps, r // dps, seqs, c // seqs).transpose(0, 2, 1, 3)
    return g.reshape(n, -1)


def gather_plain(shards):
    dps, seqs = lax.axis_size("dp"), lax.axis_size("seq")
    flat = jnp.concatenate([w.reshape(-1) for w in shards if w is not None])
    got = lax.all_gather(flat[None], BOTH, axis=0, tiled=True)
    out, at = [], 0
    for w, kind in zip(shards, KINDS):
        if w is None:
            out.append(None)
            continue
        out.append(to_whole(got[:, at : at + w.size], w.shape, kind, dps, seqs))
        at += w.size
    for i in BROAD:
        out[i] = out[i].reshape(D, seqs, -1).transpose(1, 0, 2)
    return out


def reduce_plain(grads, shards):
    dps, seqs = lax.axis_size("dp"), lax.axis_size("seq")
    grads = list(grads)
    for i in BROAD:
        grads[i] = grads[i].transpose(1, 0, 2).reshape(D, -1)
    flat = jnp.concatenate(
        [to_owner(g.astype(BF), k, dps, seqs) for g, k in zip(grads, KINDS) if g is not None], axis=1
    )
    own = lax.psum_scatter(flat, BOTH, scatter_dimension=0, tiled=True).astype(F32)[0]
    out, at = [], 0
    for w, g in zip(shards, grads):
        if g is None:
            out.append(None)
            continue
        out.append(own[at : at + w.size].reshape(w.shape))
        at += w.size
    return out


MESH = pl.DeviceIdType.MESH
LANES = 384


def where_am_i():
    d, s = lax.axis_index("dp"), lax.axis_index("seq")
    return d // 2, d % 2, s // 2, s % 2


def partners(z, y, x, c):
    at = lambda z, y, x, c: (z * 2 + y, x * 2 + c)
    zs = [at((z + j) % 4, y, x, c) for j in (1, 2, 3)]
    return zs, at(z, 1 - y, x, c), at(z, y, 1 - x, c), at(z, y, x, 1 - c)


def greet(zs, yp, xp, cp):
    barrier = pltpu.get_barrier_semaphore()
    everyone = zs + [yp, xp, cp]
    for dev in everyone:
        pl.semaphore_signal(barrier, inc=1, device_id=dev, device_id_type=MESH)
    pl.semaphore_wait(barrier, len(everyone))


def remote(src, dst, send, recv, dev):
    return pltpu.make_async_remote_copy(
        src_ref=src, dst_ref=dst, send_sem=send, recv_sem=recv, device_id=dev, device_id_type=MESH
    )


def split_at(i, rows):
    return rows // 2 if rows % 32 == 0 else 16 + 16 * (i % 2)


def lanes(x):
    return pl.ds(pl.multiple_of(x * LANES, LANES), LANES)


def spot(ref, wide, zs, ys, xs, c, rs):
    full = lambda v: slice(None) if v is None else v
    if wide:
        return ref.at[full(xs), c, full(zs), full(ys), rs, :]
    return ref.at[full(zs), full(ys), c, rs, slice(None) if xs is None else lanes(xs)]


def gather_kernel(plan, *refs):
    inputs = 1 + max(p[0] for p in plan)
    outputs = 1 + max(p[3] for p in plan)
    ins, outs = refs[:inputs], refs[inputs : inputs + outputs]
    lsem, zsend, zrecv, xsend, xrecv, ysend, yrecv, csend, crecv = refs[inputs + outputs :]
    z, y, x, c = where_am_i()
    zs, yp, xp, cp = partners(z, y, x, c)
    greet(zs, yp, xp, cp)
    n = len(plan)
    started = [[] for _ in range(n)]
    dst = []
    for src, first, rows, out, tap, wide in plan:
        dst.append(outs[out] if tap is None else outs[out].at[tap])

    def item(i):
        _, _, rows, _, _, wide = plan[i]
        h = split_at(i, rows)
        return rows, wide, slice(0, h), slice(h, rows)

    stages = {}

    def start(i, key, copies):
        for cpy in copies:
            cpy.start()
        stages[i, key] = copies

    def send_z(i):
        src, first, rows, _, _, wide = plan[i]
        block = ins[src].at[first : first + rows]
        here = spot(dst[i], wide, z, y, x, c, slice(None))
        start(i, 0, [remote(block, here, zsend.at[i, j], zrecv.at[i, j], zs[j]) for j in range(3)])
        start(i, 4, [pltpu.make_async_copy(block, here, lsem.at[i])])

    def send_1(i):
        rows, wide, a, b = item(i)
        for cpy in stages[i, 0]:
            cpy.wait_recv()
        stages[i, 4][0].wait()
        ax = spot(dst[i], wide, None, y, x, c, a)
        by = spot(dst[i], wide, None, y, x, c, b)
        start(
            i,
            1,
            [
                remote(ax, ax, xsend.at[i, 0], xrecv.at[i, 0], xp),
                remote(by, by, ysend.at[i, 0], yrecv.at[i, 0], yp),
            ],
        )

    def send_2(i):
        rows, wide, a, b = item(i)
        for cpy in stages[i, 1]:
            cpy.wait_recv()
        ay = spot(dst[i], wide, None, y, None, c, a)
        bx = spot(dst[i], wide, None, None, x, c, b)
        start(
            i,
            2,
            [
                remote(ay, ay, ysend.at[i, 1], yrecv.at[i, 1], yp),
                remote(bx, bx, xsend.at[i, 1], xrecv.at[i, 1], xp),
            ],
        )

    def send_core(i):
        rows, wide, a, b = item(i)
        for cpy in stages[i, 2]:
            cpy.wait_recv()
        half = spot(dst[i], wide, None, None, None, c, slice(None))
        start(i, 3, [remote(half, half, csend.at[i], crecv.at[i], cp)])

    for t in range(n + AHEAD[2]):
        if t == 0:
            for i in range(min(n, AHEAD[3])):
                send_z(i)
        if t + AHEAD[3] < n:
            send_z(t + AHEAD[3])
        if 0 <= t - AHEAD[0] < n:
            send_1(t - AHEAD[0])
        if 0 <= t - AHEAD[1] < n:
            send_2(t - AHEAD[1])
        if 0 <= t - AHEAD[2] < n:
            send_core(t - AHEAD[2])
    for i in range(n):
        stages[i, 3][0].wait_recv()
        for key in range(4):
            for cpy in stages[i, key]:
                cpy.wait_send()


AHEAD = (0, 1, 2, 4)


def gather_fast(plan, ins, out_shapes):
    n = len(plan)
    sem = pltpu.SemaphoreType.DMA
    hbm = pl.BlockSpec(memory_space=pl.ANY)
    return pl.pallas_call(
        functools.partial(gather_kernel, plan),
        out_shape=[jax.ShapeDtypeStruct(s, BF) for s in out_shapes],
        in_specs=[hbm] * len(ins),
        out_specs=[hbm] * len(out_shapes),
        scratch_shapes=[
            sem((n,)),
            sem((n, 3)),
            sem((n, 3)),
            sem((n, 2)),
            sem((n, 2)),
            sem((n, 2)),
            sem((n, 2)),
            sem((n,)),
            sem((n,)),
        ],
        compiler_params=pltpu.CompilerParams(collective_id=1, has_side_effects=True),
    )(*ins)


def add_into(dst, *srcs):
    lead = srcs[0].shape[:-2]
    total = math.prod(lead)

    def one(k, _):
        at = []
        for size in reversed(lead):
            at.append(lax.rem(k, size))
            k = lax.div(k, size)
        at = tuple(reversed(at))
        acc = srcs[0][at].astype(F32)
        for s in srcs[1:]:
            acc = acc + s[at].astype(F32)
        dst[at] = acc.astype(dst.dtype)
        return 0

    lax.fori_loop(0, total, one, 0)


def reduce_kernel(plan, *refs):
    inputs = 1 + max(p[0] for p in plan)
    outputs = 1 + max(p[4] for p in plan)
    n = len(plan)
    ins, refs = refs[:inputs], refs[inputs:]
    outs, refs = refs[:outputs], refs[outputs:]
    rc, refs = refs[:n], refs[n:]
    r1a, refs = refs[:n], refs[n:]
    r1b, refs = refs[:n], refs[n:]
    r2a, refs = refs[:n], refs[n:]
    r2b, refs = refs[:n], refs[n:]
    s3, refs = refs[:n], refs[n:]
    rz, refs = refs[:n], refs[n:]
    ring = {False: refs[0:2], True: refs[2:4]}
    refs = refs[4:]
    lsem, csend, crecv, xsend, xrecv, ysend, yrecv, zsend, zrecv = refs
    z, y, x, c = where_am_i()
    zs, yp, xp, cp = partners(z, y, x, c)
    greet(zs, yp, xp, cp)
    stages = {}

    def start(i, key, copies):
        for cpy in copies:
            cpy.start()
        stages[i, key] = copies

    def src(i):
        k, tap = plan[i][0], plan[i][1]
        return ins[k] if tap is None else ins[k].at[tap]

    def rows_of(i):
        r = plan[i][2]
        h = split_at(i, r)
        return plan[i][3], slice(0, h), slice(h, r), h, r

    kinds = {False: 0, True: 0}
    slot = []
    for p in plan:
        slot.append(kinds[p[3]] % 2)
        kinds[p[3]] += 1

    def own(i):
        wide, _, _, _, r = rows_of(i)
        buf = ring[wide][slot[i]]
        if wide:
            return buf.at[:, :, :, 0:r, :]
        return buf.at[:, :, 0:r, :]

    def send_core(i):
        wide, _, _, _, _ = rows_of(i)
        theirs = spot(src(i), wide, None, None, None, 1 - c, slice(None))
        start(i, 0, [remote(theirs, rc[i], csend.at[i], crecv.at[i], cp)])

    def load(i):
        wide, _, _, _, _ = rows_of(i)
        mine = spot(src(i), wide, None, None, None, c, slice(None))
        start(i, 5, [pltpu.make_async_copy(mine, own(i), lsem.at[i])])

    def send_1(i):
        wide, a, b, h, r = rows_of(i)
        stages[i, 5][0].wait()
        stages[i, 0][0].wait_recv()
        add_into(rc[i], own(i), rc[i])
        if wide:
            pa, pb = rc[i].at[:, :, 1 - y, a, :], rc[i].at[1 - x, :, :, b, :]
        else:
            pa, pb = rc[i].at[:, 1 - y, a, :], rc[i].at[:, :, b, lanes(1 - x)]
        start(
            i,
            1,
            [
                remote(pa, r1a[i], ysend.at[i, 0], yrecv.at[i, 0], yp),
                remote(pb, r1b[i], xsend.at[i, 0], xrecv.at[i, 0], xp),
            ],
        )

    def send_2(i):
        wide, a, b, h, r = rows_of(i)
        for cpy in stages[i, 1]:
            cpy.wait_recv()
        if wide:
            add_into(r1a[i], rc[i].at[:, :, y, a, :], r1a[i])
            add_into(r1b[i], rc[i].at[x, :, :, b, :], r1b[i])
            pa, pb = r1a[i].at[1 - x], r1b[i].at[:, 1 - y]
        else:
            add_into(r1a[i], rc[i].at[:, y, a, :], r1a[i])
            add_into(r1b[i], rc[i].at[:, :, b, lanes(x)], r1b[i])
            pa, pb = r1a[i].at[:, :, lanes(1 - x)], r1b[i].at[:, 1 - y]
        start(
            i,
            2,
            [
                remote(pa, r2a[i], xsend.at[i, 1], xrecv.at[i, 1], xp),
                remote(pb, r2b[i], ysend.at[i, 1], yrecv.at[i, 1], yp),
            ],
        )

    def send_z(i):
        wide, a, b, h, r = rows_of(i)
        for cpy in stages[i, 2]:
            cpy.wait_recv()
        keep = r1a[i].at[x] if wide else r1a[i].at[:, :, lanes(x)]
        add_into(s3[i].at[:, a, :], keep, r2a[i])
        add_into(s3[i].at[:, b, :], r1b[i].at[:, y], r2b[i])
        start(
            i,
            3,
            [
                remote(s3[i].at[(z + j + 1) % 4], rz[i].at[j], zsend.at[i, j], zrecv.at[i, j], zs[j])
                for j in range(3)
            ],
        )

    def finish(i):
        for cpy in stages[i, 3]:
            cpy.wait_recv()
        out, first, r = plan[i][4], plan[i][5], plan[i][2]
        acc = s3[i][z].astype(F32)
        for j in range(3):
            acc = acc + rz[i][j].astype(F32)
        outs[out][first : first + r, :] = acc

    for i in range(n):
        send_core(i)
    seen = {False: [], True: []}
    for i, p in enumerate(plan):
        seen[p[3]].append(i)
    for kind in (False, True):
        for i in seen[kind][:2]:
            load(i)
    for t in range(n + 3):
        if t < n:
            send_1(t)
            order = seen[plan[t][3]]
            k = order.index(t)
            if k + 2 < len(order):
                load(order[k + 2])
        if 0 <= t - 1 < n:
            send_2(t - 1)
        if 0 <= t - 2 < n:
            send_z(t - 2)
        if 0 <= t - 3 < n:
            finish(t - 3)
    for i in range(n):
        for key in range(4):
            for cpy in stages[i, key]:
                cpy.wait_send()


def reduce_fast(plan, ins, out_shapes):
    n = len(plan)
    sem = pltpu.SemaphoreType.DMA
    scratch = [[] for _ in range(7)]
    most = {False: 0, True: 0}
    for i, (_, _, r, wide, _, _) in enumerate(plan):
        h = split_at(i, r)
        most[wide] = max(most[wide], r)
        if wide:
            shapes = [
                (2, 4, 2, r, D),
                (2, 4, h, D),
                (4, 2, r - h, D),
                (4, h, D),
                (4, r - h, D),
                (4, r, D),
                (3, r, D),
            ]
        else:
            shapes = [
                (4, 2, r, D),
                (4, h, D),
                (4, 2, r - h, LANES),
                (4, h, LANES),
                (4, r - h, LANES),
                (4, r, LANES),
                (3, r, LANES),
            ]
        for group, shape in zip(scratch, shapes):
            group.append(pltpu.VMEM(shape, BF))
    scratch = [s for group in scratch for s in group]
    scratch += [pltpu.VMEM((4, 2, most[False], D), BF)] * 2
    scratch += [pltpu.VMEM((2, 4, 2, most[True], D), BF)] * 2
    scratch += [sem((n,)), sem((n,)), sem((n,))]
    scratch += [sem((n, 2)), sem((n, 2)), sem((n, 2)), sem((n, 2)), sem((n, 3)), sem((n, 3))]
    return pl.pallas_call(
        functools.partial(reduce_kernel, plan),
        out_shape=[jax.ShapeDtypeStruct(s, F32) for s in out_shapes],
        in_specs=[pl.BlockSpec(memory_space=pl.ANY)] * len(ins),
        out_specs=[pl.BlockSpec(memory_space=pltpu.VMEM)] * len(out_shapes),
        scratch_shapes=scratch,
        compiler_params=pltpu.CompilerParams(
            collective_id=2, has_side_effects=True, vmem_limit_bytes=60 << 20
        ),
    )(*ins)

SQUARE = (4, 5, 6, 7, 18, 19, 20, 21, 24, 25, 26, 27)
TALL = (11, 31)
BROAD = (10, 30)
VECTORS = tuple(i for i in range(32) if KINDS[i] == "v")
MISC_ROWS = 32
SWAP = ((0, 1), (1, 0), (2, 3), (3, 2))


def plans(shards):
    g, r, shapes, first = [], [], [], 0
    for i in SQUARE + (1,) + TALL:
        w = shards[i]
        rows = w.shape[-2] // 2
        one = (4, 2, 2, rows, D)
        for tap in range(w.shape[0]) if w.ndim == 3 else (None,):
            g.append((0, first, rows, len(shapes), tap, False))
            r.append((len(shapes), tap, rows, False, 0, first))
            first += rows
        shapes.append(one if w.ndim == 2 else (w.shape[0],) + one)
    at = 0
    for i in BROAD:
        rows = shards[i].shape[0]
        g.append((1, at, rows, len(shapes), None, True))
        r.append((len(shapes), None, rows, True, 1, at))
        at += rows
        shapes.append((2, 2, 4, 2, rows, D))
    g.append((2, 0, MISC_ROWS, len(shapes), None, True))
    r.append((len(shapes), None, MISC_ROWS, True, 2, 0))
    shapes.append((2, 2, 4, 2, MISC_ROWS, D))
    return g, r, shapes, first, at


def by_core(c, zero, one):
    return jnp.where(c == 0, zero, one)


def narrow_halves(shards):
    parts = []
    for i in SQUARE + (1,) + TALL:
        w = shards[i].reshape(-1, 2, shards[i].shape[-2] // 2, shards[i].shape[-1])
        parts += [w[t] for t in range(w.shape[0])]
    return jnp.concatenate(parts, axis=1)


def gather_weights(shards):
    c = lax.axis_index("seq") % 2
    g, _, shapes, _, _ = plans(shards)
    halves = narrow_halves(shards)
    mine = by_core(c, halves[0], halves[1])
    got = lax.ppermute(by_core(c, halves[1], halves[0]), "seq", SWAP)
    narrow = by_core(
        c, jnp.concatenate([mine, got], axis=1), jnp.concatenate([got, mine], axis=1)
    )
    broad = jnp.concatenate([shards[i] for i in BROAD], axis=0)
    flat = [shards[i].reshape(-1) for i in (0,) + VECTORS + (15,)]
    size = sum(f.size for f in flat)
    flat.append(jnp.zeros((MISC_ROWS * D - size,), BF))
    misc = jnp.concatenate(flat).reshape(MISC_ROWS, D)
    outs = gather_fast(g, [narrow, broad, misc], shapes)
    full = [None] * 32
    for k, i in enumerate(SQUARE + (1,) + TALL):
        full[i] = outs[k].reshape(shards[i].shape[:-2] + (8 * shards[i].shape[-2], D))
    for k, i in enumerate(BROAD):
        full[i] = outs[15 + k].reshape(4, D, D)
    misc = outs[17].reshape(2, 2, 4, 2, MISC_ROWS * D)
    at = 0
    t, a, b = shards[0].shape
    full[0] = (
        misc[..., : shards[0].size]
        .reshape(2, 2, 4, 2, t, a, b)
        .transpose(4, 0, 1, 5, 2, 3, 6)
        .reshape(t, 4 * a, 8 * b)
    )
    at += shards[0].size
    n = shards[VECTORS[0]].size
    vecs = misc[..., at : at + n * len(VECTORS)].reshape(2, 2, 4, 2, len(VECTORS), n)
    vecs = vecs.transpose(4, 2, 3, 0, 1, 5).reshape(len(VECTORS), D)
    for k, i in enumerate(VECTORS):
        full[i] = vecs[k]
    at += n * len(VECTORS)
    r, w = shards[15].shape
    full[15] = (
        misc[..., at : at + r * w]
        .reshape(2, 2, 4, 2, r, w)
        .transpose(2, 3, 4, 0, 1, 5)
        .reshape(8 * r, 4 * w)
    )
    return full


def reduce_grads(grads, shards):
    c = lax.axis_index("seq") % 2
    _, r, shapes, narrow_rows, broad_rows = plans(shards)
    ins = [grads[i].reshape(shapes[k]) for k, i in enumerate(SQUARE + (1,) + TALL + BROAD)]
    t, a, b = shards[0].shape
    conv1 = grads[0].reshape(t, 2, 2, a, 4, 2, b).transpose(1, 2, 4, 5, 0, 3, 6)
    n = shards[VECTORS[0]].size
    vecs = jnp.stack([grads[i] for i in VECTORS]).reshape(-1, 4, 2, 2, 2, n)
    flat = [conv1.reshape(2, 2, 4, 2, -1), vecs.transpose(3, 4, 1, 2, 0, 5).reshape(2, 2, 4, 2, -1)]
    size = sum(f.shape[-1] for f in flat)
    flat.append(jnp.zeros((2, 2, 4, 2, MISC_ROWS * D - size), F32))
    ins.append(jnp.concatenate(flat, axis=-1).astype(BF).reshape(shapes[-1]))
    narrow, broad, misc = reduce_fast(
        r, ins, [(narrow_rows, LANES), (broad_rows, D), (MISC_ROWS, D)]
    )
    half = LANES // 2
    mine = by_core(c, narrow[:, :half], narrow[:, half:])
    got = lax.ppermute(by_core(c, narrow[:, half:], narrow[:, :half]), "seq", SWAP)
    out, at = [None] * 32, 0
    for i in SQUARE + (1,) + TALL:
        w = shards[i]
        rows, taps = w.shape[-2] // 2, []
        for _ in range(w.shape[0] if w.ndim == 3 else 1):
            m, o = mine[at : at + rows], got[at : at + rows]
            taps.append(by_core(c, jnp.concatenate([m, o]), jnp.concatenate([o, m])))
            at += rows
        out[i] = taps[0] if w.ndim == 2 else jnp.stack(taps)
    at = 0
    for i in BROAD:
        out[i] = broad[at : at + shards[i].shape[0]]
        at += shards[i].shape[0]
    misc = misc.reshape(-1)
    out[0] = misc[: shards[0].size].reshape(shards[0].shape)
    at = shards[0].size
    for i in VECTORS:
        out[i] = misc[at : at + n]
        at += n
    return out


def one_hot(ids, table):
    first = lax.axis_index("dp") * table.shape[0]
    return ((ids - first)[:, None] == jnp.arange(table.shape[0])[None, :]).astype(BF)


def body(mel_frames, token_ids, token_counts, *rest):
    shards, cotangent = list(rest[:32]), rest[32][0]
    table = shards[14]
    dps, seqs = lax.axis_size("dp"), lax.axis_size("seq")
    me = lax.axis_index("seq")
    slots = token_ids.shape[1]
    all_slots = slots * seqs
    frames = mel_frames.shape[1] // 2

    ids = lax.all_gather(token_ids[0], BOTH, axis=0, tiled=True)
    hot = one_hot(ids, table)
    looked = mm(hot, table, BF)
    mine = lax.psum_scatter(looked, "dp", scatter_dimension=0, tiled=True)
    looked = lax.all_gather(mine, "seq", axis=0, tiled=True)
    looked = looked.reshape(seqs, all_slots, D // seqs).transpose(1, 0, 2).reshape(all_slots, D)

    weights = shards[:14] + [None] + shards[15:]
    fast = dps == 8 and seqs == 4
    full = gather_weights(weights) if fast else gather_plain(weights)
    vec = {i: full[i].astype(F32) for i in range(32) if KINDS[i] == "v"}
    conv1, conv2, position = full[0].reshape(-1, D), full[1], full[15]
    eq, ek, ev, eo = full[4:8]
    ee, ec = full[10:12]
    dq_w, dk_w, dv_w, do_w = full[18:22]
    cq_w, ck_w, cv_w, co_w = full[24:28]
    de, dc = full[30:32]

    pairs = extended(mel_frames[0], 2).reshape(frames + 2, -1)
    mels = mel_frames.shape[2]
    n = frames + 1
    even_in = jnp.concatenate([pairs[:n], pairs[1:, :mels]], axis=1)
    odd_in = jnp.concatenate([pairs[:n, mels:], pairs[1:]], axis=1)
    even_pre, odd_pre = mm(even_in, conv1), mm(odd_in, conv1)
    row = jnp.arange(n)[:, None]
    even_keep = (row > 0) | (me > 0)
    odd_keep = (row < n - 1) | (me < seqs - 1)
    even = jnp.where(even_keep, gelu(even_pre), 0.0).astype(BF)
    odd = jnp.where(odd_keep, gelu(odd_pre), 0.0).astype(BF)
    second_pre = mm(even[:frames], conv2[0]) + mm(odd[:frames], conv2[1]) + mm(even[1:], conv2[2])
    stream0 = gelu(second_pre) + sinusoid(me * frames, frames)

    enc_normed = norm(stream0, vec[2], vec[3])
    q = (mm(enc_normed, eq) * SCALE).astype(BF)
    k = mm(enc_normed, ek, BF)
    v = mm(enc_normed, ev, BF)
    kv = lax.all_gather(jnp.concatenate([k, v], axis=1), "seq", axis=0, tiled=True)
    k_all, v_all = kv[:, :D], kv[:, D:]
    enc_mixed, enc_lse = attend(q, k_all, v_all)
    enc_wide, enc_mixed = enc_mixed, enc_mixed.astype(BF)
    stream1 = stream0 + mm(enc_mixed, eo)
    enc_mlp_normed = norm(stream1, vec[8], vec[9])
    enc_pre, enc_hidden, out = mlp(enc_mlp_normed, ee, ec)
    stream2 = stream1 + out
    memory = norm(stream2, vec[12], vec[13])
    mk = mm(memory, ck_w, BF)
    mv = mm(memory, cv_w, BF)

    place = jnp.arange(all_slots)
    causal = (place[None, :] <= place[:, None]) & (place[None, :] < token_counts[0])
    embedded = looked.astype(F32) + position.astype(F32)
    dec_normed = norm(embedded, vec[16], vec[17])
    sq = (mm(dec_normed, dq_w) * SCALE).astype(BF)
    sk = mm(dec_normed, dk_w, BF)
    sv = mm(dec_normed, dv_w, BF)
    dec_mixed, dec_lse = attend(sq, sk, sv, causal)
    dec_wide, dec_mixed = dec_mixed, dec_mixed.astype(BF)
    stream4 = embedded + mm(dec_mixed, do_w)
    cross_normed = norm(stream4, vec[22], vec[23])
    xq = (mm(cross_normed, cq_w) * SCALE).astype(BF)

    part, part_lse = attend(xq, mk, mv)
    got = exchange(pack(part, [part_lse]))
    parts, (lses,) = unpack(got, 1)
    top = jnp.max(lses, axis=0)
    share = jnp.exp(lses - top)
    total = jnp.sum(share, axis=0)
    cross_lse = top + jnp.log(total)
    share = share / total
    cross_wide = jnp.sum(
        parts.reshape(seqs, slots, HEADS, HEAD) * share[..., None], axis=0
    ).reshape(slots, D)
    cross_mixed = cross_wide.astype(BF)

    own = lambda a: lax.dynamic_slice_in_dim(a, me * slots, slots, 0)
    stream4 = own(stream4)
    stream5 = stream4 + mm(cross_mixed, co_w)
    dec_mlp_normed = norm(stream5, vec[28], vec[29])
    dec_pre, dec_hidden, out = mlp(dec_mlp_normed, de, dc)
    stream6 = stream5 + out
    live = (own(place) < token_counts[0])[:, None]
    decoded = jnp.where(live, stream6, 0.0).astype(BF)

    grads = [None] * 32

    def mlp_back(ex, co, gain, normed, pre, hidden, stream, up):
        d_low = up.astype(BF)
        wide = normed.shape[1]
        first, second, total = [], [], 0.0
        for s in range(seqs):
            contract = full[co][s * wide : (s + 1) * wide]
            second.append(outer(hidden[s], d_low))
            d_pre = (gelu_slope(pre[s]) * low(mm_t(d_low, contract))).astype(BF)
            first.append(outer(normed, d_pre))
            total = total + mm_t(d_pre, full[ex][s])
        grads[co] = jnp.concatenate(second, axis=0)
        grads[ex] = jnp.stack(first)
        back, grads[gain], grads[gain + 1] = norm_back(stream, vec[gain], total)
        return up + back

    up = jnp.where(live, cotangent.astype(F32), 0.0)
    up = mlp_back(30, 31, 28, dec_mlp_normed, dec_pre, dec_hidden, stream5, up)
    d_low = up.astype(BF)
    grads[27] = outer(cross_mixed, d_low)
    d_mixed = mm_t(d_low, co_w, BF)
    sent = pack(d_mixed, [cross_lse])
    d_mixed, (lse_all,) = unpack(lax.all_gather(sent, "seq", axis=0, tiled=True), 1)
    dxq, dmk, dmv = attend_back(xq, mk, mv, None, lse_all, d_mixed.astype(BF), lambda v: lax.psum(v, "seq"))
    dxq = jnp.sum(exchange(dxq), axis=0)
    dxq = (low(dxq) * SCALE).astype(BF)
    grads[24] = outer(own(cross_normed), dxq)
    back, grads[22], grads[23] = norm_back(stream4, vec[22], mm_t(dxq, cq_w))
    up = up + back
    d_low = up.astype(BF)
    grads[21] = outer(own(dec_mixed), d_low)
    d_mixed = lax.all_gather(mm_t(d_low, do_w, BF), "seq", axis=0, tiled=True)
    dsq, dsk, dsv = attend_back(sq, sk, sv, causal, dec_lse, d_mixed)

    def inputs_back(first, gain, normed, stream, dq, dk, dv, up):
        dq = (low(dq) * SCALE).astype(BF)
        dk, dv = dk.astype(BF), dv.astype(BF)
        total = 0.0
        for i, g in enumerate((dq, dk, dv)):
            grads[first + i] = outer(normed, g)
            total = total + mm_t(g, full[first + i])
        back, grads[gain], grads[gain + 1] = norm_back(stream, vec[gain], total)
        return up + back

    up = inputs_back(18, 16, own(dec_normed), own(embedded), own(dsq), own(dsk), own(dsv), up)

    cols = exchange_columns(up.astype(BF))
    every = lax.all_gather(cols, "dp", axis=0, tiled=True)
    grad_table = dot(hot, every, 0, 0)
    per_clip = every.reshape(dps, dps, -1, D // seqs)
    grad_position = jnp.sum(
        lax.dynamic_index_in_dim(per_clip, lax.axis_index("dp"), 1, False).astype(F32), axis=0
    )

    dmk, dmv = dmk.astype(BF), dmv.astype(BF)
    grads[25] = outer(memory, dmk)
    grads[26] = outer(memory, dmv)
    up, grads[12], grads[13] = norm_back(stream2, vec[12], mm_t(dmk, ck_w) + mm_t(dmv, cv_w))
    up = mlp_back(10, 11, 8, enc_mlp_normed, enc_pre, enc_hidden, stream1, up)
    d_low = up.astype(BF)
    grads[7] = outer(enc_mixed, d_low)
    d_mixed = mm_t(d_low, eo, BF)
    dq, dk, dv = attend_back(q, k_all, v_all, None, enc_lse, d_mixed)
    dkv = jnp.concatenate([dk, dv], axis=1).astype(BF)
    dkv = lax.psum_scatter(dkv, "seq", scatter_dimension=0, tiled=True)
    up = inputs_back(4, 2, enc_normed, stream0, dq, dkv[:, :D], dkv[:, D:], up)

    d_second = (gelu_slope(second_pre) * up).astype(BF)
    grads[1] = jnp.stack(
        [outer(even[:frames], d_second), outer(odd[:frames], d_second), outer(even[1:], d_second)]
    )
    rim = extended(d_second, 1)
    d_even = mm_t(rim[1:], conv2[0]) + mm_t(rim[:n], conv2[2])
    d_odd = mm_t(rim[1:], conv2[1])
    d_even = jnp.where(even_keep, gelu_slope(even_pre) * low(d_even), 0.0).astype(BF)
    d_odd = jnp.where(odd_keep, gelu_slope(odd_pre) * low(d_odd), 0.0).astype(BF)
    grads[0] = (outer(odd_in[:frames], d_odd[:frames], F32) + outer(even_in[1:], d_even[1:], F32)).reshape(
        3, mels, D
    )
    me_g, mo_g = mm_t(d_even, conv1), mm_t(d_odd, conv1)
    mel_grad = jnp.concatenate(
        [
            me_g[1:, :mels] + me_g[:-1, 2 * mels :] + mo_g[:-1, mels : 2 * mels],
            me_g[1:, mels : 2 * mels] + mo_g[1:, :mels] + mo_g[:-1, 2 * mels :],
        ],
        axis=1,
    ).reshape(1, 2 * frames, mels)

    done = (reduce_grads if fast else reduce_plain)(grads, shards)
    done[14], done[15] = grad_table, grad_position
    return tuple([decoded[None], mel_grad] + done)


def exchange_columns(v):
    n = lax.axis_size("seq")
    wide = v.shape[1] // n
    v = v.reshape(v.shape[0], n, wide).transpose(1, 0, 2)
    return lax.all_to_all(v, "seq", split_axis=0, concat_axis=0, tiled=True).reshape(-1, wide)


def solution(mesh):
    place = {
        "1": P(None, "seq", "dp"),
        "2": P(None, "dp", "seq"),
        "v": P(BOTH),
        "m": P("dp", "seq"),
        "t": P("dp", "seq"),
    }
    rows = P("dp", "seq", None)
    weights = tuple(place[k] for k in KINDS)
    return jax.shard_map(
        body,
        mesh=mesh,
        in_specs=(rows, P("dp", "seq"), P("dp")) + weights + (rows,),
        out_specs=(rows, rows) + weights,
        check_vma=False,
    )
```

profile of v0, /device:TPU:1, one launch (start us, length us, event | category | flops | bytes accessed | tf_op | source)
XLA Modules:
  0.0 1092.6 jit_solution(12935848133221884624)
XLA Ops:
  9.0 40.6 %all-reduce = s32[3584]{0:T(1024)S(1)} all-reduce(s32[3584]{0:T(1024)S(1)} %bitcast_dynamic-update-slice_fusion), channel_id=2, replica_groups=mesh['dp'=8,'seq'=4] {'dp','seq'}, use_global_device_ids=true, to_apply=%add | all-reduce | flops 3584 | bytes 28672
  50.2 10.6 fusion.18
  84.3 180.7 %shard_map.603 = (bf16[4,2,2,48,768]{4,3,2,1,0:T(8,128)(2,1)}, bf16[4,2,2,48,768]{4,3,2,1,0:T(8,128)(2,1)}, bf16[4,2,2,48,768]{4,3,2,1,0:T(8,128)(2,1)}, bf16[4,...) custom-call(bf16[1104,384]{1,0:T(8,128)(2,1)} %maximum_select_fusion, ...), custom_call_target="tpu_custom_call" | custom-call | tf_op jit(solution)/shard_map/pallas_call | solution.py:371
  313.7 9.4 all-gather.1
  373.3 12.6 %fusion.232 = (f32[12,384]{1,0:T(8,128)S(1)}, f32[12,384,1536]{2,1,0:T(8,128)}) fusion(bf16[384,12,64]{0,2,1:T(8,128)(2,1)S(1)} %bitcast.448, bf16[1536,12,64]{0,2,1:T(8,128)(2,1)} %bitcast.433), kind=kOutput, calls=%fused_computation.550 | convolution fusion | flops 913042944 | bytes 31279104 | tf_op jit(solution)/shard_map/dot_general | solution.py:89
  385.9 12.6 %fusion.2 = f32[12,384]{1,0:T(8,128)S(1)} fusion(f32[12,384,1536]{2,1,0:T(8,128)} %get-tuple-element.456, f32[12,384]{1,0:T(8,128)S(1)} %get-tuple-element.455), kind=kLoop, calls=%fused_computation.8 | loop fusion | flops 14151168 | bytes 28348416 | tf_op jit(solution)/shard_map/reduce_sum | solution.py:101
  398.6 11.8 %fusion.62 = bf16[12,384,64]{1,2,0:T(8,128)(2,1)S(1)} fusion(bf16[1536,12,64]{0,2,1:T(8,128)(2,1)S(1)} %bitcast.428, f32[12,384,1536]{2,1,0:T(8,128)} %get-tuple-element.456, f32[12,384]{1,0:T(8,128)S(1)} %fusion.2, f32[12,384]{1,0:T(8,128)S(1)} %get-tuple-element.455), kind=kOutput, calls=%fused_computation.158 | convolution fusion | flops 927498240 | bytes 31297536 | tf_op jit(solution)/shard_map/dot_general | solution.py:89
  447.0 6.7 maximum_maximum_fusion
  470.7 10.0 all-to-all-done
  534.6 11.7 %all-gather.9.cloned.1.call-done = f32[448,896]{1,0:T(8,128)} async-done(((f32[112,896]{1,0:T(8,128)}), f32[448,896]{1,0:T(8,128)}) %all-gather.9.cloned.1.call-update) | async-done | bytes 1605648 | tf_op jit(solution)/shard_map/all_gather | solution.py:855
  551.0 8.8 fusion.17
  565.5 10.7 all-reduce.1
  576.2 6.7 multiply_convert_fusion.2
  614.0 23.9 %fusion.6 = (f32[12,384]{1,0:T(8,128)S(1)}, f32[12,384]{1,0:T(8,128)S(1)}, f32[12,384,1536]{2,1,0:T(8,128)}) fusion(f32[12,384,1536]{2,1,0:T(8,128)} %get-tuple-element.456, f32[12,384]{1,0:T(8,128)S(1)} %log_add_fusion.1, bf16[384,12,64]{0,2,1:T(8,128)(2,1)S(1)} %bitcast.451, bf16[1536,12,64]{0,2,1:T(8,128)(2,1)} %bitcast.427), kind=kOutput, calls=%fused_computation.12 | convolution fusion | flops 934272000 | bytes 59627520 | tf_op jit(solution)/shard_map/dot_general | solution.py:89
  643.6 9.0 all_gather.22
  654.9 12.2 %fusion.19 = (f32[12,448]{1,0:T(8,128)S(1)}, f32[12,448]{1,0:T(8,128)S(1)}, f32[12,448,448]{1,2,0:T(8,128)}) fusion(f32[12,448]{1,0:T(8,128)S(1)} %log_add_fusion, f32[12,448,448]{1,2,0:T(8,128)} %copy-done.3, pred[448,448]{0,1:T(8,128)(4,1)S(1)} %copy-done.29, bf16[448,12,64]{0,2,1:T(8,128)(2,1)} %bitcast.519, bf16[448,12,64]{0,2,1:T(8,128)(2,1)S(1)} %bitcast.518), kind=kOutput, calls=%fused_computation.35 | convolution fusion | flops 320312832 | bytes 20909056 | tf_op jit(solution)/shard_map/dot_general | solution.py:89
  667.1 6.6 multiply_convert_fusion.1
  690.8 23.3 %multiply_convert_fusion = bf16[12,384,1536]{2,1,0:T(8,128)(2,1)} fusion(f32[12,384,1536]{2,1,0:T(8,128)} %get-tuple-element.475, f32[12,384,1536]{2,1,0:T(8,128)} %get-tuple-element.456, f32[12,384]{1,0:T(8,128)S(1)} %div.170, f32[12,384]{1,0:T(8,128)S(1)} %log_add_fusion.1), kind=kLoop, calls=%fused_computation.3 | loop fusion | flops 28311552 | bytes 70815744 | tf_op jit(solution)/shard_map/convert_element_type | solution.py:114
  715.1 9.1 convolution_convert_fusion
  724.2 13.0 %fusion.24 = bf16[12,1536,64]{1,2,0:T(8,128)(2,1)} fusion(bf16[384,12,64]{0,2,1:T(8,128)(2,1)S(1)} %bitcast.452, f32[12,384,1536]{2,1,0:T(8,128)} %get-tuple-element.456, f32[12,384]{1,0:T(8,128)S(1)} %log_add_fusion.1), kind=kOutput, calls=%fused_computation.45 | convolution fusion | flops 921305088 | bytes 31279104 | tf_op jit(solution)/shard_map/dot_general | solution.py:89
  742.1 6.8 copy.541
  777.8 10.2 fusion.53
  828.5 13.0 %fusion = f32[3264,192]{0,1:T(8,128)} fusion(bf16[3584,192]{0,1:T(8,128)(2,1)} %reshape.1098, s32[3584]{0:T(1024)S(1)} %copy-done.230), kind=kOutput, calls=%fused_computation.1 | convolution fusion | flops 4503797760 | bytes 3897344 | tf_op jit(solution)/shard_map/dot_general | solution.py:25
  883.9 179.5 %shard_map.604 = (f32[1104,384]{1,0:T(8,128)}, f32[192,768]{1,0:T(8,128)}, f32[32,768]{1,0:T(8,128)}) custom-call(bf16[4,2,2,48,768]{4,3,2,1,0:T(8,128)(2,1)} %bitcast.471, bf16[4,2,2,48,768]{4,3,2,1,0:T(8,128)(2,1)} %bitcast.534, bf16[4,2,2,48,768]{4,3,2,1,0:T(8,128)(2,1)} %bitcast.535, bf16[4,2,2,48,768]{4,3,2,1,0:T(8,128)(2,1)} %bitcast.492, ...), custom_call_target="tpu_custom_call" | custom-call | tf_op jit(solution)/shard_map/pallas_call | solution.py:594
  (957 shorter events, 432.1 us)
Async XLA Ops:
  8.0 42.2 %copy-start = (bf16[3264,192]{0,1:T(8,128)(2,1)S(1)}, bf16[3264,192]{0,1:T(8,128)(2,1)}, u32[]{:S(2)}) copy-start(bf16[3264,192]{0,1:T(8,128)(2,1)} %param.53) | copy-start | bytes 3760132
  8.1 303.9 %reduce-scatter.7.cloned.1.call-start = ((), (), s32[]{:S(2)}) async-start(), calls=%async_computation.8 | async-start | bytes 2064384
  63.2 296.6 %all-gather.7.cloned.1.call-start = ((), (), s32[]{:S(2)}) async-start(), calls=%async_computation.5 | async-start | bytes 5898240 | tf_op jit(solution)/shard_map/all_gather | solution.py:785
  65.3 17.2 %collective-permute-start = (bf16[1104,192]{0,1:T(8,128)(2,1)S(1)}, bf16[1104,192]{0,1:T(8,128)(2,1)S(1)}, u32[]{:S(2)}, u32[]{:S(2)}) collective-permute-start(bf16[1104,192]{0,1:T(8,128)(2,1)S(1)} %copy.458), channel_id=1, source_target_pairs={{0,1},{1,0},{2,3},{3,2},{4,5},{5,4},{6,7},{7,6},{8,9},{9,8},{10,11... | collective-permute-start | bytes 1271816 | tf_op jit(solution)/shard_map/ppermute | solution.py:654
  66.9 14.2 %collective-permute-start.2 = (bf16[2,80]{0,1:T(8,128)(2,1)S(1)}, bf16[2,80]{0,1:T(8,128)(2,1)S(1)}, u32[]{:S(2)}, u32[]{:S(2)}) collective-permute-start(bf16[2,80]{0,1:T(8,128)(2,1)S(1)} %get-tuple-element.419), channel_id=1, source_target_pairs={{1,0},{2,1},{3,2},{5,4},{6,5},{7,6},{9,8},{10,9},{11,10},{13,12},{... | collective-permute-start | bytes 968 | tf_op jit(solution)/shard_map/ppermute | solution.py:135
  69.1 12.0 %collective-permute-start.1 = (bf16[2,80]{0,1:T(8,128)(2,1)S(1)}, bf16[2,80]{0,1:T(8,128)(2,1)S(1)}, u32[]{:S(2)}, u32[]{:S(2)}) collective-permute-start(bf16[2,80]{0,1:T(8,128)(2,1)S(1)} %get-tuple-element.418), channel_id=1, source_target_pairs={{0,1},{1,2},{2,3},{4,5},{5,6},{6,7},{8,9},{9,10},{10,11},{12,13},{... | collective-permute-start | bytes 968 | tf_op jit(solution)/shard_map/ppermute | solution.py:135
  75.8 200.5 %copy-start.248 = (pred[385]{0:T(512)(128)(4,1)}, pred[385]{0:T(512)(128)(4,1)S(1)}, u32[]{:S(2)}) copy-start(pred[385]{0:T(512)(128)(4,1)S(1)} %fusion.192) | copy-start | bytes 1159
  75.8 204.0 %copy-start.232 = (pred[385]{0:T(512)(128)(4,1)}, pred[385]{0:T(512)(128)(4,1)S(1)}, u32[]{:S(2)}) copy-start(pred[385]{0:T(512)(128)(4,1)S(1)} %fusion.193) | copy-start | bytes 1159
  82.0 194.3 %copy-start.144 = (bf16[385,160]{1,0:T(8,128)(2,1)}, bf16[385,160]{1,0:T(8,128)(2,1)S(1)}, u32[]{:S(2)}) copy-start(bf16[385,160]{1,0:T(8,128)(2,1)S(1)} %slice.454) | copy-start | bytes 369604
  82.4 197.1 %copy-start.121 = (bf16[385,160]{1,0:T(8,128)(2,1)}, bf16[385,160]{1,0:T(8,128)(2,1)S(1)}, u32[]{:S(2)}) copy-start(bf16[385,160]{1,0:T(8,128)(2,1)S(1)} %slice.462) | copy-start | bytes 369604
  82.5 193.8 %copy-start.167 = (bf16[385,80]{1,0:T(8,128)(2,1)}, bf16[385,80]{1,0:T(8,128)(2,1)S(1)}, u32[]{:S(2)}) copy-start(bf16[385,80]{1,0:T(8,128)(2,1)S(1)} %get-tuple-element.412) | copy-start | bytes 184804
  82.5 196.9 %copy-start.142 = (bf16[385,80]{1,0:T(8,128)(2,1)}, bf16[385,80]{1,0:T(8,128)(2,1)S(1)}, u32[]{:S(2)}) copy-start(bf16[385,80]{1,0:T(8,128)(2,1)S(1)} %get-tuple-element.411) | copy-start | bytes 184804
  294.0 62.2 %copy-start.200 = (f32[768]{0:T(1024)}, f32[768]{0:T(1024)S(1)}, u32[]{:S(2)}) copy-start(f32[768]{0:T(1024)S(1)} %reshape.1073) | copy-start | bytes 9220
  298.3 112.1 %copy-start.4 = (f32[384,768]{1,0:T(8,128)}, f32[384,768]{1,0:T(8,128)S(1)}, u32[]{:S(2)}) copy-start(f32[384,768]{1,0:T(8,128)S(1)} %get-tuple-element.349) | copy-start | bytes 3538948
  302.9 70.4 %copy-start.20 = (bf16[384,768]{0,1:T(8,128)(2,1)}, bf16[384,768]{0,1:T(8,128)(2,1)S(1)}, u32[]{:S(2)}) copy-start(bf16[384,768]{0,1:T(8,128)(2,1)S(1)} %copy.480) | copy-start | bytes 1769476
  456.5 24.1 %all-to-all-start = ((f32[4,112,896]{2,1,0:T(8,128)}), f32[4,112,896]{2,1,0:T(8,128)}, u32[]{:S(2)}, u32[]{:S(2)}) async-start(f32[4,112,896]{2,1,0:T(8,128)} %copy.489), calls=%async_computation | async-start | bytes 3211264 | tf_op jit(solution)/shard_map/all_to_all | solution.py:146
  461.0 85.3 %all-gather.9.cloned.1.call-start = ((), (), s32[]{:S(2)}) async-start(), calls=%async_computation.6 | async-start | bytes 2007040 | tf_op jit(solution)/shard_map/all_gather | solution.py:855
  609.3 28.6 %all-to-all-start.1 = ((f32[4,112,768]{2,1,0:T(8,128)}), f32[4,112,768]{2,1,0:T(8,128)}, u32[]{:S(2)}, u32[]{:S(2)}) async-start(f32[4,112,768]{2,1,0:T(8,128)} %copy.502), calls=%async_computation.1 | async-start | bytes 2752512 | tf_op jit(solution)/shard_map/all_to_all | solution.py:146
  687.3 26.8 %all-to-all-start.2 = ((bf16[4,112,192]{1,2,0:T(8,128)(2,1)}), bf16[4,112,192]{1,2,0:T(8,128)(2,1)S(1)}, u32[]{:S(2)}, u32[]{:S(2)}) async-start(bf16[4,112,192]{1,2,0:T(8,128)(2,1)} %bitcast.149), calls=%async_computation.2 | async-start | bytes 393216 | tf_op jit(solution)/shard_map/all_to_all | solution.py:930
  690.8 125.1 %all-gather.11.cloned.1.call-start = ((), (), s32[]{:S(2)}) async-start(), calls=%async_computation.7 | async-start | bytes 1769472 | tf_op jit(solution)/shard_map/all_gather | solution.py:880
  715.1 126.5 %reduce-scatter.9.cloned.1.call-start = ((), (), s32[]{:S(2)}) async-start(), calls=%async_computation.9 | async-start | bytes 5898240
  851.8 13.3 %collective-permute-start.3 = (bf16[1,768]{1,0:T(2,128)(2,1)S(1)}, bf16[1,768]{1,0:T(2,128)(2,1)S(1)}, u32[]{:S(2)}, u32[]{:S(2)}) collective-permute-start(bf16[1,768]{1,0:T(2,128)(2,1)S(1)} %get-tuple-element.410), channel_id=1, source_target_pairs={{1,0},{2,1},{3,2},{5,4},{6,5},{7,6},{9,8},{10,9},{11,10},{13,12},{... | collective-permute-start | bytes 4616 | tf_op jit(solution)/shard_map/ppermute | solution.py:135
  854.0 15.1 %collective-permute-start.4 = (bf16[1,768]{1,0:T(2,128)(2,1)S(1)}, bf16[1,768]{1,0:T(2,128)(2,1)S(1)}, u32[]{:S(2)}, u32[]{:S(2)}) collective-permute-start(bf16[1,768]{1,0:T(2,128)(2,1)S(1)} %get-tuple-element.409), channel_id=1, source_target_pairs={{0,1},{1,2},{2,3},{4,5},{5,6},{6,7},{8,9},{9,10},{10,11},{12,13},{... | collective-permute-start | bytes 4616 | tf_op jit(solution)/shard_map/ppermute | solution.py:135
  1067.3 5.1 collective-permute-start.5
  (252 other events, 820.1 us)
Sparse Core Ops, SparseCore 0:
  63.3 78.9 reduce-scatter.6
  715.2 44.5 all-gather.10
Sparse Core Ops, SparseCore 1:
  307.4 45.0 all-gather.6
  515.0 31.2 all-gather.8
  749.0 48.5 reduce-scatter.8
where the time goes:
time: 1100 us; the launch traced here: 1090 us
  Pallas kernels  360 us (33%)
  matrix products  297 us (27%)
  local copies, waits for them, and re-layouts  172 us (16%)
  other arithmetic  122 us (11%)
  blocking collectives  69.8 us (6%)
  starting transfers between devices  28.8 us (3%)
  waiting for transfers between devices  21.8 us (2%)
  between operations  20.9 us (2%)
    pallas_call x1, Pallas kernels, gather_fast(): pl.pallas_call(functools.partial(gather_kernel, plan), out_shape=[jax.Sha...  181 us
    pallas_call x1, Pallas kernels, reduce_fast(): pl.pallas_call(functools.partial(reduce_kernel, plan), out_shape=[jax.Sha...  180 us
    dot_general x101, matrix products, dot(): lax.dot_general(a, b, (((ca,), (cb,)), ((), ())), preferred_element_type=...  167 us
    dot_general x18, matrix products, bdot(): lax.dot_general(a, b, (((ca,), (cb,)), ((ba,), (bb,))), preferred_element...  130 us
    unnamed x582, local copies, waits for them, and re-layouts  59.9 us
    unnamed x1, blocking collectives  40.6 us
    convert_element_type x3, other arithmetic, attend_back(): ds = (p * (dp - inner)).astype(BF)  36.5 us
  transfers between devices with their start and end apart: 14, of which 2 were waited for; matrix products, arithmetic and copies ran while one was open for 27% of the time, Pallas kernels for 17%

commit v1 on v0

--- a/solution.py
+++ b/solution.py
@@ -67,67 +67,46 @@
     )
 
 
-def mlp(normed, expand, contract):
-    wide = expand.shape[2]
-    pre, hidden, out = [], [], 0.0
-    for s in range(expand.shape[0]):
-        pre.append(mm(normed, expand[s]))
-        hidden.append(gelu(pre[s]).astype(BF))
-        out = out + mm(hidden[s], contract[s * wide : (s + 1) * wide])
-    return pre, hidden, out
-
-
 def low(v):
     return lax.reduce_precision(v, 8, 7)
 
 
-def heads(v):
-    return v.reshape(v.shape[0], HEADS, HEAD)
-
-
-def bdot(a, b, ca, cb, ba, bb):
-    return lax.dot_general(a, b, (((ca,), (cb,)), ((ba,), (bb,))), preferred_element_type=F32)
-
-
-def scores_of(q, k, allowed):
-    s = bdot(heads(q), heads(k), 2, 2, 1, 1)
-    return s if allowed is None else jnp.where(allowed, s, NEGATIVE)
-
-
-def attend(q, k, v, allowed=None):
-    s = scores_of(q, k, allowed)
-    top = jnp.max(s, axis=-1, keepdims=True)
-    e = jnp.exp(s - top)
-    total = jnp.sum(e, axis=-1, keepdims=True)
-    o = bdot((e / total).astype(BF), heads(v), 2, 0, 0, 1)
-    o = o.transpose(1, 0, 2).reshape(q.shape)
-    return o, (top + jnp.log(total))[..., 0].T
-
-
-def attend_back(q, k, v, allowed, lse, up, total=lambda v: v):
-    s = scores_of(q, k, allowed)
-    p = jnp.exp(s - lse.T[:, :, None])
-    dv = bdot(p.astype(BF), heads(up), 1, 0, 0, 1)
-    dp = bdot(heads(up), heads(v), 2, 2, 1, 1)
-    mass = total(jnp.sum(p, axis=-1, keepdims=True))
-    inner = total(jnp.sum(p * dp, axis=-1, keepdims=True)) / mass
-    ds = (p * (dp - inner)).astype(BF)
-    dq = bdot(ds, heads(k), 2, 0, 0, 1)
-    dk = bdot(ds, heads(q), 1, 0, 0, 1)
-    flat = lambda a, like: a.transpose(1, 0, 2).reshape(like.shape)
-    return flat(dq, q), flat(dk, k), flat(dv, v)
-
-
-def pack(rows, extras):
-    cols = [rows.astype(F32)] + extras
+PAIR = 2 * HEAD
+
+
+def tdot(a, b, ca, cb):
+    return lax.dot_general(a, b, (((ca,), (cb,)), ((), ())), preferred_element_type=F32)
+
+
+def one_head(rows, half):
+    lane = lax.broadcasted_iota(jnp.int32, rows.shape, 1)
+    return jnp.where((lane < HEAD) == (half == 0), rows, jnp.zeros_like(rows))
+
+
+def masked(s, count_ref):
+    if count_ref is None:
+        return s
+    key = lax.broadcasted_iota(jnp.int32, s.shape, 0)
+    query = lax.broadcasted_iota(jnp.int32, s.shape, 1)
+    return jnp.where((key <= query) & (key < count_ref[0]), s, NEGATIVE)
+
+
+def pack(rows, log_sums):
+    cols, rest = [rows], log_sums.T
+    for _ in range(3):
+        term = low(rest)
+        cols.append(term.astype(BF))
+        rest = rest - term
     wide = sum(c.shape[1] for c in cols)
-    return jnp.concatenate(cols + [jnp.zeros((rows.shape[0], -wide % 128), F32)], axis=1)
-
-
-def unpack(packed, count):
-    return packed[..., :D], [
-        packed[..., D + i * HEADS : D + (i + 1) * HEADS] for i in range(count)
-    ]
+    return jnp.concatenate(cols + [jnp.zeros((rows.shape[0], -wide % 128), BF)], axis=1)
+
+
+def unpack(packed):
+    terms = [packed[..., D + i * HEADS : D + (i + 1) * HEADS].astype(F32) for i in range(3)]
+    return packed[..., :D], terms[0] + terms[1] + terms[2]
+
+
+SWAP = ((0, 1), (1, 0), (2, 3), (3, 2))
 
 
 def shift(v, axis, step):
@@ -208,11 +187,20 @@
     return out
 
 
+def product(factors):
+    left, right = factors
+    if right.ndim == 3:
+        return jnp.concatenate([outer(left, r) for r in right], axis=1)
+    if isinstance(left, list) or left.ndim == 3:
+        return jnp.stack([outer(l, right) for l in left])
+    return outer(left, right)
+
+
 def reduce_plain(grads, shards):
     dps, seqs = lax.axis_size("dp"), lax.axis_size("seq")
-    grads = list(grads)
-    for i in BROAD:
-        grads[i] = grads[i].transpose(1, 0, 2).reshape(D, -1)
+    grads = [product(g) if isinstance(g, tuple) else g for g in grads]
+    for i in TALL:
+        grads[i] = grads[i].reshape(-1, D)
     flat = jnp.concatenate(
         [to_owner(g.astype(BF), k, dps, seqs) for g, k in zip(grads, KINDS) if g is not None], axis=1
     )
@@ -407,231 +395,650 @@
     lax.fori_loop(0, total, one, 0)
 
 
-def reduce_kernel(plan, *refs):
-    inputs = 1 + max(p[0] for p in plan)
-    outputs = 1 + max(p[4] for p in plan)
-    n = len(plan)
-    ins, refs = refs[:inputs], refs[inputs:]
-    outs, refs = refs[:outputs], refs[outputs:]
-    rc, refs = refs[:n], refs[n:]
-    r1a, refs = refs[:n], refs[n:]
-    r1b, refs = refs[:n], refs[n:]
-    r2a, refs = refs[:n], refs[n:]
-    r2b, refs = refs[:n], refs[n:]
-    s3, refs = refs[:n], refs[n:]
-    rz, refs = refs[:n], refs[n:]
-    ring = {False: refs[0:2], True: refs[2:4]}
-    refs = refs[4:]
-    lsem, csend, crecv, xsend, xrecv, ysend, yrecv, zsend, zrecv = refs
+RB = 48
+
+
+def item_shapes(kind, h):
+    if kind == "n":
+        g = RB - h
+        return [
+            (4, 2, RB, D),
+            (4, h, D),
+            (4, 2, g, LANES),
+            (4, h, LANES),
+            (4, g, LANES),
+            (4, RB, LANES),
+            (3, RB, LANES),
+        ]
+    if kind == "t":
+        return [
+            (4, 4, 2, RB, D),
+            (4, 2, RB, D),
+            (4, 4, RB, LANES),
+            (4, 2, RB, LANES),
+            (4, 2, RB, LANES),
+            (4, 2, 2, RB, LANES),
+            (3, 2, 2, RB, LANES),
+        ]
+    r = RB if kind == "w" else MISC_ROWS // 2
+    return [
+        (2, 4, 2, 2, r, D),
+        (2, 4, r, D),
+        (4, 2, r, D),
+        (4, r, D),
+        (4, r, D),
+        (4, 2, r, D),
+        (3, 2, r, D),
+    ]
+
+
+def halves_of(k):
+    return 16 + 16 * (k % 2)
+
+
+def reduce_kernel(items, jobs, inputs, outputs, *refs):
+    n = len(items)
+    take = lambda count: (refs[:count], refs[count:])
+    ins, refs = take(inputs)
+    outs, refs = take(outputs)
+    rc, refs = take(n)
+    r1a, refs = take(n)
+    r1b, refs = take(n)
+    r2a, refs = take(n)
+    r2b, refs = take(n)
+    s3, refs = take(n)
+    rz, refs = take(n)
+    sbuf, refs = take(n)
+    ring, wide_ring, given, xbuf, ybuf = refs[:5]
+    loads, csend, crecv, xsend, xrecv, ysend, yrecv, zsend, zrecv, fsend, frecv = refs[5:]
     z, y, x, c = where_am_i()
     zs, yp, xp, cp = partners(z, y, x, c)
     greet(zs, yp, xp, cp)
-    stages = {}
-
-    def start(i, key, copies):
-        for cpy in copies:
-            cpy.start()
-        stages[i, key] = copies
-
-    def src(i):
-        k, tap = plan[i][0], plan[i][1]
-        return ins[k] if tap is None else ins[k].at[tap]
-
-    def rows_of(i):
-        r = plan[i][2]
-        h = split_at(i, r)
-        return plan[i][3], slice(0, h), slice(h, r), h, r
-
-    kinds = {False: 0, True: 0}
-    slot = []
-    for p in plan:
-        slot.append(kinds[p[3]] % 2)
-        kinds[p[3]] += 1
-
-    def own(i):
-        wide, _, _, _, r = rows_of(i)
-        buf = ring[wide][slot[i]]
-        if wide:
-            return buf.at[:, :, :, 0:r, :]
-        return buf.at[:, :, 0:r, :]
-
-    def send_core(i):
-        wide, _, _, _, _ = rows_of(i)
-        theirs = spot(src(i), wide, None, None, None, 1 - c, slice(None))
-        start(i, 0, [remote(theirs, rc[i], csend.at[i], crecv.at[i], cp)])
-
-    def load(i):
-        wide, _, _, _, _ = rows_of(i)
-        mine = spot(src(i), wide, None, None, None, c, slice(None))
-        start(i, 5, [pltpu.make_async_copy(mine, own(i), lsem.at[i])])
+    started = []
+
+    def start(copy):
+        copy.start()
+        started.append(copy)
+        return copy
+
+    cores, ones, twos, threes, loaded = {}, {}, {}, {}, {}
+    half = lambda i: halves_of(i)
+
+    def load(t):
+        _, part, xi, yi, rows = jobs[t]
+        xsrc, ysrc = ins[xi], ins[yi]
+        if len(xsrc.shape) == 3:
+            xsrc = xsrc.at[part]
+        if len(ysrc.shape) == 3:
+            ysrc = ysrc.at[2 * (part // 2) + (c if part % 2 else 1 - c)]
+        pair = []
+        for k, (src, buf) in enumerate(((xsrc, xbuf), (ysrc, ybuf))):
+            copy = pltpu.make_async_copy(src, buf.at[t % 2, 0:rows], loads.at[t % 2, k])
+            copy.start()
+            pair.append(copy)
+        loaded[t] = pair
+
+    def room(t):
+        return wide_ring if items[jobs[t][0]][1] == F32 else ring.at[t % RING]
+
+    def compute(t):
+        i, part, _, _, rows = jobs[t]
+        if t >= RING and t - RING in cores and items[jobs[t - RING][0]][1] == BF:
+            cores[t - RING].wait_send()
+        for copy in loaded[t]:
+            copy.wait()
+        room_t = room(t)
+        left = xbuf[t % 2, 0:rows, :]
+
+        def column(k, _):
+            at = pl.ds(pl.multiple_of(k * 256, 256), 256)
+            product = tdot(left, ybuf[t % 2, 0:rows, at], 0, 0)
+            room_t[:, :, :, :, at] = product.reshape(4, 2, 2, RB, 256).astype(room_t.dtype)
+            return 0
+
+        lax.fori_loop(0, D // 256, column, 0)
+        if t + 2 < len(jobs):
+            load(t + 2)
+        kind = items[i][0]
+        if kind == "n":
+            cores[t] = remote(room_t.at[:, :, 1 - c], rc[i], csend.at[t], crecv.at[t], cp)
+        elif kind == "t":
+            cores[t] = remote(room_t.at[:, :, 1 - c], rc[i].at[part], csend.at[t], crecv.at[t], cp)
+        elif part % 2 == 0:
+            cores[t] = remote(room_t, rc[i].at[part // 2], csend.at[t], crecv.at[t], cp)
+        if t in cores:
+            cores[t].start()
+
+    def add_own(t):
+        i, part, _, _, _ = jobs[t]
+        kind, mine = items[i][0], room(t)
+        if kind == "w":
+            if part % 2 == 0:
+                return False
+            cores[t - 1].wait_recv()
+            add_into(rc[i].at[part // 2], mine, rc[i].at[part // 2])
+            return part == 3
+        cores[t].wait_recv()
+        dst = rc[i] if kind == "n" else rc[i].at[part]
+        add_into(dst, mine.at[:, :, c], dst)
+        return kind == "n" or part == 3
+
+    def views(i):
+        kind, h = items[i][0], half(i)
+        r, a, b = rc[i], r1a[i], r1b[i]
+        here, there = lanes(x), lanes(1 - x)
+        if kind == "n":
+            one = (r.at[:, 1 - y, 0:h, :], r.at[:, :, h:RB, there], r.at[:, y, 0:h, :], r.at[:, :, h:RB, here])
+            two = (a.at[:, :, there], b.at[:, 1 - y], a.at[:, :, here], b.at[:, y])
+            parts = (s3[i].at[:, 0:h, :], s3[i].at[:, h:RB, :])
+        elif kind == "t":
+            up, down = pl.ds(2 * y, 2), pl.ds(2 * (1 - y), 2)
+            one = (r.at[:, down, 0], r.at[:, :, 1, :, there], r.at[:, up, 0], r.at[:, :, 1, :, here])
+            two = (a.at[:, :, :, there], b.at[:, down], a.at[:, :, :, here], b.at[:, up])
+            parts = (s3[i].at[:, 0], s3[i].at[:, 1])
+        else:
+            one = (r.at[:, :, 1 - y, 0], r.at[1 - x, :, :, 1], r.at[:, :, y, 0], r.at[x, :, :, 1])
+            two = (a.at[1 - x], b.at[:, 1 - y], a.at[x], b.at[:, y])
+            parts = (s3[i].at[:, 0], s3[i].at[:, 1])
+        return one, two, parts
 
     def send_1(i):
-        wide, a, b, h, r = rows_of(i)
-        stages[i, 5][0].wait()
-        stages[i, 0][0].wait_recv()
-        add_into(rc[i], own(i), rc[i])
-        if wide:
-            pa, pb = rc[i].at[:, :, 1 - y, a, :], rc[i].at[1 - x, :, :, b, :]
-        else:
-            pa, pb = rc[i].at[:, 1 - y, a, :], rc[i].at[:, :, b, lanes(1 - x)]
-        start(
-            i,
-            1,
-            [
-                remote(pa, r1a[i], ysend.at[i, 0], yrecv.at[i, 0], yp),
-                remote(pb, r1b[i], xsend.at[i, 0], xrecv.at[i, 0], xp),
-            ],
-        )
+        (over_y, over_x, _, _), _, _ = views(i)
+        ones[i] = [
+            start(remote(over_y, r1a[i], ysend.at[i, 0], yrecv.at[i, 0], yp)),
+            start(remote(over_x, r1b[i], xsend.at[i, 0], xrecv.at[i, 0], xp)),
+        ]
 
     def send_2(i):
-        wide, a, b, h, r = rows_of(i)
-        for cpy in stages[i, 1]:
-            cpy.wait_recv()
-        if wide:
-            add_into(r1a[i], rc[i].at[:, :, y, a, :], r1a[i])
-            add_into(r1b[i], rc[i].at[x, :, :, b, :], r1b[i])
-            pa, pb = r1a[i].at[1 - x], r1b[i].at[:, 1 - y]
-        else:
-            add_into(r1a[i], rc[i].at[:, y, a, :], r1a[i])
-            add_into(r1b[i], rc[i].at[:, :, b, lanes(x)], r1b[i])
-            pa, pb = r1a[i].at[:, :, lanes(1 - x)], r1b[i].at[:, 1 - y]
-        start(
-            i,
-            2,
-            [
-                remote(pa, r2a[i], xsend.at[i, 1], xrecv.at[i, 1], xp),
-                remote(pb, r2b[i], ysend.at[i, 1], yrecv.at[i, 1], yp),
-            ],
-        )
+        (_, _, stay_a, stay_b), (over_x, over_y, _, _), _ = views(i)
+        ones[i][0].wait_recv()
+        add_into(r1a[i], stay_a, r1a[i])
+        first = start(remote(over_x, r2a[i], xsend.at[i, 1], xrecv.at[i, 1], xp))
+        ones[i][1].wait_recv()
+        add_into(r1b[i], stay_b, r1b[i])
+        twos[i] = [first, start(remote(over_y, r2b[i], ysend.at[i, 1], yrecv.at[i, 1], yp))]
 
     def send_z(i):
-        wide, a, b, h, r = rows_of(i)
-        for cpy in stages[i, 2]:
-            cpy.wait_recv()
-        keep = r1a[i].at[x] if wide else r1a[i].at[:, :, lanes(x)]
-        add_into(s3[i].at[:, a, :], keep, r2a[i])
-        add_into(s3[i].at[:, b, :], r1b[i].at[:, y], r2b[i])
-        start(
-            i,
-            3,
-            [
-                remote(s3[i].at[(z + j + 1) % 4], rz[i].at[j], zsend.at[i, j], zrecv.at[i, j], zs[j])
-                for j in range(3)
-            ],
-        )
+        _, (_, _, stay_a, stay_b), (part_a, part_b) = views(i)
+        twos[i][0].wait_recv()
+        add_into(part_a, stay_a, r2a[i])
+        twos[i][1].wait_recv()
+        add_into(part_b, stay_b, r2b[i])
+        threes[i] = [
+            start(remote(s3[i].at[(z + j + 1) % 4], rz[i].at[j], zsend.at[i, j], zrecv.at[i, j], zs[j]))
+            for j in range(3)
+        ]
+
+    finals = []
 
     def finish(i):
-        for cpy in stages[i, 3]:
-            cpy.wait_recv()
-        out, first, r = plan[i][4], plan[i][5], plan[i][2]
+        kind, _, out, tap = items[i]
+        for copy in threes[i]:
+            copy.wait_recv()
         acc = s3[i][z].astype(F32)
         for j in range(3):
             acc = acc + rz[i][j].astype(F32)
-        outs[out][first : first + r, :] = acc
-
-    for i in range(n):
-        send_core(i)
-    seen = {False: [], True: []}
-    for i, p in enumerate(plan):
-        seen[p[3]].append(i)
-    for kind in (False, True):
-        for i in seen[kind][:2]:
-            load(i)
-    for t in range(n + 3):
-        if t < n:
-            send_1(t)
-            order = seen[plan[t][3]]
-            k = order.index(t)
-            if k + 2 < len(order):
-                load(order[k + 2])
-        if 0 <= t - 1 < n:
-            send_2(t - 1)
-        if 0 <= t - 2 < n:
-            send_z(t - 2)
-        if 0 <= t - 3 < n:
-            finish(t - 3)
-    for i in range(n):
-        for key in range(4):
-            for cpy in stages[i, key]:
-                cpy.wait_send()
-
-
-def reduce_fast(plan, ins, out_shapes):
-    n = len(plan)
+        dst = outs[out] if tap is None else outs[out].at[tap]
+        if kind in "wm":
+            dst[...] = acc
+            return
+        mine = acc[..., : LANES // 2]
+        theirs = acc[..., LANES // 2 :]
+        keep = jnp.where(c == 0, mine, theirs)
+        other = jnp.where(c == 0, theirs, mine)
+        if kind == "n":
+            sbuf[i][...] = other
+            dst[c] = keep
+            finals.append(start(remote(sbuf[i], dst.at[c], fsend.at[i], frecv.at[i], cp)))
+            return
+        for a in (0, 1):
+            for b in (0, 1):
+                dst[b, a, c] = keep[a, b]
+                sbuf[i][b, a] = other[a, b]
+        finals.append(start(remote(sbuf[i], dst.at[:, :, c], fsend.at[i], frecv.at[i], cp)))
+
+    g = [i for i in range(n) if items[i][0] == "m"][0]
+    last = len(jobs)
+    theirs = start(remote(ins[-1].at[:, 1 - c], rc[g], csend.at[last], crecv.at[last], cp))
+    mine = pltpu.make_async_copy(ins[-1].at[:, c], given, loads.at[0, 2])
+    mine.start()
+    load(0)
+    load(1)
+    queue = [[], [], []]
+    steps = (send_2, send_z, finish)
+
+    def advance(keep):
+        for k in (2, 1, 0):
+            while len(queue[k]) > keep:
+                i = queue[k].pop(0)
+                steps[k](i)
+                if k < 2:
+                    queue[k + 1].append(i)
+
+    mine.wait()
+    for t in range(last + 1):
+        if t < last:
+            compute(t)
+        if t == 1:
+            theirs.wait_recv()
+            add_into(rc[g], given, rc[g])
+            send_1(g)
+            queue[0].append(g)
+        if t >= 1 and add_own(t - 1):
+            i = jobs[t - 1][0]
+            send_1(i)
+            queue[0].append(i)
+        advance(LAG)
+    for keep in range(LAG - 1, -1, -1):
+        advance(keep)
+    while queue[0] or queue[1] or queue[2]:
+        advance(0)
+    for copy in finals:
+        copy.wait_recv()
+    for copy in started:
+        copy.wait_send()
+    for t in cores:
+        if t + RING >= last or items[jobs[t][0]][1] == F32:
+            cores[t].wait_send()
+
+
+RING = 3
+LAG = 1
+
+
+def reduce_fast(items, jobs, ins, out_shapes):
+    n, m = len(items), len(jobs)
     sem = pltpu.SemaphoreType.DMA
-    scratch = [[] for _ in range(7)]
-    most = {False: 0, True: 0}
-    for i, (_, _, r, wide, _, _) in enumerate(plan):
-        h = split_at(i, r)
-        most[wide] = max(most[wide], r)
-        if wide:
-            shapes = [
-                (2, 4, 2, r, D),
-                (2, 4, h, D),
-                (4, 2, r - h, D),
-                (4, h, D),
-                (4, r - h, D),
-                (4, r, D),
-                (3, r, D),
-            ]
-        else:
-            shapes = [
-                (4, 2, r, D),
-                (4, h, D),
-                (4, 2, r - h, LANES),
-                (4, h, LANES),
-                (4, r - h, LANES),
-                (4, r, LANES),
-                (3, r, LANES),
-            ]
-        for group, shape in zip(scratch, shapes):
-            group.append(pltpu.VMEM(shape, BF))
-    scratch = [s for group in scratch for s in group]
-    scratch += [pltpu.VMEM((4, 2, most[False], D), BF)] * 2
-    scratch += [pltpu.VMEM((2, 4, 2, most[True], D), BF)] * 2
-    scratch += [sem((n,)), sem((n,)), sem((n,))]
-    scratch += [sem((n, 2)), sem((n, 2)), sem((n, 2)), sem((n, 2)), sem((n, 3)), sem((n, 3))]
+    groups = [[] for _ in range(8)]
+    for i, (kind, dtype, _, _) in enumerate(items):
+        for group, shape in zip(groups, item_shapes(kind, halves_of(i))):
+            group.append(pltpu.VMEM(shape, dtype))
+        last = {"n": (RB, LANES // 2), "t": (2, 2, RB, LANES // 2)}.get(kind, (8, 128))
+        groups[7].append(pltpu.VMEM(last, F32))
+    scratch = [s for group in groups for s in group]
+    scratch += [
+        pltpu.VMEM((RING, 4, 2, 2, RB, D), BF),
+        pltpu.VMEM((4, 2, 2, RB, D), F32),
+        pltpu.VMEM((2, 4, 2, 2, MISC_ROWS // 2, D), BF),
+    ]
+    most = max(j[4] for j in jobs)
+    scratch += [pltpu.VMEM((2, most, D), BF)] * 2
+    scratch += [sem((2, 3)), sem((m + 1,)), sem((m + 1,))]
+    scratch += [sem((n, 2))] * 4 + [sem((n, 3))] * 2 + [sem((n,))] * 2
     return pl.pallas_call(
-        functools.partial(reduce_kernel, plan),
+        functools.partial(reduce_kernel, items, jobs, len(ins), len(out_shapes)),
         out_shape=[jax.ShapeDtypeStruct(s, F32) for s in out_shapes],
         in_specs=[pl.BlockSpec(memory_space=pl.ANY)] * len(ins),
         out_specs=[pl.BlockSpec(memory_space=pltpu.VMEM)] * len(out_shapes),
         scratch_shapes=scratch,
         compiler_params=pltpu.CompilerParams(
-            collective_id=2, has_side_effects=True, vmem_limit_bytes=60 << 20
+            collective_id=2, has_side_effects=True, vmem_limit_bytes=62 << 20
         ),
     )(*ins)
+
+
+def lanes_of(pair):
+    return pl.ds(pl.multiple_of(pair * PAIR, PAIR), PAIR)
+
+
+def clip_partners():
+    d, s = lax.axis_index("dp"), lax.axis_index("seq")
+    x, c = s // 2, s % 2
+    return (d, (1 - x) * 2 + c), (d, x * 2 + 1 - c)
+
+
+def greet_pair(xp, cp):
+    barrier = pltpu.get_barrier_semaphore()
+    for dev in (xp, cp):
+        pl.semaphore_signal(barrier, inc=1, device_id=dev, device_id_type=MESH)
+    pl.semaphore_wait(barrier, 2)
+
+
+def forward_head(q_one, k_slab, v_slab, half, count):
+    s = masked(tdot(k_slab, q_one, 1, 1), count)
+    top = jnp.max(s, axis=0, keepdims=True)
+    e = jnp.exp(s - top)
+    total = jnp.sum(e, axis=0, keepdims=True)
+    mixed = tdot(v_slab, e.astype(BF), 0, 0)[half * HEAD : (half + 1) * HEAD]
+    return mixed / total, top + jnp.log(total)
+
+
+def forward_pair(pair, q, k, v, o, lse, count):
+    at = lanes_of(pair)
+    q_slab, k_slab, v_slab = q[:, at], k[:, at], v[:, at]
+    both = []
+    for half in (0, 1):
+        mixed, log_sum = forward_head(one_head(q_slab, half), k_slab, v_slab, half, count)
+        both.append(mixed)
+        lse[pl.ds(2 * pair + half, 1), :] = log_sum
+    o[:, at] = jnp.concatenate(both, axis=0).T.astype(o.dtype)
+
+
+def backward_pair(pair, q, k, v, up, lse, dq, dk, dv, count, known):
+    at = lanes_of(pair)
+    q_slab, k_slab, v_slab, u_slab = q[:, at], k[:, at], v[:, at], up[:, at]
+    both, dk_sum, dv_sum = [], 0.0, 0.0
+    for half in (0, 1):
+        row = pl.ds(2 * pair + half, 1)
+        q_one, u_one = one_head(q_slab, half), one_head(u_slab, half)
+        p = jnp.exp(masked(tdot(k_slab, q_one, 1, 1), count) - lse[row, :])
+        dp = tdot(v_slab, u_one, 1, 1)
+        if known is None:
+            mass = jnp.sum(p, axis=0, keepdims=True)
+            inner = jnp.sum(p * dp, axis=0, keepdims=True) / mass
+        else:
+            inner = known[row, :]
+        ds = (p * (dp - inner)).astype(BF)
+        dv_sum = dv_sum + tdot(p.astype(BF), u_one, 1, 0)
+        dk_sum = dk_sum + tdot(ds, q_one, 1, 0)
+        both.append(tdot(k_slab, ds, 0, 0)[half * HEAD : (half + 1) * HEAD])
+    dq[:, at] = jnp.concatenate(both, axis=0).T.astype(dq.dtype)
+    dk[:, at] = dk_sum.astype(dk.dtype)
+    dv[:, at] = dv_sum.astype(dv.dtype)
+
+
+def attend_kernel(causal, *refs):
+    count = refs[0] if causal else None
+    q, k, v, o, lse = refs[1:] if causal else refs
+
+    def step(pair, _):
+        forward_pair(pair, q, k, v, o, lse, count)
+        return 0
+
+    lax.fori_loop(0, HEADS // 2, step, 0)
+
+
+def sums_kernel(q, k, v, up, lse, mass, inner):
+    def step(pair, _):
+        at = lanes_of(pair)
+        q_slab, k_slab, v_slab, u_slab = q[:, at], k[:, at], v[:, at], up[:, at]
+        for half in (0, 1):
+            row = pl.ds(2 * pair + half, 1)
+            p = jnp.exp(tdot(k_slab, one_head(q_slab, half), 1, 1) - lse[row, :])
+            dp = tdot(v_slab, one_head(u_slab, half), 1, 1)
+            mass[row, :] = jnp.sum(p, axis=0, keepdims=True)
+            inner[row, :] = jnp.sum(p * dp, axis=0, keepdims=True)
+        return 0
+
+    lax.fori_loop(0, HEADS // 2, step, 0)
+
+
+def back_kernel(causal, given, *refs):
+    count, known = None, None
+    if causal:
+        count, refs = refs[0], refs[1:]
+    q, k, v, up, lse = refs[:5]
+    refs = refs[5:]
+    if given:
+        known, refs = refs[0], refs[1:]
+    dq, dk, dv = refs
+
+    def step(pair, _):
+        backward_pair(pair, q, k, v, up, lse, dq, dk, dv, count, known)
+        return 0
+
+    lax.fori_loop(0, HEADS // 2, step, 0)
+
+
+def clip_attend_kernel(q, k, v, o, lse, k_all, v_all, xsend, xrecv, csend, crecv):
+    xp, cp = clip_partners()
+    r = q.shape[0]
+    greet_pair(xp, cp)
+    pairs = HEADS // 2
+
+    def across(pair):
+        at = lanes_of(pair)
+        return [
+            remote(src.at[:, at], dst.at[r : 2 * r, at], xsend.at[j, pair], xrecv.at[j, pair], xp)
+            for j, (src, dst) in enumerate(((k, k_all), (v, v_all)))
+        ]
+
+    def beside(pair):
+        at = lanes_of(pair)
+        return [
+            remote(a.at[0 : 2 * r, at], a.at[2 * r : 4 * r, at], csend.at[j, pair], crecv.at[j, pair], cp)
+            for j, a in enumerate((k_all, v_all))
+        ]
+
+    for pair in range(pairs):
+        for copy in across(pair):
+            copy.start()
+    k_all[0:r, :] = k[...]
+    v_all[0:r, :] = v[...]
+
+    def pass_on(pair):
+        for copy in across(pair):
+            copy.wait_recv()
+        for copy in beside(pair):
+            copy.start()
+
+    pass_on(0)
+
+    def step(pair, _):
+        @pl.when(pair + 1 < pairs)
+        def _():
+            pass_on(pair + 1)
+
+        for copy in beside(pair):
+            copy.wait_recv()
+        forward_pair(pair, q, k_all, v_all, o, lse, None)
+        return 0
+
+    lax.fori_loop(0, pairs, step, 0)
+    for pair in range(pairs):
+        for copy in across(pair) + beside(pair):
+            copy.wait_send()
+
+
+def clip_back_kernel(q, k, v, up, lse, dq, dk, dv, *refs):
+    k_sum, v_sum, k_near, v_near, k_far, v_far, xsend, xrecv, csend, crecv = refs
+    xp, cp = clip_partners()
+    r = q.shape[0]
+    greet_pair(xp, cp)
+    pairs = HEADS // 2
+    sums, nears, fars, outs = (k_sum, v_sum), (k_near, v_near), (k_far, v_far), (dk, dv)
+
+    def beside(pair):
+        at = lanes_of(pair)
+        return [
+            remote(sums[j].at[2 * r : 4 * r, at], nears[j].at[:, at], csend.at[j, pair], crecv.at[j, pair], cp)
+            for j in (0, 1)
+        ]
+
+    def across(pair):
+        at = lanes_of(pair)
+        return [
+            remote(sums[j].at[r : 2 * r, at], fars[j].at[:, at], xsend.at[j, pair], xrecv.at[j, pair], xp)
+            for j in (0, 1)
+        ]
+
+    def step(t, _):
+        @pl.when(t < pairs)
+        def _():
+            backward_pair(t, q, k, v, up, lse, dq, k_sum, v_sum, None, None)
+            for copy in beside(t):
+                copy.start()
+
+        @pl.when((t >= 1) & (t <= pairs))
+        def _():
+            pair = t - 1
+            at = lanes_of(pair)
+            for copy in beside(pair):
+                copy.wait_recv()
+            for j in (0, 1):
+                near = sums[j][0 : 2 * r, at].astype(F32) + nears[j][:, at].astype(F32)
+                sums[j][0 : 2 * r, at] = near.astype(BF)
+            for copy in across(pair):
+                copy.start()
+
+        @pl.when(t >= 2)
+        def _():
+            pair = t - 2
+            at = lanes_of(pair)
+            for copy in across(pair):
+                copy.wait_recv()
+            for j in (0, 1):
+                total = sums[j][0:r, at].astype(F32) + fars[j][:, at].astype(F32)
+                outs[j][:, at] = total.astype(BF)
+
+        return 0
+
+    lax.fori_loop(0, pairs + 2, step, 0)
+    for pair in range(pairs):
+        for copy in across(pair) + beside(pair):
+            copy.wait_send()
+
+
+def local_call(kernel, out_shape, args, cost, count=None, scratch=(), barrier=None):
+    vmem = pl.BlockSpec(memory_space=pltpu.VMEM)
+    specs = [vmem] * len(args)
+    if count is not None:
+        specs, args = [pl.BlockSpec(memory_space=pltpu.SMEM)] + specs, [count] + args
+    params = dict(vmem_limit_bytes=56 << 20)
+    if barrier is not None:
+        params.update(collective_id=barrier, has_side_effects=True)
+    return pl.pallas_call(
+        kernel,
+        out_shape=[jax.ShapeDtypeStruct(s, t) for s, t in out_shape],
+        in_specs=specs,
+        out_specs=[vmem] * len(out_shape),
+        scratch_shapes=list(scratch),
+        cost_estimate=pl.CostEstimate(flops=cost, bytes_accessed=8 << 20, transcendentals=0),
+        compiler_params=pltpu.CompilerParams(**params),
+    )(*args)
+
+
+def rows_cost(q, k):
+    return 8 * q.shape[0] * k.shape[0] * D
+
+
+def attend(q, k, v, count=None):
+    shapes = [(q.shape, BF), ((HEADS, q.shape[0]), F32)]
+    kernel = functools.partial(attend_kernel, count is not None)
+    return local_call(kernel, shapes, [q, k, v], rows_cost(q, k), count)
+
+
+def attend_sums(q, k, v, up, lse):
+    return local_call(sums_kernel, [(lse.shape, F32)] * 2, [q, k, v, up, lse], rows_cost(q, k))
+
+
+def attend_back(q, k, v, up, lse, count=None, inner=None, out=BF):
+    shapes = [(q.shape, out), (k.shape, BF), (k.shape, BF)]
+    kernel = functools.partial(back_kernel, count is not None, inner is not None)
+    args = [q, k, v, up, lse] + ([] if inner is None else [inner])
+    return local_call(kernel, shapes, args, 3 * rows_cost(q, k), count)
+
+
+def clip_attend(q, k, v):
+    r = k.shape[0]
+    shapes = [(q.shape, BF), ((HEADS, r), F32), ((4 * r, D), BF), ((4 * r, D), BF)]
+    sems = [pltpu.SemaphoreType.DMA((2, HEADS // 2))] * 4
+    return local_call(clip_attend_kernel, shapes, [q, k, v], 4 * rows_cost(q, k), None, sems, 3)
+
+
+def clip_attend_back(q, k_all, v_all, up, lse):
+    r = q.shape[0]
+    scratch = [pltpu.VMEM((4 * r, D), BF)] * 2 + [pltpu.VMEM((2 * r, D), BF)] * 2
+    scratch += [pltpu.VMEM((r, D), BF)] * 2 + [pltpu.SemaphoreType.DMA((2, HEADS // 2))] * 4
+    args = [q, k_all, v_all, up, lse]
+    return local_call(clip_back_kernel, [(q.shape, BF)] * 3, args, 3 * rows_cost(q, k_all), None, scratch, 4)
+
+
+def mlp_kernel(stream, gain, bias, expand, contract, normed, pre, hidden, out):
+    @pl.when(pl.program_id(0) == 0)
+    def _():
+        normed[...] = norm(stream[...], gain[...], bias[...])
+        out[...] = stream[...]
+
+    before = tdot(normed[...], expand[0], 1, 0)
+    pre[0] = before
+    after = gelu(before).astype(BF)
+    hidden[0] = after
+    out[...] += tdot(after, contract[0], 1, 0)
+
+
+def mlp_back_kernel(up, stream, gain, pre, expand, contract, out, d_low, d_pre, d_gain, d_bias, total):
+    s = pl.program_id(0)
+
+    @pl.when(s == 0)
+    def _():
+        d_low[...] = up[...].astype(BF)
+        total[...] = jnp.zeros_like(total)
+
+    d_hidden = low(tdot(d_low[...], contract[0], 1, 1))
+    grad = (gelu_slope(pre[0]) * d_hidden).astype(BF)
+    d_pre[0] = grad
+    total[...] += tdot(grad, expand[0], 1, 1)
+
+    @pl.when(s == pl.num_programs(0) - 1)
+    def _():
+        hat, inv = norm_parts(stream[...])
+        g = total[...] * gain[...]
+        mean = lambda v: jnp.mean(v, axis=-1, keepdims=True)
+        out[...] = up[...] + inv * (g - mean(g) - hat * mean(g * hat))
+        d_gain[...] = jnp.sum(total[...] * hat, axis=0, keepdims=True)
+        d_bias[...] = jnp.sum(total[...], axis=0, keepdims=True)
+
+
+def blocks(kernel, grid, ins, outs, args, cost, scratch=()):
+    def spec(shape, cut):
+        if cut:
+            return pl.BlockSpec((1,) + shape[1:], lambda s: (s,) + (0,) * (len(shape) - 1))
+        return pl.BlockSpec(shape, lambda s: (0,) * len(shape))
+
+    return pl.pallas_call(
+        kernel,
+        grid=(grid,),
+        out_shape=[jax.ShapeDtypeStruct(s, t) for s, t, _ in outs],
+        in_specs=[spec(a.shape, cut) for a, cut in zip(args, ins)],
+        out_specs=[spec(s, cut) for s, _, cut in outs],
+        scratch_shapes=list(scratch),
+        cost_estimate=pl.CostEstimate(flops=cost, bytes_accessed=16 << 20, transcendentals=0),
+        compiler_params=pltpu.CompilerParams(vmem_limit_bytes=48 << 20),
+    )(*args)
+
+
+def mlp(stream, gain, bias, expand, contract):
+    n, (r, _) = expand.shape[0], stream.shape
+    outs = [((r, D), BF, False), ((n, r, D), F32, True), ((n, r, D), BF, True), ((r, D), F32, False)]
+    args = [stream, gain[None], bias[None], expand, contract.reshape(n, D, D)]
+    return blocks(mlp_kernel, n, [False] * 3 + [True] * 2, outs, args, 4 * n * r * D * D)
+
+
+def mlp_backward(up, stream, gain, pre, expand, contract):
+    n, (r, _) = expand.shape[0], stream.shape
+    outs = [((r, D), F32, False), ((r, D), BF, False), ((n, r, D), BF, True)]
+    outs += [((1, D), F32, False)] * 2
+    args = [up, stream, gain[None], pre, expand, contract.reshape(n, D, D)]
+    scratch = [pltpu.VMEM((r, D), F32)]
+    return blocks(mlp_back_kernel, n, [False] * 3 + [True] * 3, outs, args, 4 * n * r * D * D, scratch)
+
 
 SQUARE = (4, 5, 6, 7, 18, 19, 20, 21, 24, 25, 26, 27)
 TALL = (11, 31)
 BROAD = (10, 30)
 VECTORS = tuple(i for i in range(32) if KINDS[i] == "v")
 MISC_ROWS = 32
-SWAP = ((0, 1), (1, 0), (2, 3), (3, 2))
-
-
-def plans(shards):
-    g, r, shapes, first = [], [], [], 0
+
+
+def plan_gather(shards):
+    g, shapes, first, at = [], [], 0, 0
     for i in SQUARE + (1,) + TALL:
         w = shards[i]
         rows = w.shape[-2] // 2
         one = (4, 2, 2, rows, D)
         for tap in range(w.shape[0]) if w.ndim == 3 else (None,):
             g.append((0, first, rows, len(shapes), tap, False))
-            r.append((len(shapes), tap, rows, False, 0, first))
             first += rows
         shapes.append(one if w.ndim == 2 else (w.shape[0],) + one)
-    at = 0
     for i in BROAD:
         rows = shards[i].shape[0]
         g.append((1, at, rows, len(shapes), None, True))
-        r.append((len(shapes), None, rows, True, 1, at))
         at += rows
         shapes.append((2, 2, 4, 2, rows, D))
     g.append((2, 0, MISC_ROWS, len(shapes), None, True))
-    r.append((len(shapes), None, MISC_ROWS, True, 2, 0))
     shapes.append((2, 2, 4, 2, MISC_ROWS, D))
-    return g, r, shapes, first, at
+    return g, shapes
 
 
 def by_core(c, zero, one):
@@ -646,9 +1053,9 @@
     return jnp.concatenate(parts, axis=1)
 
 
-def gather_weights(shards):
+def gather_weights(shards, ids):
     c = lax.axis_index("seq") % 2
-    g, _, shapes, _, _ = plans(shards)
+    g, shapes = plan_gather(shards)
     halves = narrow_halves(shards)
     mine = by_core(c, halves[0], halves[1])
     got = lax.ppermute(by_core(c, halves[1], halves[0]), "seq", SWAP)
@@ -657,6 +1064,7 @@
     )
     broad = jnp.concatenate([shards[i] for i in BROAD], axis=0)
     flat = [shards[i].reshape(-1) for i in (0,) + VECTORS + (15,)]
+    flat += [(ids // 256).astype(BF), (ids % 256).astype(BF)]
     size = sum(f.size for f in flat)
     flat.append(jnp.zeros((MISC_ROWS * D - size,), BF))
     misc = jnp.concatenate(flat).reshape(MISC_ROWS, D)
@@ -689,13 +1097,44 @@
         .transpose(2, 3, 4, 0, 1, 5)
         .reshape(8 * r, 4 * w)
     )
-    return full
+    at += r * w
+    both = misc[..., at : at + 2 * ids.size].reshape(2, 2, 4, 2, 2, ids.size).astype(jnp.int32)
+    all_ids = (both[..., 0, :] * 256 + both[..., 1, :]).transpose(2, 3, 0, 1, 4).reshape(-1)
+    return full, all_ids
+
+
+ORDER = (31, 30, 27, 24, 21, 18, 19, 20, 11, 10, 25, 26, 7, 4, 5, 6, 1)
+EXACT = 25
 
 
 def reduce_grads(grads, shards):
-    c = lax.axis_index("seq") % 2
-    _, r, shapes, narrow_rows, broad_rows = plans(shards)
-    ins = [grads[i].reshape(shapes[k]) for k, i in enumerate(SQUARE + (1,) + TALL + BROAD)]
+    items, jobs, ins, shapes, seen = [], [], [], [], {}
+
+    def place(v):
+        if id(v) not in seen:
+            seen[id(v)] = len(ins)
+            ins.append(v)
+        return seen[id(v)]
+
+    for i in ORDER:
+        left, right = grads[i]
+        if i in TALL:
+            jobs += [(len(items), s, place(left), place(right), left.shape[1]) for s in range(4)]
+            items.append(("t", BF, len(shapes), None))
+            shapes.append((2, 2, 2, RB, LANES // 2))
+        elif i in BROAD:
+            jobs += [(len(items), s, place(left), place(right), left.shape[0]) for s in range(4)]
+            items.append(("w", BF, len(shapes), None))
+            shapes.append((2, RB, D))
+        elif i == 1:
+            for tap, l in enumerate(left):
+                jobs.append((len(items), 0, place(l), place(right), l.shape[0]))
+                items.append(("n", BF, len(shapes), tap))
+            shapes.append((3, 2, RB, LANES // 2))
+        else:
+            jobs.append((len(items), 0, place(left), place(right), left.shape[0]))
+            items.append(("n", F32 if i == EXACT else BF, len(shapes), None))
+            shapes.append((2, RB, LANES // 2))
     t, a, b = shards[0].shape
     conv1 = grads[0].reshape(t, 2, 2, a, 4, 2, b).transpose(1, 2, 4, 5, 0, 3, 6)
     n = shards[VECTORS[0]].size
@@ -703,27 +1142,14 @@
     flat = [conv1.reshape(2, 2, 4, 2, -1), vecs.transpose(3, 4, 1, 2, 0, 5).reshape(2, 2, 4, 2, -1)]
     size = sum(f.shape[-1] for f in flat)
     flat.append(jnp.zeros((2, 2, 4, 2, MISC_ROWS * D - size), F32))
-    ins.append(jnp.concatenate(flat, axis=-1).astype(BF).reshape(shapes[-1]))
-    narrow, broad, misc = reduce_fast(
-        r, ins, [(narrow_rows, LANES), (broad_rows, D), (MISC_ROWS, D)]
-    )
-    half = LANES // 2
-    mine = by_core(c, narrow[:, :half], narrow[:, half:])
-    got = lax.ppermute(by_core(c, narrow[:, half:], narrow[:, :half]), "seq", SWAP)
-    out, at = [None] * 32, 0
-    for i in SQUARE + (1,) + TALL:
-        w = shards[i]
-        rows, taps = w.shape[-2] // 2, []
-        for _ in range(w.shape[0] if w.ndim == 3 else 1):
-            m, o = mine[at : at + rows], got[at : at + rows]
-            taps.append(by_core(c, jnp.concatenate([m, o]), jnp.concatenate([o, m])))
-            at += rows
-        out[i] = taps[0] if w.ndim == 2 else jnp.stack(taps)
-    at = 0
-    for i in BROAD:
-        out[i] = broad[at : at + shards[i].shape[0]]
-        at += shards[i].shape[0]
-    misc = misc.reshape(-1)
+    ins.append(jnp.concatenate(flat, axis=-1).astype(BF).reshape(2, 2, 4, 2, 2, MISC_ROWS // 2, D))
+    items.append(("m", BF, len(shapes), None))
+    shapes.append((2, MISC_ROWS // 2, D))
+    got = reduce_fast(items, jobs, ins, shapes)
+    out = [None] * 32
+    for i, v in zip(ORDER, got):
+        out[i] = v.reshape(shards[i].shape)
+    misc = got[-1].reshape(-1)
     out[0] = misc[: shards[0].size].reshape(shards[0].shape)
     at = shards[0].size
     for i in VECTORS:
@@ -746,16 +1172,16 @@
     all_slots = slots * seqs
     frames = mel_frames.shape[1] // 2
 
-    ids = lax.all_gather(token_ids[0], BOTH, axis=0, tiled=True)
+    fast = dps == 8 and seqs == 4
+    weights = shards[:14] + [None] + shards[15:]
+    if fast:
+        full, ids = gather_weights(weights, token_ids[0])
+    else:
+        full, ids = gather_plain(weights), lax.all_gather(token_ids[0], BOTH, axis=0, tiled=True)
     hot = one_hot(ids, table)
     looked = mm(hot, table, BF)
     mine = lax.psum_scatter(looked, "dp", scatter_dimension=0, tiled=True)
-    looked = lax.all_gather(mine, "seq", axis=0, tiled=True)
-    looked = looked.reshape(seqs, all_slots, D // seqs).transpose(1, 0, 2).reshape(all_slots, D)
-
-    weights = shards[:14] + [None] + shards[15:]
-    fast = dps == 8 and seqs == 4
-    full = gather_weights(weights) if fast else gather_plain(weights)
+
     vec = {i: full[i].astype(F32) for i in range(32) if KINDS[i] == "v"}
     conv1, conv2, position = full[0].reshape(-1, D), full[1], full[15]
     eq, ek, ev, eo = full[4:8]
@@ -782,94 +1208,78 @@
     q = (mm(enc_normed, eq) * SCALE).astype(BF)
     k = mm(enc_normed, ek, BF)
     v = mm(enc_normed, ev, BF)
-    kv = lax.all_gather(jnp.concatenate([k, v], axis=1), "seq", axis=0, tiled=True)
-    k_all, v_all = kv[:, :D], kv[:, D:]
-    enc_mixed, enc_lse = attend(q, k_all, v_all)
-    enc_wide, enc_mixed = enc_mixed, enc_mixed.astype(BF)
+    enc_mixed, enc_lse, k_all, v_all = clip_attend(q, k, v)
     stream1 = stream0 + mm(enc_mixed, eo)
-    enc_mlp_normed = norm(stream1, vec[8], vec[9])
-    enc_pre, enc_hidden, out = mlp(enc_mlp_normed, ee, ec)
-    stream2 = stream1 + out
+    enc_mlp_normed, enc_pre, enc_hidden, stream2 = mlp(stream1, vec[8], vec[9], ee, ec)
     memory = norm(stream2, vec[12], vec[13])
     mk = mm(memory, ck_w, BF)
     mv = mm(memory, cv_w, BF)
 
+    mine, enc_mixed = lax.optimization_barrier((mine, enc_mixed))
+    looked = lax.all_gather(mine, "seq", axis=0, tiled=True)
+    looked = looked.reshape(seqs, all_slots, D // seqs).transpose(1, 0, 2).reshape(all_slots, D)
     place = jnp.arange(all_slots)
-    causal = (place[None, :] <= place[:, None]) & (place[None, :] < token_counts[0])
     embedded = looked.astype(F32) + position.astype(F32)
     dec_normed = norm(embedded, vec[16], vec[17])
     sq = (mm(dec_normed, dq_w) * SCALE).astype(BF)
     sk = mm(dec_normed, dk_w, BF)
     sv = mm(dec_normed, dv_w, BF)
-    dec_mixed, dec_lse = attend(sq, sk, sv, causal)
-    dec_wide, dec_mixed = dec_mixed, dec_mixed.astype(BF)
+    dec_mixed, dec_lse = attend(sq, sk, sv, token_counts)
     stream4 = embedded + mm(dec_mixed, do_w)
     cross_normed = norm(stream4, vec[22], vec[23])
     xq = (mm(cross_normed, cq_w) * SCALE).astype(BF)
 
     part, part_lse = attend(xq, mk, mv)
-    got = exchange(pack(part, [part_lse]))
-    parts, (lses,) = unpack(got, 1)
+    parts, lses = unpack(exchange(pack(part, part_lse)))
     top = jnp.max(lses, axis=0)
     share = jnp.exp(lses - top)
     total = jnp.sum(share, axis=0)
     cross_lse = top + jnp.log(total)
     share = share / total
-    cross_wide = jnp.sum(
-        parts.reshape(seqs, slots, HEADS, HEAD) * share[..., None], axis=0
+    cross_mixed = jnp.sum(
+        parts.astype(F32).reshape(seqs, slots, HEADS, HEAD) * share[..., None], axis=0
     ).reshape(slots, D)
-    cross_mixed = cross_wide.astype(BF)
+    cross_mixed = cross_mixed.astype(BF)
 
     own = lambda a: lax.dynamic_slice_in_dim(a, me * slots, slots, 0)
     stream4 = own(stream4)
     stream5 = stream4 + mm(cross_mixed, co_w)
-    dec_mlp_normed = norm(stream5, vec[28], vec[29])
-    dec_pre, dec_hidden, out = mlp(dec_mlp_normed, de, dc)
-    stream6 = stream5 + out
+    dec_mlp_normed, dec_pre, dec_hidden, stream6 = mlp(stream5, vec[28], vec[29], de, dc)
     live = (own(place) < token_counts[0])[:, None]
     decoded = jnp.where(live, stream6, 0.0).astype(BF)
 
     grads = [None] * 32
 
     def mlp_back(ex, co, gain, normed, pre, hidden, stream, up):
-        d_low = up.astype(BF)
-        wide = normed.shape[1]
-        first, second, total = [], [], 0.0
-        for s in range(seqs):
-            contract = full[co][s * wide : (s + 1) * wide]
-            second.append(outer(hidden[s], d_low))
-            d_pre = (gelu_slope(pre[s]) * low(mm_t(d_low, contract))).astype(BF)
-            first.append(outer(normed, d_pre))
-            total = total + mm_t(d_pre, full[ex][s])
-        grads[co] = jnp.concatenate(second, axis=0)
-        grads[ex] = jnp.stack(first)
-        back, grads[gain], grads[gain + 1] = norm_back(stream, vec[gain], total)
-        return up + back
+        up, d_low, d_pre, d_gain, d_bias = mlp_backward(up, stream, vec[gain], pre, full[ex], full[co])
+        grads[co], grads[ex] = (hidden, d_low), (normed, d_pre)
+        grads[gain], grads[gain + 1] = d_gain[0], d_bias[0]
+        return up
 
     up = jnp.where(live, cotangent.astype(F32), 0.0)
     up = mlp_back(30, 31, 28, dec_mlp_normed, dec_pre, dec_hidden, stream5, up)
     d_low = up.astype(BF)
-    grads[27] = outer(cross_mixed, d_low)
+    grads[27] = (cross_mixed, d_low)
     d_mixed = mm_t(d_low, co_w, BF)
-    sent = pack(d_mixed, [cross_lse])
-    d_mixed, (lse_all,) = unpack(lax.all_gather(sent, "seq", axis=0, tiled=True), 1)
-    dxq, dmk, dmv = attend_back(xq, mk, mv, None, lse_all, d_mixed.astype(BF), lambda v: lax.psum(v, "seq"))
+    d_mixed, lse_all = unpack(lax.all_gather(pack(d_mixed, cross_lse.T), "seq", axis=0, tiled=True))
+    lse_all = lse_all.T
+    sums = lax.psum(jnp.stack(attend_sums(xq, mk, mv, d_mixed, lse_all)), "seq")
+    dxq, dmk, dmv = attend_back(xq, mk, mv, d_mixed, lse_all, inner=sums[1] / sums[0], out=F32)
     dxq = jnp.sum(exchange(dxq), axis=0)
     dxq = (low(dxq) * SCALE).astype(BF)
-    grads[24] = outer(own(cross_normed), dxq)
+    grads[24] = (own(cross_normed), dxq)
     back, grads[22], grads[23] = norm_back(stream4, vec[22], mm_t(dxq, cq_w))
     up = up + back
     d_low = up.astype(BF)
-    grads[21] = outer(own(dec_mixed), d_low)
+    grads[21] = (own(dec_mixed), d_low)
     d_mixed = lax.all_gather(mm_t(d_low, do_w, BF), "seq", axis=0, tiled=True)
-    dsq, dsk, dsv = attend_back(sq, sk, sv, causal, dec_lse, d_mixed)
+    dsq, dsk, dsv = attend_back(sq, sk, sv, d_mixed, dec_lse, token_counts)
 
     def inputs_back(first, gain, normed, stream, dq, dk, dv, up):
-        dq = (low(dq) * SCALE).astype(BF)
-        dk, dv = dk.astype(BF), dv.astype(BF)
+        dq = (dq.astype(F32) * SCALE).astype(BF)
         total = 0.0
         for i, g in enumerate((dq, dk, dv)):
-            grads[first + i] = outer(normed, g)
+            grads[first + i] = (normed, g)
             total = total + mm_t(g, full[first + i])
         back, grads[gain], grads[gain + 1] = norm_back(stream, vec[gain], total)
         return up + back
@@ -884,23 +1294,18 @@
         lax.dynamic_index_in_dim(per_clip, lax.axis_index("dp"), 1, False).astype(F32), axis=0
     )
 
-    dmk, dmv = dmk.astype(BF), dmv.astype(BF)
-    grads[25] = outer(memory, dmk)
-    grads[26] = outer(memory, dmv)
+    grads[25] = (memory, dmk)
+    grads[26] = (memory, dmv)
     up, grads[12], grads[13] = norm_back(stream2, vec[12], mm_t(dmk, ck_w) + mm_t(dmv, cv_w))
     up = mlp_back(10, 11, 8, enc_mlp_normed, enc_pre, enc_hidden, stream1, up)
     d_low = up.astype(BF)
-    grads[7] = outer(enc_mixed, d_low)
+    grads[7] = (enc_mixed, d_low)
     d_mixed = mm_t(d_low, eo, BF)
-    dq, dk, dv = attend_back(q, k_all, v_all, None, enc_lse, d_mixed)
-    dkv = jnp.concatenate([dk, dv], axis=1).astype(BF)
-    dkv = lax.psum_scatter(dkv, "seq", scatter_dimension=0, tiled=True)
-    up = inputs_back(4, 2, enc_normed, stream0, dq, dkv[:, :D], dkv[:, D:], up)
+    dq, dk, dv = clip_attend_back(q, k_all, v_all, d_mixed, enc_lse)
+    up = inputs_back(4, 2, enc_normed, stream0, dq, dk, dv, up)
 
     d_second = (gelu_slope(second_pre) * up).astype(BF)
-    grads[1] = jnp.stack(
-        [outer(even[:frames], d_second), outer(odd[:frames], d_second), outer(even[1:], d_second)]
-    )
+    grads[1] = ([even[:frames], odd[:frames], even[1:]], d_second)
     rim = extended(d_second, 1)
     d_even = mm_t(rim[1:], conv2[0]) + mm_t(rim[:n], conv2[2])
     d_odd = mm_t(rim[1:], conv2[1])

time: 1100 us -> 889 us (0.81)
  matrix products: 297 us -> 72.7 us
  Pallas kernels: 360 us -> 548 us
  other arithmetic: 122 us -> 37.1 us
  local copies, waits for them, and re-layouts: 172 us -> 123 us
  blocking collectives: 69.8 us -> 37 us
    pallas_call x1 -> x12, Pallas kernels: 180 us -> 372 us  [the longest x1 214 us: reduce_fast(): pl.pallas_call(functools.partial(reduce_kernel, items, jobs, len(ins), le...]
    dot_general x18 -> x0, matrix products: 130 us -> none  [bdot(): lax.dot_general(a, b, (((ca,), (cb,)), ((ba,), (bb,))), preferred_element...]
    dot_general x101 -> x38, matrix products: 167 us -> 72.7 us  [dot(): lax.dot_general(a, b, (((ca,), (cb,)), ((), ())), preferred_element_type=...]
    unnamed x1 -> x0, blocking collectives: 40.6 us -> none
    convert_element_type x4 -> x9, other arithmetic: 36.9 us -> 2.06 us  [the longest x1 0.9 us: inputs_back(): dq = (dq.astype(F32) * SCALE).astype(BF)]
    slice x13 -> x5, local copies, waits for them, and re-layouts: 31.1 us -> 3.36 us  [the longest x2 2.04 us: unpack(): return (packed[..., :D], terms[0] + terms[1] + terms[2])]
    concatenate x6 -> x0, other arithmetic: 19.4 us -> none  [the longest x2 7.53 us: pack(): jnp.concatenate(cols + [jnp.zeros((rows.shape[0], -wide % 128), F32)], ax...]
    reduce_sum x4 -> x1, other arithmetic: 18.3 us -> 1.37 us  [body(): jnp.sum(parts.astype(F32).reshape(seqs, slots, HEADS, HEAD) * share[...,...]
  transfers between devices with their start and end apart: 14 -> 10, of which waited for: 2 -> 3; matrix products, arithmetic and copies ran while one was open for 27% -> 10% of each run, Pallas kernels for 17% -> 29%
where the time goes in v1:
time: 889 us; the launch traced here: 878 us
  Pallas kernels  548 us (62%)
  local copies, waits for them, and re-layouts  123 us (14%)
  matrix products  72.7 us (8%)
  other arithmetic  37.1 us (4%)
  blocking collectives  37 us (4%)
  starting transfers between devices  25 us (3%)
  between operations  17.5 us (2%)
  waiting for transfers between devices  17.1 us (2%)
    pallas_call x1, Pallas kernels, reduce_fast(): pl.pallas_call(functools.partial(reduce_kernel, items, jobs, len(ins), le...  214 us
    pallas_call x1, Pallas kernels, gather_fast(): pl.pallas_call(functools.partial(gather_kernel, plan), out_shape=[jax.Sha...  176 us
    pallas_call x7, Pallas kernels, local_call(): pl.pallas_call(kernel, out_shape=[jax.ShapeDtypeStruct(s, t) for s, t in...  126 us
    dot_general x38, matrix products, dot(): lax.dot_general(a, b, (((ca,), (cb,)), ((), ())), preferred_element_type=...  72.7 us
    unnamed x362, local copies, waits for them, and re-layouts  54.3 us
    pallas_call x4, Pallas kernels, blocks(): pl.pallas_call(kernel, grid=(grid,), out_shape=[jax.ShapeDtypeStruct(s, t...  31.9 us
  transfers between devices with their start and end apart: 10, of which 3 were waited for; matrix products, arithmetic and copies ran while one was open for 10% of the time, Pallas kernels for 29%

profile of v1, /device:TPU:1, one launch (start us, length us, event | category | flops | bytes accessed | tf_op | source)
XLA Modules:
  0.0 877.5 jit_solution(14858213145339742126)
XLA Ops:
  44.7 176.2 %shard_map.603 = (bf16[4,2,2,48,768]{4,3,2,1,0:T(8,128)(2,1)}, bf16[4,2,2,48,768]{4,3,2,1,0:T(8,128)(2,1)}, bf16[4,2,2,48,768]{4,3,2,1,0:T(8,128)(2,1)}, bf16[4,...) custom-call(bf16[1104,384]{1,0:T(8,128)(2,1)} %maximum_select_fusion, ...), custom_call_target="tpu_custom_call" | custom-call | tf_op jit(solution)/shard_map/pallas_call | solution.py:359
  226.9 10.6 %fusion.4 = bf16[3584,192]{0,1:T(8,128)(2,1)S(1)} fusion(bf16[3264,192]{0,1:T(8,128)(2,1)S(1)} %copy-done, s32[3584]{0:T(1024)S(1)} %sub.158), kind=kOutput, calls=%fused_computation.5 | convolution fusion | flops 4504485888 | bytes 2643968 | tf_op jit(solution)/shard_map/dot_general | solution.py:25
  277.3 36.0 %shard_map.604 = (bf16[384,768]{1,0:T(8,128)(2,1)}, f32[12,384]{1,0:T(8,128)}, bf16[1536,768]{1,0:T(8,128)(2,1)}, bf16[1536,768]{1,0:T(8,128)(2,1)}) custom-call(bf16[384,768]{1,0:T(8,128)(2,1)} %fusion.15.q, bf16[384,768]{1,0:T(8,128)(2,1)} %convolution_convert_fusion.6.k, bf16[384,768]{1,0:T(8,128)(2,1)} %convolution_convert_fusion.5.v), custom_call_target="tpu_custom_call" | custom-call | flops 3623878656 | bytes 8388608 | tf_op jit(solution)/shard_map/pallas_call | solution.py:900
  315.0 8.4 shard_map.606
  332.8 8.7 all-gather
  355.1 9.7 %shard_map.605 = (bf16[448,768]{1,0:T(8,128)(2,1)}, f32[12,448]{1,0:T(8,128)}) custom-call(s32[1]{0:T(128)} %copy.421.refs_0_, bf16[448,768]{1,0:T(8,128)(2,1)} %fusion.11.refs_1_, bf16[448,768]{1,0:T(8,128)(2,1)} %convolution_convert_fusion.1.refs_2_, bf16[448,768]{1,0:T(8,128)(2,1)} %convolution_convert_fusion.refs_3_), custom_call_target="tpu_custom_call" | custom-call | flops 1233125376 | bytes 8388608 | tf_op jit(solution)/shard_map/pallas_call | solution.py:900
  370.0 9.0 %shard_map.607 = (bf16[448,768]{1,0:T(8,128)(2,1)}, f32[12,448]{1,0:T(8,128)}) custom-call(bf16[448,768]{1,0:T(8,128)(2,1)} %fusion.12.refs_0_.q, bf16[384,768]{1,0:T(8,128)(2,1)} %convolution_convert_fusion.4.refs_1_.k, bf16[384,768]{1,0:T(8,128)(2,1)} %convolution_convert_fusion.3.refs_2_.v), custom_call_target="tpu_custom_call" | custom-call | flops 1056964608 | bytes 8388608 | tf_op jit(solution)/shard_map/pallas_call | solution.py:900
  382.3 4.3 all-to-all-start
  392.7 5.0 all-to-all-done
  407.1 5.6 shard_map.608
  413.7 6.9 shard_map.609
  424.8 8.8 %all_gather.13 = bf16[448,896]{1,0:T(8,128)(2,1)S(1)} all-gather(bf16[112,896]{1,0:T(8,128)(2,1)S(1)} %concatenate.67), channel_id=1, replica_groups=mesh['dp'=8,'seq'=4] {'seq'}, dimensions={0}, use_global_device_ids=true | all-gather | bytes 1003520 | tf_op jit(solution)/shard_map/all_gather | solution.py:1264
  436.3 6.1 shard_map.610
  443.3 10.8 %psum.7 = f32[2,12,448]{2,1,0:T(8,128)S(1)} all-reduce(f32[2,12,448]{2,1,0:T(8,128)S(1)} %pad_maximum_fusion.8), channel_id=1, replica_groups=mesh['dp'=8,'seq'=4] {'seq'}, use_global_device_ids=true, to_apply=%region_12.13 | all-reduce | flops 10752 | bytes 86016 | tf_op jit(solution)/shard_map/psum | solution.py:1266
  454.7 11.1 %shard_map.611 = (f32[448,768]{1,0:T(8,128)}, bf16[384,768]{1,0:T(8,128)(2,1)}, bf16[384,768]{1,0:T(8,128)(2,1)}) custom-call(bf16[448,768]{1,0:T(8,128)(2,1)} %fusion.12.refs_0_.q, bf16[384,768]{1,0:T(8,128)(2,1)} %convolution_convert_fusion.4.refs_1_.k, bf16[384,768]{1,0:T(8,128)(2,1)} %convolution_convert_fusion.3.refs_2_.v, ...), custom_call_target="tpu_custom_call" | custom-call | flops 3170893824 | bytes 8388608 | tf_op jit(solution)/shard_map/pallas_call | solution.py:900
  469.1 11.0 %shard_map.612 = (f32[384,768]{1,0:T(8,128)S(1)}, bf16[384,768]{1,0:T(8,128)(2,1)S(1)}, bf16[4,384,768]{2,1,0:T(8,128)(2,1)}, f32[1,768]{1,0:T(1,128)S(1)}, f32[1,768]{1,0:T(1,128)S(1)}) custom-call(f32[384,768]{1,0:T(8,128)S(1)} %subtract_multiply_fusion.up, f32[384,768]{1,0:T(8,128)S(1)} %convolution_add_fusion.5.stream, f32[1,768]{1,0:T(1,128)S(1)} %reshape.715.gain, ...), custom_call_target="tpu_custom_call" | custom-call | flops 3623878656 | bytes 16777216 | tf_op jit(solution)/shard_map/pallas_call | solution.py:989
  483.1 40.6 %shard_map.613 = (bf16[384,768]{1,0:T(8,128)(2,1)}, bf16[384,768]{1,0:T(8,128)(2,1)}, bf16[384,768]{1,0:T(8,128)(2,1)}) custom-call(bf16[384,768]{1,0:T(8,128)(2,1)} %fusion.15.q, bf16[1536,768]{1,0:T(8,128)(2,1)} %get-tuple-element.142.k, bf16[1536,768]{1,0:T(8,128)(2,1)} %get-tuple-element.143.v, bf16[384,768]{1,0:T(8,128)(2,1)} %convolution_convert_fusion.2.up, ...), custom_call_target="tpu_custom_call" | custom-call | flops 10871635968 | bytes 8388608 | tf_op jit(solution)/shard_map/pallas_call | solution.py:900
  536.9 4.4 all-to-all-start.1
  549.3 9.2 %all-to-all-done.1 = f32[4,112,768]{2,1,0:T(8,128)} async-done(((f32[4,112,768]{2,1,0:T(8,128)}), f32[4,112,768]{2,1,0:T(8,128)}, u32[]{:S(2)}, u32[]{:S(2)}) %all-to-all-start.1) | async-done | bytes 1376288 | tf_op jit(solution)/shard_map/all_to_all | solution.py:125
  564.9 8.6 all_gather.14.refs_4_
  573.6 13.6 %shard_map.614 = (bf16[448,768]{1,0:T(8,128)(2,1)}, bf16[448,768]{1,0:T(8,128)(2,1)}, bf16[448,768]{1,0:T(8,128)(2,1)}) custom-call(s32[1]{0:T(128)} %copy.421.refs_0_, bf16[448,768]{1,0:T(8,128)(2,1)} %fusion.11.refs_1_, bf16[448,768]{1,0:T(8,128)(2,1)} %convolution_convert_fusion.1.refs_2_, bf16[448,768]{1,0:T(8,128)(2,1)} %convolution_convert_fusion.refs_3_, ...), custom_call_target="tpu_custom_call" | custom-call | flops 3699376128 | bytes 8388608 | tf_op jit(solution)/shard_map/pallas_call | solution.py:900
  611.1 6.2 concatenate.71
  619.3 213.9 %shard_map.615 = (f32[2,2,2,48,192]{4,3,2,1,0:T(8,128)}, f32[2,48,768]{2,1,0:T(8,128)}, f32[2,48,192]{2,1,0:T(8,128)}, f32[2,48,192]{2,1,0:T(8,128)}, f32[2,48,1...) custom-call(bf16[4,112,768]{2,1,0:T(8,128)(2,1)} %copy-done.3, ...), custom_call_target="tpu_custom_call" | custom-call | tf_op jit(solution)/shard_map/pallas_call | solution.py:668
  843.2 13.1 %fusion = f32[3264,192]{0,1:T(8,128)} fusion(bf16[3584,192]{0,1:T(8,128)(2,1)} %reshape.731, s32[3584]{0:T(1024)S(1)} %copy-done.127), kind=kOutput, calls=%fused_computation.1 | convolution fusion | flops 4503797760 | bytes 3897344 | tf_op jit(solution)/shard_map/dot_general | solution.py:25
  (611 shorter events, 222.2 us)
Async XLA Ops:
  7.2 219.7 %copy-start = (bf16[3264,192]{0,1:T(8,128)(2,1)S(1)}, bf16[3264,192]{0,1:T(8,128)(2,1)}, u32[]{:S(2)}) copy-start(bf16[3264,192]{0,1:T(8,128)(2,1)} %param.53) | copy-start | bytes 3760132
  7.3 11.7 %copy-start.123 = (bf16[96,192]{1,0:T(8,128)(2,1)S(1)}, bf16[96,192]{1,0:T(8,128)(2,1)}, u32[]{:S(2)}) copy-start(bf16[96,192]{1,0:T(8,128)(2,1)} %param.66) | copy-start | bytes 110596
  7.3 324.4 %reduce-scatter.4.cloned.1.call-start = ((), (), s32[]{:S(2)}) async-start(), calls=%async_computation.5 | async-start | bytes 2064384
  25.4 13.0 %copy-start.91 = (bf16[1,112,768]{2,1,0:T(8,128)(2,1)S(1)}, bf16[1,112,768]{2,1,0:T(8,128)(2,1)}, u32[]{:S(2)}) copy-start(bf16[1,112,768]{2,1,0:T(8,128)(2,1)} %param.71) | copy-start | bytes 516100
  25.4 16.4 %collective-permute-start = (bf16[1104,192]{0,1:T(8,128)(2,1)}, bf16[1104,192]{0,1:T(8,128)(2,1)}, u32[]{:S(2)}, u32[]{:S(2)}) collective-permute-start(bf16[1104,192]{0,1:T(8,128)(2,1)} %copy.309), channel_id=1, source_target_pairs={{0,1},{1,0},{2,3},{3,2},{4,5},{5,4},{6,7},{7,6},{8,9},{9,8},{10,11... | collective-permute-start | bytes 1271816 | tf_op jit(solution)/shard_map/ppermute | solution.py:1061
  25.6 13.0 %collective-permute-start.2 = (bf16[2,80]{0,1:T(8,128)(2,1)S(1)}, bf16[2,80]{0,1:T(8,128)(2,1)S(1)}, u32[]{:S(2)}, u32[]{:S(2)}) collective-permute-start(bf16[2,80]{0,1:T(8,128)(2,1)S(1)} %get-tuple-element.466), channel_id=1, source_target_pairs={{1,0},{2,1},{3,2},{5,4},{6,5},{7,6},{9,8},{10,9},{11,10},{13,12},{... | collective-permute-start | bytes 968 | tf_op jit(solution)/shard_map/ppermute | solution.py:114
  27.9 10.6 %collective-permute-start.1 = (bf16[2,80]{0,1:T(8,128)(2,1)S(1)}, bf16[2,80]{0,1:T(8,128)(2,1)S(1)}, u32[]{:S(2)}, u32[]{:S(2)}) collective-permute-start(bf16[2,80]{0,1:T(8,128)(2,1)S(1)} %get-tuple-element.465), channel_id=1, source_target_pairs={{0,1},{1,2},{2,3},{4,5},{5,6},{6,7},{8,9},{9,10},{10,11},{12,13},{... | collective-permute-start | bytes 968 | tf_op jit(solution)/shard_map/ppermute | solution.py:114
  33.7 215.7 %copy-start.145 = (pred[385]{0:T(512)(128)(4,1)}, pred[385]{0:T(512)(128)(4,1)S(1)}, u32[]{:S(2)}) copy-start(pred[385]{0:T(512)(128)(4,1)S(1)} %fusion.66) | copy-start | bytes 1159
  41.9 206.8 %copy-start.80 = (bf16[385,80]{1,0:T(8,128)(2,1)}, bf16[385,80]{1,0:T(8,128)(2,1)S(1)}, u32[]{:S(2)}) copy-start(bf16[385,80]{1,0:T(8,128)(2,1)S(1)} %get-tuple-element.458) | copy-start | bytes 184804
  255.0 58.3 %copy-start.9 = (f32[384,768]{1,0:T(8,128)}, f32[384,768]{1,0:T(8,128)S(1)}, u32[]{:S(2)}) copy-start(f32[384,768]{1,0:T(8,128)S(1)} %get-tuple-element.441) | copy-start | bytes 3538948
  277.3 36.0 %copy-start.74 = (bf16[4,2,2,48,768]{4,3,2,1,0:T(8,128)(2,1)S(1)}, bf16[4,2,2,48,768]{4,3,2,1,0:T(8,128)(2,1)}, u32[]{:S(2)}) copy-start(bf16[4,2,2,48,768]{4,3,2,1,0:T(8,128)(2,1)} %get-tuple-element.122) | copy-start | bytes 3538948
  382.3 15.4 %all-to-all-start = ((bf16[4,112,896]{2,1,0:T(8,128)(2,1)}), bf16[4,112,896]{2,1,0:T(8,128)(2,1)}, u32[]{:S(2)}, u32[]{:S(2)}) async-start(bf16[4,112,896]{2,1,0:T(8,128)(2,1)} %bitcast.227), calls=%async_computation | async-start | bytes 1605632 | tf_op jit(solution)/shard_map/all_to_all | solution.py:125
  386.6 12.2 %copy-start.130 = (f32[112]{0:T(128)}, f32[112]{0:T(128)S(1)}, u32[]{:S(2)}) copy-start(f32[112]{0:T(128)S(1)} %broadcast_multiply_fusion.13) | copy-start | bytes 1348
  483.1 40.6 %copy-start.73 = (bf16[4,2,2,48,768]{4,3,2,1,0:T(8,128)(2,1)S(1)}, bf16[4,2,2,48,768]{4,3,2,1,0:T(8,128)(2,1)}, u32[]{:S(2)}) copy-start(bf16[4,2,2,48,768]{4,3,2,1,0:T(8,128)(2,1)} %get-tuple-element.111) | copy-start | bytes 3538948
  530.6 16.0 %collective-permute-start.3 = (bf16[1,768]{1,0:T(2,128)(2,1)S(1)}, bf16[1,768]{1,0:T(2,128)(2,1)S(1)}, u32[]{:S(2)}, u32[]{:S(2)}) collective-permute-start(bf16[1,768]{1,0:T(2,128)(2,1)S(1)} %get-tuple-element.457), channel_id=1, source_target_pairs={{1,0},{2,1},{3,2},{5,4},{6,5},{7,6},{9,8},{10,9},{11,10},{13,12},{... | collective-permute-start | bytes 4616 | tf_op jit(solution)/shard_map/ppermute | solution.py:114
  534.4 8.8 %collective-permute-start.4 = (bf16[1,768]{1,0:T(2,128)(2,1)S(1)}, bf16[1,768]{1,0:T(2,128)(2,1)S(1)}, u32[]{:S(2)}, u32[]{:S(2)}) collective-permute-start(bf16[1,768]{1,0:T(2,128)(2,1)S(1)} %get-tuple-element.456), channel_id=1, source_target_pairs={{0,1},{1,2},{2,3},{4,5},{5,6},{6,7},{8,9},{9,10},{10,11},{12,13},{... | collective-permute-start | bytes 4616 | tf_op jit(solution)/shard_map/ppermute | solution.py:114
  536.9 21.6 %all-to-all-start.1 = ((f32[4,112,768]{2,1,0:T(8,128)}), f32[4,112,768]{2,1,0:T(8,128)}, u32[]{:S(2)}, u32[]{:S(2)}) async-start(f32[4,112,768]{2,1,0:T(8,128)} %bitcast.62), calls=%async_computation.1 | async-start | bytes 2752512 | tf_op jit(solution)/shard_map/all_to_all | solution.py:125
  549.3 11.4 %copy-start.132 = (f32[112]{0:T(128)S(1)}, f32[112]{0:T(128)}, u32[]{:S(2)}) copy-start(f32[112]{0:T(128)} %add_rsqrt_fusion.5) | copy-start | bytes 1348
  573.6 13.7 %copy-start.17 = (f32[448,768]{1,0:T(8,128)S(1)}, f32[448,768]{1,0:T(8,128)}, u32[]{:S(2)}) copy-start(f32[448,768]{1,0:T(8,128)} %copy-done.16) | copy-start | bytes 4128772
  573.6 13.7 %copy-start.129 = (f32[112]{0:T(128)S(1)}, f32[112]{0:T(128)}, u32[]{:S(2)}) copy-start(f32[112]{0:T(128)} %broadcast_multiply_fusion.10) | copy-start | bytes 1348
  573.6 14.8 %copy-start.66 = (bf16[4,2,2,48,768]{4,3,2,1,0:T(8,128)(2,1)S(1)}, bf16[4,2,2,48,768]{4,3,2,1,0:T(8,128)(2,1)}, u32[]{:S(2)}) copy-start(bf16[4,2,2,48,768]{4,3,2,1,0:T(8,128)(2,1)} %get-tuple-element.116) | copy-start | bytes 3538948
  593.8 8.0 all-to-all-start.2
  597.3 240.9 %all-gather.4.cloned.1.call-start = ((), (), s32[]{:S(2)}) async-start(), calls=%async_computation.4 | async-start | bytes 1769472 | tf_op jit(solution)/shard_map/all_gather | solution.py:1290
  843.2 13.1 %copy-start.18 = (bf16[8,448,192]{1,2,0:T(8,128)(2,1)S(1)}, bf16[8,448,192]{1,2,0:T(8,128)(2,1)}, u32[]{:S(2)}) copy-start(bf16[8,448,192]{1,2,0:T(8,128)(2,1)} %all-gather.4.cloned.1.call-done) | copy-start | bytes 4128772
  (142 other events, 612.9 us)
Sparse Core Ops, SparseCore 0:
  240.1 73.1 reduce-scatter.3
  602.9 60.3 all-gather.3

commit v2 on v1

--- a/solution.py
+++ b/solution.py
@@ -104,9 +104,6 @@
 def unpack(packed):
     terms = [packed[..., D + i * HEADS : D + (i + 1) * HEADS].astype(F32) for i in range(3)]
     return packed[..., :D], terms[0] + terms[1] + terms[2]
-
-
-SWAP = ((0, 1), (1, 0), (2, 3), (3, 2))
 
 
 def shift(v, axis, step):
@@ -257,123 +254,6 @@
     if wide:
         return ref.at[full(xs), c, full(zs), full(ys), rs, :]
     return ref.at[full(zs), full(ys), c, rs, slice(None) if xs is None else lanes(xs)]
-
-
-def gather_kernel(plan, *refs):
-    inputs = 1 + max(p[0] for p in plan)
-    outputs = 1 + max(p[3] for p in plan)
-    ins, outs = refs[:inputs], refs[inputs : inputs + outputs]
-    lsem, zsend, zrecv, xsend, xrecv, ysend, yrecv, csend, crecv = refs[inputs + outputs :]
-    z, y, x, c = where_am_i()
-    zs, yp, xp, cp = partners(z, y, x, c)
-    greet(zs, yp, xp, cp)
-    n = len(plan)
-    started = [[] for _ in range(n)]
-    dst = []
-    for src, first, rows, out, tap, wide in plan:
-        dst.append(outs[out] if tap is None else outs[out].at[tap])
-
-    def item(i):
-        _, _, rows, _, _, wide = plan[i]
-        h = split_at(i, rows)
-        return rows, wide, slice(0, h), slice(h, rows)
-
-    stages = {}
-
-    def start(i, key, copies):
-        for cpy in copies:
-            cpy.start()
-        stages[i, key] = copies
-
-    def send_z(i):
-        src, first, rows, _, _, wide = plan[i]
-        block = ins[src].at[first : first + rows]
-        here = spot(dst[i], wide, z, y, x, c, slice(None))
-        start(i, 0, [remote(block, here, zsend.at[i, j], zrecv.at[i, j], zs[j]) for j in range(3)])
-        start(i, 4, [pltpu.make_async_copy(block, here, lsem.at[i])])
-
-    def send_1(i):
-        rows, wide, a, b = item(i)
-        for cpy in stages[i, 0]:
-            cpy.wait_recv()
-        stages[i, 4][0].wait()
-        ax = spot(dst[i], wide, None, y, x, c, a)
-        by = spot(dst[i], wide, None, y, x, c, b)
-        start(
-            i,
-            1,
-            [
-                remote(ax, ax, xsend.at[i, 0], xrecv.at[i, 0], xp),
-                remote(by, by, ysend.at[i, 0], yrecv.at[i, 0], yp),
-            ],
-        )
-
-    def send_2(i):
-        rows, wide, a, b = item(i)
-        for cpy in stages[i, 1]:
-            cpy.wait_recv()
-        ay = spot(dst[i], wide, None, y, None, c, a)
-        bx = spot(dst[i], wide, None, None, x, c, b)
-        start(
-            i,
-            2,
-            [
-                remote(ay, ay, ysend.at[i, 1], yrecv.at[i, 1], yp),
-                remote(bx, bx, xsend.at[i, 1], xrecv.at[i, 1], xp),
-            ],
-        )
-
-    def send_core(i):
-        rows, wide, a, b = item(i)
-        for cpy in stages[i, 2]:
-            cpy.wait_recv()
-        half = spot(dst[i], wide, None, None, None, c, slice(None))
-        start(i, 3, [remote(half, half, csend.at[i], crecv.at[i], cp)])
-
-    for t in range(n + AHEAD[2]):
-        if t == 0:
-            for i in range(min(n, AHEAD[3])):
-                send_z(i)
-        if t + AHEAD[3] < n:
-            send_z(t + AHEAD[3])
-        if 0 <= t - AHEAD[0] < n:
-            send_1(t - AHEAD[0])
-        if 0 <= t - AHEAD[1] < n:
-            send_2(t - AHEAD[1])
-        if 0 <= t - AHEAD[2] < n:
-            send_core(t - AHEAD[2])
-    for i in range(n):
-        stages[i, 3][0].wait_recv()
-        for key in range(4):
-            for cpy in stages[i, key]:
-                cpy.wait_send()
-
-
-AHEAD = (0, 1, 2, 4)
-
-
-def gather_fast(plan, ins, out_shapes):
-    n = len(plan)
-    sem = pltpu.SemaphoreType.DMA
-    hbm = pl.BlockSpec(memory_space=pl.ANY)
-    return pl.pallas_call(
-        functools.partial(gather_kernel, plan),
-        out_shape=[jax.ShapeDtypeStruct(s, BF) for s in out_shapes],
-        in_specs=[hbm] * len(ins),
-        out_specs=[hbm] * len(out_shapes),
-        scratch_shapes=[
-            sem((n,)),
-            sem((n, 3)),
-            sem((n, 3)),
-            sem((n, 2)),
-            sem((n, 2)),
-            sem((n, 2)),
-            sem((n, 2)),
-            sem((n,)),
-            sem((n,)),
-        ],
-        compiler_params=pltpu.CompilerParams(collective_id=1, has_side_effects=True),
-    )(*ins)
 
 
 def add_into(dst, *srcs):
@@ -463,6 +343,7 @@
 
     cores, ones, twos, threes, loaded = {}, {}, {}, {}, {}
     half = lambda i: halves_of(i)
+    at = {(j[0], j[1]): t for t, j in enumerate(jobs)}
 
     def load(t):
         _, part, xi, yi, rows = jobs[t]
@@ -491,9 +372,9 @@
         left = xbuf[t % 2, 0:rows, :]
 
         def column(k, _):
-            at = pl.ds(pl.multiple_of(k * 256, 256), 256)
-            product = tdot(left, ybuf[t % 2, 0:rows, at], 0, 0)
-            room_t[:, :, :, :, at] = product.reshape(4, 2, 2, RB, 256).astype(room_t.dtype)
+            cols = pl.ds(pl.multiple_of(k * 256, 256), 256)
+            product = tdot(left, ybuf[t % 2, 0:rows, cols], 0, 0)
+            room_t[:, :, :, :, cols] = product.reshape(4, 2, 2, RB, 256).astype(room_t.dtype)
             return 0
 
         lax.fori_loop(0, D // 256, column, 0)
@@ -515,7 +396,7 @@
         if kind == "w":
             if part % 2 == 0:
                 return False
-            cores[t - 1].wait_recv()
+            cores[at[i, part - 1]].wait_recv()
             add_into(rc[i].at[part // 2], mine, rc[i].at[part // 2])
             return part == 3
         cores[t].wait_recv()
@@ -1021,90 +902,379 @@
 MISC_ROWS = 32
 
 
-def plan_gather(shards):
-    g, shapes, first, at = [], [], 0, 0
-    for i in SQUARE + (1,) + TALL:
+ROW_PAD = 400
+CHUNK = 80
+SMALL_ROWS = 96
+
+
+def gather_split(i, rows):
+    return rows // 2 if rows % 32 == 0 else 16 + 16 * (i % 2)
+
+
+def stem_kernel(plan, inputs, outputs, *refs):
+    n = len(plan)
+    ins, refs = refs[:inputs], refs[inputs:]
+    patches, angles, refs = refs[:3], refs[3], refs[4:]
+    outs, refs = refs[:outputs], refs[outputs:]
+    even_pre, odd_pre, even, odd, even_next, second, stream, normed, q, k_all, v_all, o, lse, vec = refs[:14]
+    got, stage, refs = refs[14 : 14 + n], refs[14 + n : 14 + 2 * n], refs[14 + 2 * n :]
+    small, weights, k_own, v_own = refs[:4]
+    lsem, zsend, zrecv, xsend, xrecv, ysend, yrecv, csend, crecv, psend, precv = refs[4:15]
+    wsem, kxs, kxr, kcs, kcr = refs[15:]
+    z, y, x, c = where_am_i()
+    zs, yp, xp, cp = partners(z, y, x, c)
+    greet(zs, yp, xp, cp)
+    dst, src, swaps = [], [], []
+    for i, (k, rows, out, tap, kind) in enumerate(plan):
+        dst.append(outs[out] if tap is None else outs[out].at[tap])
+        src.append(ins[k] if tap is None else ins[k].at[tap])
+        swaps.append(None)
+        if kind == "n":
+            theirs = src[i].at[pl.ds(pl.multiple_of((1 - c) * rows, 16), rows), :]
+            swaps[i] = remote(theirs, got[i], psend.at[i], precv.at[i], cp)
+            swaps[i].start()
+
+    def item(i):
+        rows, wide = plan[i][1], plan[i][4] == "w"
+        h = gather_split(i, rows)
+        return rows, wide, slice(0, h), slice(h, rows)
+
+    stages = {}
+
+    def start(i, key, copies):
+        for cpy in copies:
+            cpy.start()
+        stages[i, key] = copies
+
+    def send_z(i):
+        rows, wide, _, _ = item(i)
+        block = src[i]
+        if not wide:
+            mine = src[i][pl.ds(pl.multiple_of(c * rows, 16), rows), :]
+            swaps[i].wait_recv()
+            theirs = got[i][...]
+            stage[i][...] = jnp.concatenate(
+                [jnp.where(c == 0, mine, theirs), jnp.where(c == 0, theirs, mine)], axis=1
+            )
+            block = stage[i]
+        here = spot(dst[i], wide, z, y, x, c, slice(None))
+        start(i, 0, [remote(block, here, zsend.at[i, j], zrecv.at[i, j], zs[j]) for j in range(3)])
+        start(i, 4, [pltpu.make_async_copy(block, here, lsem.at[i])])
+
+    def send_1(i):
+        rows, wide, a, b = item(i)
+        for cpy in stages[i, 0]:
+            cpy.wait_recv()
+        stages[i, 4][0].wait()
+        ax = spot(dst[i], wide, None, y, x, c, a)
+        by = spot(dst[i], wide, None, y, x, c, b)
+        start(
+            i,
+            1,
+            [
+                remote(ax, ax, xsend.at[i, 0], xrecv.at[i, 0], xp),
+                remote(by, by, ysend.at[i, 0], yrecv.at[i, 0], yp),
+            ],
+        )
+
+    def send_2(i):
+        rows, wide, a, b = item(i)
+        for cpy in stages[i, 1]:
+            cpy.wait_recv()
+        ay = spot(dst[i], wide, None, y, None, c, a)
+        bx = spot(dst[i], wide, None, None, x, c, b)
+        start(
+            i,
+            2,
+            [
+                remote(ay, ay, ysend.at[i, 1], yrecv.at[i, 1], yp),
+                remote(bx, bx, xsend.at[i, 1], xrecv.at[i, 1], xp),
+            ],
+        )
+
+    def send_core(i):
+        rows, wide, a, b = item(i)
+        for cpy in stages[i, 2]:
+            cpy.wait_recv()
+        half = spot(dst[i], wide, None, None, None, c, slice(None))
+        start(i, 3, [remote(half, half, csend.at[i], crecv.at[i], cp)])
+
+    arrived = set()
+
+    def arrive(i):
+        if i not in arrived:
+            stages[i, 3][0].wait_recv()
+            arrived.add(i)
+
+    r = q.shape[0]
+    pairs = HEADS // 2
+
+    def fetch(items, slots):
+        copies = []
+        for i, slot in zip(items, slots):
+            arrive(i)
+            copies.append(pltpu.make_async_copy(dst[i], weights.at[slot], wsem.at[slot]))
+            copies[-1].start()
+        for cpy in copies:
+            cpy.wait()
+
+    def weight(slot):
+        return weights[slot].reshape(D, D)
+
+    def open_small():
+        arrive(0)
+        copy = pltpu.make_async_copy(dst[0], small, wsem.at[3])
+        copy.start()
+        copy.wait()
+        cells = []
+        for zy in range(8):
+            for s in range(4):
+                cells.append(small[s // 2, s % 2, zy // 2, zy % 2, 64:80, 0:24].astype(F32))
+        vec[...] = jnp.concatenate(cells, axis=1)
+
+    def convolve(patch, pre, act, edge):
+        def one(t, _):
+            rows = pl.ds(pl.multiple_of(t * CHUNK, 16), CHUNK)
+            left = patch[rows, :]
+            cells = []
+            for zy in range(8):
+                taps = [small[s // 2, s % 2, zy // 2, zy % 2, 0:64, :] for s in range(4)]
+                cells.append(tdot(left, jnp.concatenate(taps, axis=0), 1, 0)[:, 0:96])
+            before = jnp.concatenate(cells, axis=1)
+            if pre is not None:
+                pre[rows, :] = before
+            after = gelu(before)
+            if edge is not None:
+                row, outside = edge
+                at = t * CHUNK + lax.broadcasted_iota(jnp.int32, after.shape, 0)
+                after = jnp.where((at == row) & outside, 0.0, after)
+            act[rows, :] = after.astype(BF)
+            return 0
+
+        lax.fori_loop(0, ROW_PAD // CHUNK, one, 0)
+
+    me = 2 * x + c
+    part = 128
+
+    def convolve_second(t):
+        rows = slice(t * part, (t + 1) * part)
+        total = tdot(even[rows, :], weight(0), 1, 0)
+        total = total + tdot(odd[rows, :], weight(1), 1, 0)
+        total = total + tdot(even_next[rows, :], weight(2), 1, 0)
+        second[rows, :] = total
+        out = gelu(total) + angles[rows, :]
+        stream[rows, :] = out
+        normed[rows, :] = norm(out, vec[0:1, :], vec[1:2, :])
+
+    def project():
+        for t in range(r // part):
+            rows = slice(t * part, (t + 1) * part)
+            left = normed[rows, :]
+            q[rows, :] = (tdot(left, weight(0), 1, 0) * SCALE).astype(BF)
+            k_own[rows, :] = tdot(left, weight(1), 1, 0).astype(BF)
+            v_own[rows, :] = tdot(left, weight(2), 1, 0).astype(BF)
+        for pair in range(pairs):
+            for cpy in across(pair):
+                cpy.start()
+        k_all[0:r, :] = k_own[...]
+        v_all[0:r, :] = v_own[...]
+
+    def across(pair):
+        at = lanes_of(pair)
+        return [
+            remote(a.at[:, at], b.at[r : 2 * r, at], kxs.at[j, pair], kxr.at[j, pair], xp)
+            for j, (a, b) in enumerate(((k_own, k_all), (v_own, v_all)))
+        ]
+
+    def beside(pair):
+        at = lanes_of(pair)
+        return [
+            remote(a.at[0 : 2 * r, at], a.at[2 * r : 4 * r, at], kcs.at[j, pair], kcr.at[j, pair], cp)
+            for j, a in enumerate((k_all, v_all))
+        ]
+
+    def pass_on(pair):
+        for cpy in across(pair):
+            cpy.wait_recv()
+        for cpy in beside(pair):
+            cpy.start()
+
+    def attend_pair(pair):
+        if pair + 1 < pairs:
+            pass_on(pair + 1)
+        for cpy in beside(pair):
+            cpy.wait_recv()
+        forward_pair(pair, q, k_all, v_all, o, lse, None)
+
+    pieces = [
+        open_small,
+        lambda: convolve(patches[0], even_pre, even, (0, me == 0)),
+        lambda: convolve(patches[1], odd_pre, odd, (r, me == 3)),
+        lambda: convolve(patches[2], None, even_next, None),
+        lambda: fetch((1, 2, 3), (0, 1, 2)),
+    ]
+    pieces += [functools.partial(convolve_second, t) for t in range(r // part)]
+    pieces += [lambda: (fetch((4, 5, 6), (0, 1, 2)), project()), lambda: pass_on(0)]
+    pieces += [functools.partial(attend_pair, pair) for pair in range(pairs)]
+
+    for t in range(n + AHEAD[2]):
+        if t == 0:
+            for i in range(min(n, AHEAD[3])):
+                send_z(i)
+        if t + AHEAD[3] < n:
+            send_z(t + AHEAD[3])
+        if 0 <= t - AHEAD[0] < n:
+            send_1(t - AHEAD[0])
+        if 0 <= t - AHEAD[1] < n:
+            send_2(t - AHEAD[1])
+        if 0 <= t - AHEAD[2] < n:
+            send_core(t - AHEAD[2])
+        if t >= PIECES_FROM and pieces:
+            pieces.pop(0)()
+    while pieces:
+        pieces.pop(0)()
+    for i in range(n):
+        if swaps[i] is not None:
+            swaps[i].wait_send()
+        arrive(i)
+        for key in range(4):
+            for cpy in stages[i, key]:
+                cpy.wait_send()
+    for pair in range(pairs):
+        for cpy in across(pair) + beside(pair):
+            cpy.wait_send()
+
+
+AHEAD = (0, 1, 3, 6)
+PIECES_FROM = 5
+
+
+def gather_and_stem(plan, ins, out_shapes, patches, angles):
+    n, r = len(plan), angles.shape[0]
+    sem = pltpu.SemaphoreType.DMA
+    hbm, vmem = pl.BlockSpec(memory_space=pl.ANY), pl.BlockSpec(memory_space=pltpu.VMEM)
+    got, stage = [], []
+    for _, rows, _, _, kind in plan:
+        got.append(pltpu.VMEM((rows, LANES // 2) if kind == "n" else (16, 128), BF))
+        stage.append(pltpu.VMEM((rows, LANES) if kind == "n" else (16, 128), BF))
+    sems = [sem((n,)), sem((n, 3)), sem((n, 3))] + [sem((n, 2))] * 4 + [sem((n,))] * 4
+    made = [((ROW_PAD, D), F32)] * 2 + [((ROW_PAD, D), BF)] * 3 + [((r, D), F32)] * 2
+    made += [((r, D), BF)] * 2 + [((4 * r, D), BF)] * 2 + [((r, D), BF), ((HEADS, r), F32), ((16, D), F32)]
+    held = [pltpu.VMEM((2, 2, 4, 2, SMALL_ROWS, 128), BF), pltpu.VMEM((3, 4, 2, 2, 48, D), BF)]
+    held += [pltpu.VMEM((r, D), BF)] * 2
+    return pl.pallas_call(
+        functools.partial(stem_kernel, plan, len(ins), len(out_shapes)),
+        out_shape=[jax.ShapeDtypeStruct(s, BF) for s in out_shapes]
+        + [jax.ShapeDtypeStruct(s, t) for s, t in made],
+        in_specs=[vmem] * (len(ins) + 4),
+        out_specs=[hbm] * len(out_shapes) + [vmem] * len(made),
+        scratch_shapes=got + stage + held + sems + [sem((4,))] + [sem((2, HEADS // 2))] * 4,
+        compiler_params=pltpu.CompilerParams(
+            collective_id=1, has_side_effects=True, vmem_limit_bytes=60 << 20
+        ),
+    )(*ins, *patches, angles)
+
+
+def share_kernel(own, out, send, zrecv, xrecv, yrecv, crecv):
+    z, y, x, c = where_am_i()
+    zs, yp, xp, cp = partners(z, y, x, c)
+    greet(zs, yp, xp, cp)
+    here = out.at[x, c, z, y]
+    here[...] = own[...]
+    started = []
+
+    def go(copies):
+        for cpy in copies:
+            cpy.start()
+        for cpy in copies:
+            cpy.wait_recv()
+        started.extend(copies)
+
+    go([remote(own, here, send.at[j], zrecv.at[j], zs[j]) for j in range(3)])
+    line = out.at[x, c, :, y]
+    go([remote(line, line, send.at[3], xrecv.at[0], xp)])
+    plane = out.at[:, c, :, y]
+    go([remote(plane, plane, send.at[4], yrecv.at[0], yp)])
+    half = out.at[:, c]
+    go([remote(half, half, send.at[5], crecv.at[0], cp)])
+    for cpy in started:
+        cpy.wait_send()
+
+
+def share_ids(ids):
+    own = jnp.pad(ids[None], ((0, 7), (0, 128 - ids.size)))
+    sem, vmem = pltpu.SemaphoreType.DMA, pl.BlockSpec(memory_space=pltpu.VMEM)
+    out = pl.pallas_call(
+        share_kernel,
+        out_shape=jax.ShapeDtypeStruct((2, 2, 4, 2, 8, 128), jnp.int32),
+        in_specs=[vmem],
+        out_specs=vmem,
+        scratch_shapes=[sem((6,)), sem((3,)), sem((1,)), sem((1,)), sem((1,))],
+        compiler_params=pltpu.CompilerParams(collective_id=5, has_side_effects=True),
+    )(own)
+    return out[..., 0, : ids.size].transpose(2, 3, 0, 1, 4).reshape(-1)
+
+
+def small_block(shards):
+    w = shards[0]
+    t, i, o = w.shape
+    top = jnp.pad(w.reshape(t * i, o), ((0, 64 - t * i), (0, 128 - o)))
+    rows = jnp.stack([shards[k] for k in VECTORS])
+    rows = jnp.pad(rows, ((0, SMALL_ROWS - 64 - rows.shape[0]), (0, 128 - rows.shape[1])))
+    return jnp.concatenate([top, rows])
+
+
+def patch_rows(patch, mels):
+    p = patch.reshape(patch.shape[0], 3, 4, mels // 4).transpose(0, 2, 1, 3).reshape(patch.shape[0], 4, -1)
+    p = jnp.pad(p, ((0, ROW_PAD - p.shape[0]), (0, 0), (0, 64 - p.shape[2])))
+    return p.reshape(ROW_PAD, 256)
+
+
+def gather_weights(shards, patches, angles):
+    plan, ins, shapes, at = [], [], [], {}
+    for i in SQUARE + (1,) + TALL + (15,):
         w = shards[i]
+        if i == 15:
+            w = jnp.concatenate([w, jnp.zeros((-w.shape[0] % 32, w.shape[1]), BF)])
         rows = w.shape[-2] // 2
-        one = (4, 2, 2, rows, D)
-        for tap in range(w.shape[0]) if w.ndim == 3 else (None,):
-            g.append((0, first, rows, len(shapes), tap, False))
-            first += rows
-        shapes.append(one if w.ndim == 2 else (w.shape[0],) + one)
+        for tap in range(3) if w.ndim == 3 else (None,):
+            at[i, tap] = len(plan)
+            plan.append((len(ins), rows, len(shapes), None, "n"))
+            ins.append(w if tap is None else w[tap])
+            shapes.append((4, 2, 2, rows, D))
     for i in BROAD:
-        rows = shards[i].shape[0]
-        g.append((1, at, rows, len(shapes), None, True))
-        at += rows
-        shapes.append((2, 2, 4, 2, rows, D))
-    g.append((2, 0, MISC_ROWS, len(shapes), None, True))
-    shapes.append((2, 2, 4, 2, MISC_ROWS, D))
-    return g, shapes
-
-
-def by_core(c, zero, one):
-    return jnp.where(c == 0, zero, one)
-
-
-def narrow_halves(shards):
-    parts = []
-    for i in SQUARE + (1,) + TALL:
-        w = shards[i].reshape(-1, 2, shards[i].shape[-2] // 2, shards[i].shape[-1])
-        parts += [w[t] for t in range(w.shape[0])]
-    return jnp.concatenate(parts, axis=1)
-
-
-def gather_weights(shards, ids):
-    c = lax.axis_index("seq") % 2
-    g, shapes = plan_gather(shards)
-    halves = narrow_halves(shards)
-    mine = by_core(c, halves[0], halves[1])
-    got = lax.ppermute(by_core(c, halves[1], halves[0]), "seq", SWAP)
-    narrow = by_core(
-        c, jnp.concatenate([mine, got], axis=1), jnp.concatenate([got, mine], axis=1)
-    )
-    broad = jnp.concatenate([shards[i] for i in BROAD], axis=0)
-    flat = [shards[i].reshape(-1) for i in (0,) + VECTORS + (15,)]
-    flat += [(ids // 256).astype(BF), (ids % 256).astype(BF)]
-    size = sum(f.size for f in flat)
-    flat.append(jnp.zeros((MISC_ROWS * D - size,), BF))
-    misc = jnp.concatenate(flat).reshape(MISC_ROWS, D)
-    outs = gather_fast(g, [narrow, broad, misc], shapes)
+        at[i, None] = len(plan)
+        plan.append((len(ins), shards[i].shape[0], len(shapes), None, "w"))
+        ins.append(shards[i])
+        shapes.append((2, 2, 4, 2) + shards[i].shape)
+    at[0, None] = len(plan)
+    plan.append((len(ins), SMALL_ROWS, len(shapes), None, "w"))
+    ins.append(small_block(shards))
+    shapes.append((2, 2, 4, 2, SMALL_ROWS, 128))
+    first = [at[0, None], at[1, 0], at[1, 1], at[1, 2], at[4, None], at[5, None], at[6, None]]
+    order = first + [k for k in range(len(plan)) if k not in first]
+    outs = gather_and_stem([plan[k] for k in order], ins, shapes, patches, angles)
+    outs, made = outs[: len(plan)], outs[len(plan) :]
     full = [None] * 32
-    for k, i in enumerate(SQUARE + (1,) + TALL):
-        full[i] = outs[k].reshape(shards[i].shape[:-2] + (8 * shards[i].shape[-2], D))
-    for k, i in enumerate(BROAD):
-        full[i] = outs[15 + k].reshape(4, D, D)
-    misc = outs[17].reshape(2, 2, 4, 2, MISC_ROWS * D)
-    at = 0
+    for i in SQUARE + TALL:
+        full[i] = outs[at[i, None]].reshape(-1, D)
+    full[1] = [outs[at[1, tap]].reshape(D, D) for tap in range(3)]
+    r = shards[15].shape[0]
+    full[15] = outs[at[15, None]].reshape(8, -1, D)[:, :r].reshape(8 * r, D)
+    for i in BROAD:
+        full[i] = outs[at[i, None]].reshape(4, D, D)
     t, a, b = shards[0].shape
-    full[0] = (
-        misc[..., : shards[0].size]
-        .reshape(2, 2, 4, 2, t, a, b)
-        .transpose(4, 0, 1, 5, 2, 3, 6)
-        .reshape(t, 4 * a, 8 * b)
-    )
-    at += shards[0].size
-    n = shards[VECTORS[0]].size
-    vecs = misc[..., at : at + n * len(VECTORS)].reshape(2, 2, 4, 2, len(VECTORS), n)
-    vecs = vecs.transpose(4, 2, 3, 0, 1, 5).reshape(len(VECTORS), D)
+    conv1 = outs[at[0, None]][..., : t * a, :b].reshape(2, 2, 4, 2, t, a, b)
+    full[0] = conv1.transpose(4, 0, 1, 5, 2, 3, 6).reshape(t, 4 * a, 8 * b)
     for k, i in enumerate(VECTORS):
-        full[i] = vecs[k]
-    at += n * len(VECTORS)
-    r, w = shards[15].shape
-    full[15] = (
-        misc[..., at : at + r * w]
-        .reshape(2, 2, 4, 2, r, w)
-        .transpose(2, 3, 4, 0, 1, 5)
-        .reshape(8 * r, 4 * w)
-    )
-    at += r * w
-    both = misc[..., at : at + 2 * ids.size].reshape(2, 2, 4, 2, 2, ids.size).astype(jnp.int32)
-    all_ids = (both[..., 0, :] * 256 + both[..., 1, :]).transpose(2, 3, 0, 1, 4).reshape(-1)
-    return full, all_ids
+        full[i] = made[13][k]
+    return full, made[:13]
 
 
 ORDER = (31, 30, 27, 24, 21, 18, 19, 20, 11, 10, 25, 26, 7, 4, 5, 6, 1)
 EXACT = 25
+HEAD_START = 1
+MIX = 2
 
 
 def reduce_grads(grads, shards):
@@ -1145,6 +1315,13 @@
     ins.append(jnp.concatenate(flat, axis=-1).astype(BF).reshape(2, 2, 4, 2, 2, MISC_ROWS // 2, D))
     items.append(("m", BF, len(shapes), None))
     shapes.append((2, MISC_ROWS // 2, D))
+    small = [j for j in jobs if items[j[0]][0] == "n"]
+    large = [j for j in jobs if items[j[0]][0] != "n"]
+    jobs, large = small[:HEAD_START], list(large)
+    for j in small[HEAD_START:]:
+        jobs += large[:MIX] + [j]
+        large = large[MIX:]
+    jobs = jobs[:-1] + large + jobs[-1:]
     got = reduce_fast(items, jobs, ins, shapes)
     out = [None] * 32
     for i, v in zip(ORDER, got):
@@ -1175,40 +1352,53 @@
     fast = dps == 8 and seqs == 4
     weights = shards[:14] + [None] + shards[15:]
     if fast:
-        full, ids = gather_weights(weights, token_ids[0])
+        ids = share_ids(token_ids[0])
     else:
-        full, ids = gather_plain(weights), lax.all_gather(token_ids[0], BOTH, axis=0, tiled=True)
+        ids = lax.all_gather(token_ids[0], BOTH, axis=0, tiled=True)
     hot = one_hot(ids, table)
     looked = mm(hot, table, BF)
+
     mine = lax.psum_scatter(looked, "dp", scatter_dimension=0, tiled=True)
-
-    vec = {i: full[i].astype(F32) for i in range(32) if KINDS[i] == "v"}
-    conv1, conv2, position = full[0].reshape(-1, D), full[1], full[15]
-    eq, ek, ev, eo = full[4:8]
-    ee, ec = full[10:12]
-    dq_w, dk_w, dv_w, do_w = full[18:22]
-    cq_w, ck_w, cv_w, co_w = full[24:28]
-    de, dc = full[30:32]
 
     pairs = extended(mel_frames[0], 2).reshape(frames + 2, -1)
     mels = mel_frames.shape[2]
     n = frames + 1
     even_in = jnp.concatenate([pairs[:n], pairs[1:, :mels]], axis=1)
     odd_in = jnp.concatenate([pairs[:n, mels:], pairs[1:]], axis=1)
-    even_pre, odd_pre = mm(even_in, conv1), mm(odd_in, conv1)
+    angles = sinusoid(me * frames, frames)
     row = jnp.arange(n)[:, None]
     even_keep = (row > 0) | (me > 0)
     odd_keep = (row < n - 1) | (me < seqs - 1)
-    even = jnp.where(even_keep, gelu(even_pre), 0.0).astype(BF)
-    odd = jnp.where(odd_keep, gelu(odd_pre), 0.0).astype(BF)
-    second_pre = mm(even[:frames], conv2[0]) + mm(odd[:frames], conv2[1]) + mm(even[1:], conv2[2])
-    stream0 = gelu(second_pre) + sinusoid(me * frames, frames)
-
-    enc_normed = norm(stream0, vec[2], vec[3])
-    q = (mm(enc_normed, eq) * SCALE).astype(BF)
-    k = mm(enc_normed, ek, BF)
-    v = mm(enc_normed, ev, BF)
-    enc_mixed, enc_lse, k_all, v_all = clip_attend(q, k, v)
+    if fast:
+        patches = [patch_rows(p, mels) for p in (even_in, odd_in, even_in[1:])]
+        patches[0], _ = lax.optimization_barrier((patches[0], looked))
+        full, made = gather_weights(weights, patches, angles)
+        even_pre, odd_pre, even0, odd0, even1, second_pre, stream0, enc_normed, q, k_all, v_all = made[:11]
+        enc_mixed, enc_lse = made[11:]
+        even_pre, odd_pre = even_pre[:n], odd_pre[:n]
+        even0, odd0, even1 = even0[:frames], odd0[:frames], even1[:frames]
+    else:
+        full = gather_plain(weights)
+        conv1, conv2 = full[0].reshape(-1, D), full[1]
+        even_pre, odd_pre = mm(even_in, conv1), mm(odd_in, conv1)
+        even = jnp.where(even_keep, gelu(even_pre), 0.0).astype(BF)
+        odd0 = jnp.where(odd_keep, gelu(odd_pre), 0.0).astype(BF)[:frames]
+        even0, even1 = even[:frames], even[1:]
+        second_pre = mm(even0, conv2[0]) + mm(odd0, conv2[1]) + mm(even1, conv2[2])
+        stream0 = gelu(second_pre) + angles
+        enc_normed = norm(stream0, full[2].astype(F32), full[3].astype(F32))
+        q = (mm(enc_normed, full[4]) * SCALE).astype(BF)
+        k, v = mm(enc_normed, full[5], BF), mm(enc_normed, full[6], BF)
+        enc_mixed, enc_lse, k_all, v_all = clip_attend(q, k, v)
+    vec = {i: full[i].astype(F32) for i in range(32) if KINDS[i] == "v"}
+    conv1, conv2, position = full[0].reshape(-1, D), full[1], full[15]
+    eo = full[7]
+    ee, ec = full[10:12]
+    dq_w, dk_w, dv_w, do_w = full[18:22]
+    cq_w, ck_w, cv_w, co_w = full[24:28]
+    de, dc = full[30:32]
+
+
     stream1 = stream0 + mm(enc_mixed, eo)
     enc_mlp_normed, enc_pre, enc_hidden, stream2 = mlp(stream1, vec[8], vec[9], ee, ec)
     memory = norm(stream2, vec[12], vec[13])
@@ -1305,7 +1495,7 @@
     up = inputs_back(4, 2, enc_normed, stream0, dq, dk, dv, up)
 
     d_second = (gelu_slope(second_pre) * up).astype(BF)
-    grads[1] = ([even[:frames], odd[:frames], even[1:]], d_second)
+    grads[1] = ([even0, odd0, even1], d_second)
     rim = extended(d_second, 1)
     d_even = mm_t(rim[1:], conv2[0]) + mm_t(rim[:n], conv2[2])
     d_odd = mm_t(rim[1:], conv2[1])

time: 889 us -> 839 us (0.944)
  local copies, waits for them, and re-layouts: 123 us -> 98.7 us
  matrix products: 72.7 us -> 58.3 us
    pallas_call x1 -> x2, Pallas kernels: 176 us -> 231 us  [the longest x1 215 us: gather_and_stem(): pl.pallas_call(functools.partial(stem_kernel, plan, len(ins), len(out_sha...]
    pallas_call x7 -> x6, Pallas kernels: 126 us -> 91.1 us  [local_call(): pl.pallas_call(kernel, out_shape=[jax.ShapeDtypeStruct(s, t) for s, t in...]
    pallas_call x1, Pallas kernels: 214 us -> 192 us  [reduce_fast(): pl.pallas_call(functools.partial(reduce_kernel, items, jobs, len(ins), le...]
    dot_general x38 -> x30, matrix products: 72.7 us -> 58.3 us  [dot(): lax.dot_general(a, b, (((ca,), (cb,)), ((), ())), preferred_element_type=...]
    unnamed x362 -> x277, local copies, waits for them, and re-layouts: 54.3 us -> 41.5 us
    convert_element_type x5 -> x3, local copies, waits for them, and re-layouts: 17.3 us -> 8.28 us  [body(): embedded = looked.astype(F32) + position.astype(F32)]
  transfers between devices with their start and end apart: 10 -> 9, of which waited for: 3 -> 3; matrix products, arithmetic and copies ran while one was open for 10% -> 11% of each run, Pallas kernels for 29% -> 57%
where the time goes in v2:
time: 839 us; the launch traced here: 828 us
  Pallas kernels  545 us (65%)
  local copies, waits for them, and re-layouts  98.7 us (12%)
  matrix products  58.3 us (7%)
  other arithmetic  36.8 us (4%)
  blocking collectives  36.8 us (4%)
  starting transfers between devices  26.1 us (3%)
  between operations  17.2 us (2%)
  waiting for transfers between devices  8.68 us (1%)
    pallas_call x1, Pallas kernels, gather_and_stem(): pl.pallas_call(functools.partial(stem_kernel, plan, len(ins), len(out_sha...  215 us
    pallas_call x1, Pallas kernels, reduce_fast(): pl.pallas_call(functools.partial(reduce_kernel, items, jobs, len(ins), le...  192 us
    pallas_call x6, Pallas kernels, local_call(): pl.pallas_call(kernel, out_shape=[jax.ShapeDtypeStruct(s, t) for s, t in...  91.1 us
    dot_general x30, matrix products, dot(): lax.dot_general(a, b, (((ca,), (cb,)), ((), ())), preferred_element_type=...  58.3 us
    unnamed x277, local copies, waits for them, and re-layouts  41.5 us
    pallas_call x4, Pallas kernels, blocks(): pl.pallas_call(kernel, grid=(grid,), out_shape=[jax.ShapeDtypeStruct(s, t...  32.1 us
  transfers between devices with their start and end apart: 9, of which 3 were waited for; matrix products, arithmetic and copies ran while one was open for 11% of the time, Pallas kernels for 57%

profile of v2, /device:TPU:1, one launch (start us, length us, event | category | flops | bytes accessed | tf_op | source)
XLA Modules:
  0.0 828.0 jit_solution(10446620346298530527)
XLA Ops:
  8.2 4.5 collective-permute-start
  15.9 15.3 %shard_map.603 = s32[2,2,4,2,8,128]{5,4,3,2,1,0:T(8,128)} custom-call(s32[8,128]{1,0:T(8,128)} %pad.24.own), custom_call_target="tpu_custom_call" | custom-call | tf_op jit(solution)/shard_map/pallas_call | solution.py:1207
  32.2 10.6 %fusion.4 = bf16[3584,192]{0,1:T(8,128)(2,1)S(1)} fusion(bf16[3264,192]{0,1:T(8,128)(2,1)S(1)} %copy-done, s32[3584]{0:T(1024)S(1)} %sub.147), kind=kOutput, calls=%fused_computation.5 | convolution fusion | flops 4504485888 | bytes 2643968 | tf_op jit(solution)/shard_map/dot_general | solution.py:25
  59.7 215.3 %shard_map.604 = (bf16[4,2,2,48,768]{4,3,2,1,0:T(8,128)(2,1)}, bf16[4,2,2,48,768]{4,3,2,1,0:T(8,128)(2,1)}, bf16[4,2,2,48,768]{4,3,2,1,0:T(8,128)(2,1)}, bf16[4,...) custom-call(bf16[96,192]{1,0:T(8,128)(2,1)} %refs_0_.3, ...), custom_call_target="tpu_custom_call" | custom-call | tf_op jit(solution)/shard_map/pallas_call | solution.py:1165
  290.7 8.6 %shard_map.606 = (bf16[384,768]{1,0:T(8,128)(2,1)S(1)}, f32[4,384,768]{2,1,0:T(8,128)}, bf16[4,384,768]{2,1,0:T(8,128)(2,1)S(1)}, f32[384,768]{1,0:T(8,128)S(1)}) custom-call(f32[384,768]{1,0:T(8,128)S(1)} %convolution_add_fusion.5.stream, f32[1,768]{1,0:T(1,128)S(1)} %get-tuple-element.506.gain, f32[1,768]{1,0:T(1,128)S(1)} %get-tuple-element.515.bias, ...), custom_call_target="tpu_custom_call" | custom-call | flops 3623878656 | bytes 16777216 | tf_op jit(solution)/shard_map/pallas_call | solution.py:870
  308.9 8.7 %all-gather = bf16[4,448,192]{1,2,0:T(8,128)(2,1)S(1)} all-gather(bf16[1,448,192]{1,2,0:T(8,128)(2,1)S(1)} %bitcast.230), channel_id=1, replica_groups=mesh['dp'=8,'seq'=4] {'seq'}, dimensions={0}, use_global_device_ids=true | all-gather | bytes 860160 | tf_op jit(solution)/shard_map/all_gather | solution.py:1409
  331.9 9.1 %shard_map.605 = (bf16[448,768]{1,0:T(8,128)(2,1)}, f32[12,448]{1,0:T(8,128)}) custom-call(s32[1]{0:T(128)} %copy.374.refs_0_, bf16[448,768]{1,0:T(8,128)(2,1)} %fusion.11.refs_1_, bf16[448,768]{1,0:T(8,128)(2,1)} %convolution_convert_fusion.1.refs_2_, bf16[448,768]{1,0:T(8,128)(2,1)} %convolution_convert_fusion.refs_3_), custom_call_target="tpu_custom_call" | custom-call | flops 1233125376 | bytes 8388608 | tf_op jit(solution)/shard_map/pallas_call | solution.py:781
  348.3 9.0 %shard_map.607 = (bf16[448,768]{1,0:T(8,128)(2,1)}, f32[12,448]{1,0:T(8,128)}) custom-call(bf16[448,768]{1,0:T(8,128)(2,1)} %fusion.12.refs_0_.q, bf16[384,768]{1,0:T(8,128)(2,1)} %convolution_convert_fusion.4.refs_1_.k, bf16[384,768]{1,0:T(8,128)(2,1)} %convolution_convert_fusion.3.refs_2_.v), custom_call_target="tpu_custom_call" | custom-call | flops 1056964608 | bytes 8388608 | tf_op jit(solution)/shard_map/pallas_call | solution.py:781
  360.6 4.5 all-to-all-start
  370.1 6.0 all-to-all-done
  388.1 5.6 shard_map.608
  394.7 6.8 shard_map.609
  404.4 9.0 %all_gather.13 = bf16[448,896]{1,0:T(8,128)(2,1)S(1)} all-gather(bf16[112,896]{1,0:T(8,128)(2,1)} %concatenate.55), channel_id=1, replica_groups=mesh['dp'=8,'seq'=4] {'seq'}, dimensions={0}, use_global_device_ids=true | all-gather | bytes 1003520 | tf_op jit(solution)/shard_map/all_gather | solution.py:1454
  416.1 6.1 shard_map.610
  423.0 10.6 %psum.7 = f32[2,12,448]{2,1,0:T(8,128)S(1)} all-reduce(f32[2,12,448]{2,1,0:T(8,128)S(1)} %pad_maximum_fusion.10), channel_id=1, replica_groups=mesh['dp'=8,'seq'=4] {'seq'}, use_global_device_ids=true, to_apply=%region_10.11 | all-reduce | flops 10752 | bytes 86016 | tf_op jit(solution)/shard_map/psum | solution.py:1456
  434.2 11.0 %shard_map.611 = (f32[448,768]{1,0:T(8,128)}, bf16[384,768]{1,0:T(8,128)(2,1)}, bf16[384,768]{1,0:T(8,128)(2,1)}) custom-call(bf16[448,768]{1,0:T(8,128)(2,1)} %fusion.12.refs_0_.q, bf16[384,768]{1,0:T(8,128)(2,1)} %convolution_convert_fusion.4.refs_1_.k, bf16[384,768]{1,0:T(8,128)(2,1)} %convolution_convert_fusion.3.refs_2_.v, ...), custom_call_target="tpu_custom_call" | custom-call | flops 3170893824 | bytes 8388608 | tf_op jit(solution)/shard_map/pallas_call | solution.py:781
  448.5 11.0 %shard_map.612 = (f32[384,768]{1,0:T(8,128)S(1)}, bf16[384,768]{1,0:T(8,128)(2,1)S(1)}, bf16[4,384,768]{2,1,0:T(8,128)(2,1)}, f32[1,768]{1,0:T(1,128)S(1)}, f32[1,768]{1,0:T(1,128)S(1)}) custom-call(f32[384,768]{1,0:T(8,128)S(1)} %subtract_multiply_fusion.up, f32[384,768]{1,0:T(8,128)S(1)} %convolution_add_fusion.5.stream, ...), custom_call_target="tpu_custom_call" | custom-call | flops 3623878656 | bytes 16777216 | tf_op jit(solution)/shard_map/pallas_call | solution.py:870
  460.7 5.9 all-to-all-start.1
  469.4 42.2 %shard_map.613 = (bf16[384,768]{1,0:T(8,128)(2,1)}, bf16[384,768]{1,0:T(8,128)(2,1)}, bf16[384,768]{1,0:T(8,128)(2,1)}) custom-call(bf16[384,768]{1,0:T(8,128)(2,1)} %get-tuple-element.157.q, bf16[1536,768]{1,0:T(8,128)(2,1)} %get-tuple-element.158.k, bf16[1536,768]{1,0:T(8,128)(2,1)} %get-tuple-element.159.v, ...), custom_call_target="tpu_custom_call" | custom-call | flops 10871635968 | bytes 8388608 | tf_op jit(solution)/shard_map/pallas_call | solution.py:781
  539.8 8.4 %all_gather.14.refs_4_ = bf16[448,768]{1,0:T(8,128)(2,1)} all-gather(bf16[112,768]{1,0:T(8,128)(2,1)S(1)} %convolution_convert_fusion.5), channel_id=1, replica_groups=mesh['dp'=8,'seq'=4] {'seq'}, dimensions={0}, use_global_device_ids=true | all-gather | bytes 860160 | tf_op jit(solution)/shard_map/all_gather | solution.py:1465
  548.3 13.7 %shard_map.614 = (bf16[448,768]{1,0:T(8,128)(2,1)}, bf16[448,768]{1,0:T(8,128)(2,1)}, bf16[448,768]{1,0:T(8,128)(2,1)}) custom-call(s32[1]{0:T(128)} %copy.374.refs_0_, bf16[448,768]{1,0:T(8,128)(2,1)} %fusion.11.refs_1_, bf16[448,768]{1,0:T(8,128)(2,1)} %convolution_convert_fusion.1.refs_2_, bf16[448,768]{1,0:T(8,128)(2,1)} %convolution_convert_fusion.refs_3_, ...), custom_call_target="tpu_custom_call" | custom-call | flops 3699376128 | bytes 8388608 | tf_op jit(solution)/shard_map/pallas_call | solution.py:781
  584.1 6.2 concatenate.59
  593.9 191.6 %shard_map.615 = (f32[2,2,2,48,192]{4,3,2,1,0:T(8,128)}, f32[2,48,768]{2,1,0:T(8,128)}, f32[2,48,192]{2,1,0:T(8,128)}, f32[2,48,192]{2,1,0:T(8,128)}, f32[2,48,1...) custom-call(bf16[4,112,768]{2,1,0:T(8,128)(2,1)} %copy-done.3, ...), custom_call_target="tpu_custom_call" | custom-call | tf_op jit(solution)/shard_map/pallas_call | solution.py:549
  794.7 11.5 %fusion = f32[3264,192]{0,1:T(8,128)} fusion(bf16[3584,192]{0,1:T(8,128)(2,1)S(1)} %reshape.586, s32[3584]{0:T(1024)S(1)} %copy-done.91), kind=kOutput, calls=%fused_computation.1 | convolution fusion | flops 4503797760 | bytes 3897344 | tf_op jit(solution)/shard_map/dot_general | solution.py:25
  (497 shorter events, 179.3 us)
Async XLA Ops:
  7.2 25.0 %copy-start = (bf16[3264,192]{0,1:T(8,128)(2,1)S(1)}, bf16[3264,192]{0,1:T(8,128)(2,1)}, u32[]{:S(2)}) copy-start(bf16[3264,192]{0,1:T(8,128)(2,1)} %param.53) | copy-start | bytes 3760132
  7.2 300.6 %reduce-scatter.4.cloned.1.call-start = ((), (), s32[]{:S(2)}) async-start(), calls=%async_computation.5 | async-start | bytes 2064384
  8.2 46.1 %collective-permute-start = (bf16[2,80]{0,1:T(8,128)(2,1)S(1)}, bf16[2,80]{0,1:T(8,128)(2,1)S(1)}, u32[]{:S(2)}, u32[]{:S(2)}) collective-permute-start(bf16[2,80]{0,1:T(8,128)(2,1)S(1)} %get-tuple-element.491), channel_id=1, source_target_pairs={{0,1},{1,2},{2,3},{4,5},{5,6},{6,7},{8,9},{9,10},{10,11},{12,13},{... | collective-permute-start | bytes 968 | tf_op jit(solution)/shard_map/ppermute | solution.py:111
  12.7 41.6 %collective-permute-start.1 = (bf16[2,80]{0,1:T(8,128)(2,1)S(1)}, bf16[2,80]{0,1:T(8,128)(2,1)S(1)}, u32[]{:S(2)}, u32[]{:S(2)}) collective-permute-start(bf16[2,80]{0,1:T(8,128)(2,1)S(1)} %get-tuple-element.492), channel_id=1, source_target_pairs={{1,0},{2,1},{3,2},{5,4},{6,5},{7,6},{9,8},{10,9},{11,10},{13,12},{... | collective-permute-start | bytes 968 | tf_op jit(solution)/shard_map/ppermute | solution.py:111
  32.2 10.6 %copy-start.90 = (s32[3584]{0:T(1024)}, s32[3584]{0:T(1024)S(1)}, u32[]{:S(2)}) copy-start(s32[3584]{0:T(1024)S(1)} %sub.147) | copy-start | bytes 43012
  324.1 18.5 %copy-start.17 = (f32[448,768]{1,0:T(8,128)}, f32[448,768]{1,0:T(8,128)S(1)}, u32[]{:S(2)}) copy-start(f32[448,768]{1,0:T(8,128)S(1)} %bitcast_add_fusion.1) | copy-start | bytes 4128772
  331.9 10.7 %copy-start.21 = (bf16[4,2,2,48,768]{4,3,2,1,0:T(8,128)(2,1)S(1)}, bf16[4,2,2,48,768]{4,3,2,1,0:T(8,128)(2,1)}, u32[]{:S(2)}) copy-start(bf16[4,2,2,48,768]{4,3,2,1,0:T(8,128)(2,1)} %get-tuple-element.132) | copy-start | bytes 3538948
  344.6 23.3 %copy-start.96 = (f32[112]{0:T(128)}, f32[112]{0:T(128)S(1)}, u32[]{:S(2)}) copy-start(f32[112]{0:T(128)S(1)} %broadcast_multiply_fusion.13) | copy-start | bytes 1348
  360.6 15.6 %all-to-all-start = ((bf16[4,112,896]{2,1,0:T(8,128)(2,1)}), bf16[4,112,896]{2,1,0:T(8,128)(2,1)}, u32[]{:S(2)}, u32[]{:S(2)}) async-start(bf16[4,112,896]{2,1,0:T(8,128)(2,1)} %bitcast.197), calls=%async_computation | async-start | bytes 1605632 | tf_op jit(solution)/shard_map/all_to_all | solution.py:122
  386.4 7.4 copy-start.42
  394.7 8.4 %copy-start.20 = (bf16[4,2,2,48,768]{4,3,2,1,0:T(8,128)(2,1)S(1)}, bf16[4,2,2,48,768]{4,3,2,1,0:T(8,128)(2,1)}, u32[]{:S(2)}) copy-start(bf16[4,2,2,48,768]{4,3,2,1,0:T(8,128)(2,1)} %get-tuple-element.143) | copy-start | bytes 3538948
  403.1 10.3 %copy-start.39 = (bf16[112,768]{1,0:T(8,128)(2,1)}, bf16[112,768]{1,0:T(8,128)(2,1)S(1)}, u32[]{:S(2)}) copy-start(bf16[112,768]{1,0:T(8,128)(2,1)S(1)} %convert_element_type.236.refs_5_) | copy-start | bytes 516100
  434.2 11.0 %copy-start.59 = (bf16[4,2,2,48,768]{4,3,2,1,0:T(8,128)(2,1)S(1)}, bf16[4,2,2,48,768]{4,3,2,1,0:T(8,128)(2,1)}, u32[]{:S(2)}) copy-start(bf16[4,2,2,48,768]{4,3,2,1,0:T(8,128)(2,1)} %get-tuple-element.139) | copy-start | bytes 3538948
  460.7 73.1 %all-to-all-start.1 = ((f32[4,112,768]{2,1,0:T(8,128)}), f32[4,112,768]{2,1,0:T(8,128)}, u32[]{:S(2)}, u32[]{:S(2)}) async-start(f32[4,112,768]{2,1,0:T(8,128)} %bitcast.201), calls=%async_computation.1 | async-start | bytes 2752512 | tf_op jit(solution)/shard_map/all_to_all | solution.py:122
  469.4 44.2 %copy-start.54 = (bf16[4,2,2,48,768]{4,3,2,1,0:T(8,128)(2,1)S(1)}, bf16[4,2,2,48,768]{4,3,2,1,0:T(8,128)(2,1)}, u32[]{:S(2)}) copy-start(bf16[4,2,2,48,768]{4,3,2,1,0:T(8,128)(2,1)} %get-tuple-element.162) | copy-start | bytes 3538948
  522.0 6.9 collective-permute-start.3
  527.0 4.9 collective-permute-start.2
  538.2 10.1 %copy-start.41 = (bf16[112,768]{1,0:T(8,128)(2,1)}, bf16[112,768]{1,0:T(8,128)(2,1)S(1)}, u32[]{:S(2)}) copy-start(bf16[112,768]{1,0:T(8,128)(2,1)S(1)} %get-tuple-element.473.refs_9_) | copy-start | bytes 516100
  548.3 14.8 %copy-start.50 = (bf16[4,2,2,48,768]{4,3,2,1,0:T(8,128)(2,1)S(1)}, bf16[4,2,2,48,768]{4,3,2,1,0:T(8,128)(2,1)}, u32[]{:S(2)}) copy-start(bf16[4,2,2,48,768]{4,3,2,1,0:T(8,128)(2,1)} %get-tuple-element.128) | copy-start | bytes 3538948
  569.3 8.0 all-to-all-start.2
  572.8 217.7 %all-gather.4.cloned.1.call-start = ((), (), s32[]{:S(2)}) async-start(), calls=%async_computation.4 | async-start | bytes 1769472 | tf_op jit(solution)/shard_map/all_gather | solution.py:1480
  794.7 11.6 %copy-start.19 = (bf16[8,448,192]{1,2,0:T(8,128)(2,1)S(1)}, bf16[8,448,192]{1,2,0:T(8,128)(2,1)}, u32[]{:S(2)}) copy-start(bf16[8,448,192]{1,2,0:T(8,128)(2,1)} %all-gather.4.cloned.1.call-done) | copy-start | bytes 4128772
  808.9 7.9 copy-start.79
  810.6 7.5 copy-start.77
  (103 other events, 287.7 us)
Sparse Core Ops, SparseCore 0:
  45.3 81.1 reduce-scatter.3
  578.4 53.9 all-gather.3

commit v3 on v2

--- a/solution.py
+++ b/solution.py
@@ -300,15 +300,15 @@
             (4, 2, 2, RB, LANES),
             (3, 2, 2, RB, LANES),
         ]
-    r = RB if kind == "w" else MISC_ROWS // 2
+    w = D if kind == "w" else 128
     return [
-        (2, 4, 2, 2, r, D),
-        (2, 4, r, D),
-        (4, 2, r, D),
-        (4, r, D),
-        (4, r, D),
-        (4, 2, r, D),
-        (3, 2, r, D),
+        (2, 4, 2, 2, RB, w),
+        (2, 4, RB, w),
+        (4, 2, RB, w),
+        (4, RB, w),
+        (4, RB, w),
+        (4, 2, RB, w),
+        (3, 2, RB, w),
     ]
 
 
@@ -350,6 +350,8 @@
         xsrc, ysrc = ins[xi], ins[yi]
         if len(xsrc.shape) == 3:
             xsrc = xsrc.at[part]
+        elif xsrc.shape[0] > rows:
+            xsrc = xsrc.at[0:rows]
         if len(ysrc.shape) == 3:
             ysrc = ysrc.at[2 * (part // 2) + (c if part % 2 else 1 - c)]
         pair = []
@@ -540,17 +542,18 @@
     scratch += [
         pltpu.VMEM((RING, 4, 2, 2, RB, D), BF),
         pltpu.VMEM((4, 2, 2, RB, D), F32),
-        pltpu.VMEM((2, 4, 2, 2, MISC_ROWS // 2, D), BF),
+        pltpu.VMEM((2, 4, 2, 2, RB, 128), BF),
     ]
     most = max(j[4] for j in jobs)
     scratch += [pltpu.VMEM((2, most, D), BF)] * 2
     scratch += [sem((2, 3)), sem((m + 1,)), sem((m + 1,))]
     scratch += [sem((n, 2))] * 4 + [sem((n, 3))] * 2 + [sem((n,))] * 2
+    vmem = pl.BlockSpec(memory_space=pltpu.VMEM)
     return pl.pallas_call(
         functools.partial(reduce_kernel, items, jobs, len(ins), len(out_shapes)),
         out_shape=[jax.ShapeDtypeStruct(s, F32) for s in out_shapes],
         in_specs=[pl.BlockSpec(memory_space=pl.ANY)] * len(ins),
-        out_specs=[pl.BlockSpec(memory_space=pltpu.VMEM)] * len(out_shapes),
+        out_specs=[vmem] * len(out_shapes),
         scratch_shapes=scratch,
         compiler_params=pltpu.CompilerParams(
             collective_id=2, has_side_effects=True, vmem_limit_bytes=62 << 20
@@ -899,7 +902,6 @@
 TALL = (11, 31)
 BROAD = (10, 30)
 VECTORS = tuple(i for i in range(32) if KINDS[i] == "v")
-MISC_ROWS = 32
 
 
 ROW_PAD = 400
@@ -911,16 +913,17 @@
     return rows // 2 if rows % 32 == 0 else 16 + 16 * (i % 2)
 
 
-def stem_kernel(plan, inputs, outputs, *refs):
+def stem_kernel(plan, inputs, outputs, rows_held, *refs):
     n = len(plan)
     ins, refs = refs[:inputs], refs[inputs:]
-    patches, angles, refs = refs[:3], refs[3], refs[4:]
+    patches, angles, table, refs = refs[:3], refs[3], refs[4], refs[5:]
     outs, refs = refs[:outputs], refs[outputs:]
     even_pre, odd_pre, even, odd, even_next, second, stream, normed, q, k_all, v_all, o, lse, vec = refs[:14]
+    looked, refs = refs[14], refs[:14] + refs[15:]
     got, stage, refs = refs[14 : 14 + n], refs[14 + n : 14 + 2 * n], refs[14 + 2 * n :]
-    small, weights, k_own, v_own = refs[:4]
-    lsem, zsend, zrecv, xsend, xrecv, ysend, yrecv, csend, crecv, psend, precv = refs[4:15]
-    wsem, kxs, kxr, kcs, kcr = refs[15:]
+    small, weights, k_own, v_own, found, heard, strips = refs[:7]
+    lsem, zsend, zrecv, xsend, xrecv, ysend, yrecv, csend, crecv, psend, precv = refs[7:18]
+    wsem, kxs, kxr, kcs, kcr, tsend, trecv, usend, urecv = refs[18:]
     z, y, x, c = where_am_i()
     zs, yp, xp, cp = partners(z, y, x, c)
     greet(zs, yp, xp, cp)
@@ -1055,6 +1058,58 @@
 
     me = 2 * x + c
     part = 128
+    slots = looked.shape[0]
+    eighth = slots // 8
+
+    def other_clip(m):
+        return lax.rem(z + m // 2, 4), lax.rem(y + m % 2, 2)
+
+    def tell(m):
+        zt, yt = other_clip(m)
+        return remote(found.at[m], heard.at[m], tsend.at[m], trecv.at[m], (zt * 2 + yt, 2 * x + c))
+
+    def look_up(m):
+        zt, yt = other_clip(m)
+        cells = []
+        for s in range(4):
+            for half in (0, 1):
+                code = small[s // 2, s % 2, zt, yt, 0:64, 96:128].astype(F32)[0:eighth]
+                cells.append(code[:, 2 * half : 2 * half + 1] * 256.0 + code[:, 2 * half + 1 : 2 * half + 2])
+        first = (z * 2 + y) * rows_held
+        place = jnp.concatenate(cells, axis=0).astype(jnp.int32) - first
+
+        def one(k, total):
+            lane = lax.broadcasted_iota(jnp.int32, (slots, 384), 1) + k * 384
+            hot = jnp.where((lane == place) & (lane < rows_held), 1.0, 0.0).astype(BF)
+            return total + tdot(hot, table[pl.ds(pl.multiple_of(k * 384, 384), 384), :], 1, 0)
+
+        total = lax.fori_loop(0, table.shape[0] // 384, one, jnp.zeros((slots, D // 4), F32))
+        if m == 0:
+            heard[0] = total.astype(BF)
+        else:
+            found[m] = total.astype(BF)
+            tell(m).start()
+
+    def strip(over):
+        if over == 0:
+            return remote(strips.at[x, c], strips.at[x, c], usend.at[0], urecv.at[0], xp)
+        return remote(strips.at[:, c], strips.at[:, c], usend.at[1], urecv.at[1], cp)
+
+    def sum_found():
+        total = heard[0].astype(F32)
+        for m in range(1, 8):
+            tell(m).wait_recv()
+            total = total + heard[m].astype(F32)
+        strips[x, c] = total.astype(BF)
+        strip(0).start()
+
+    def pass_strips():
+        strip(0).wait_recv()
+        strip(1).start()
+
+    def join_strips():
+        strip(1).wait_recv()
+        looked[...] = jnp.concatenate([strips[s // 2, s % 2] for s in range(4)], axis=1)
 
     def convolve_second(t):
         rows = slice(t * part, (t + 1) * part)
@@ -1109,13 +1164,18 @@
     pieces = [
         open_small,
         lambda: convolve(patches[0], even_pre, even, (0, me == 0)),
+        lambda: (look_up(0), look_up(1)),
         lambda: convolve(patches[1], odd_pre, odd, (r, me == 3)),
+        lambda: (look_up(2), look_up(3)),
         lambda: convolve(patches[2], None, even_next, None),
-        lambda: fetch((1, 2, 3), (0, 1, 2)),
+        lambda: (look_up(4), look_up(5)),
+        lambda: (fetch((1, 2, 3), (0, 1, 2)), convolve_second(0)),
     ]
-    pieces += [functools.partial(convolve_second, t) for t in range(r // part)]
-    pieces += [lambda: (fetch((4, 5, 6), (0, 1, 2)), project()), lambda: pass_on(0)]
-    pieces += [functools.partial(attend_pair, pair) for pair in range(pairs)]
+    pieces += [functools.partial(convolve_second, t) for t in range(1, r // part)]
+    pieces += [lambda: (fetch((4, 5, 6), (0, 1, 2)), project()), lambda: (look_up(6), look_up(7))]
+    pieces += [lambda: (pass_on(0), sum_found()), lambda: (attend_pair(0), pass_strips())]
+    pieces += [lambda: (attend_pair(1), join_strips())]
+    pieces += [functools.partial(attend_pair, pair) for pair in range(2, pairs)]
 
     for t in range(n + AHEAD[2]):
         if t == 0:
@@ -1143,13 +1203,17 @@
     for pair in range(pairs):
         for cpy in across(pair) + beside(pair):
             cpy.wait_send()
+    for m in range(1, 8):
+        tell(m).wait_send()
+    strip(0).wait_send()
+    strip(1).wait_send()
 
 
 AHEAD = (0, 1, 3, 6)
 PIECES_FROM = 5
 
 
-def gather_and_stem(plan, ins, out_shapes, patches, angles):
+def gather_and_stem(plan, ins, out_shapes, patches, angles, table, slots, rows_held):
     n, r = len(plan), angles.shape[0]
     sem = pltpu.SemaphoreType.DMA
     hbm, vmem = pl.BlockSpec(memory_space=pl.ANY), pl.BlockSpec(memory_space=pltpu.VMEM)
@@ -1160,65 +1224,30 @@
     sems = [sem((n,)), sem((n, 3)), sem((n, 3))] + [sem((n, 2))] * 4 + [sem((n,))] * 4
     made = [((ROW_PAD, D), F32)] * 2 + [((ROW_PAD, D), BF)] * 3 + [((r, D), F32)] * 2
     made += [((r, D), BF)] * 2 + [((4 * r, D), BF)] * 2 + [((r, D), BF), ((HEADS, r), F32), ((16, D), F32)]
+    made += [((slots, D), BF)]
     held = [pltpu.VMEM((2, 2, 4, 2, SMALL_ROWS, 128), BF), pltpu.VMEM((3, 4, 2, 2, 48, D), BF)]
-    held += [pltpu.VMEM((r, D), BF)] * 2
+    held += [pltpu.VMEM((r, D), BF)] * 2 + [pltpu.VMEM((8, slots, D // 4), BF)] * 2
+    held += [pltpu.VMEM((2, 2, slots, D // 4), BF)]
     return pl.pallas_call(
-        functools.partial(stem_kernel, plan, len(ins), len(out_shapes)),
+        functools.partial(stem_kernel, plan, len(ins), len(out_shapes), rows_held),
         out_shape=[jax.ShapeDtypeStruct(s, BF) for s in out_shapes]
         + [jax.ShapeDtypeStruct(s, t) for s, t in made],
-        in_specs=[vmem] * (len(ins) + 4),
+        in_specs=[vmem] * (len(ins) + 5),
         out_specs=[hbm] * len(out_shapes) + [vmem] * len(made),
-        scratch_shapes=got + stage + held + sems + [sem((4,))] + [sem((2, HEADS // 2))] * 4,
+        scratch_shapes=got + stage + held + sems + [sem((4,))] + [sem((2, HEADS // 2))] * 4 + [sem((8,))] * 2 + [sem((2,))] * 2,
         compiler_params=pltpu.CompilerParams(
             collective_id=1, has_side_effects=True, vmem_limit_bytes=60 << 20
         ),
-    )(*ins, *patches, angles)
-
-
-def share_kernel(own, out, send, zrecv, xrecv, yrecv, crecv):
-    z, y, x, c = where_am_i()
-    zs, yp, xp, cp = partners(z, y, x, c)
-    greet(zs, yp, xp, cp)
-    here = out.at[x, c, z, y]
-    here[...] = own[...]
-    started = []
-
-    def go(copies):
-        for cpy in copies:
-            cpy.start()
-        for cpy in copies:
-            cpy.wait_recv()
-        started.extend(copies)
-
-    go([remote(own, here, send.at[j], zrecv.at[j], zs[j]) for j in range(3)])
-    line = out.at[x, c, :, y]
-    go([remote(line, line, send.at[3], xrecv.at[0], xp)])
-    plane = out.at[:, c, :, y]
-    go([remote(plane, plane, send.at[4], yrecv.at[0], yp)])
-    half = out.at[:, c]
-    go([remote(half, half, send.at[5], crecv.at[0], cp)])
-    for cpy in started:
-        cpy.wait_send()
-
-
-def share_ids(ids):
-    own = jnp.pad(ids[None], ((0, 7), (0, 128 - ids.size)))
-    sem, vmem = pltpu.SemaphoreType.DMA, pl.BlockSpec(memory_space=pltpu.VMEM)
-    out = pl.pallas_call(
-        share_kernel,
-        out_shape=jax.ShapeDtypeStruct((2, 2, 4, 2, 8, 128), jnp.int32),
-        in_specs=[vmem],
-        out_specs=vmem,
-        scratch_shapes=[sem((6,)), sem((3,)), sem((1,)), sem((1,)), sem((1,))],
-        compiler_params=pltpu.CompilerParams(collective_id=5, has_side_effects=True),
-    )(own)
-    return out[..., 0, : ids.size].transpose(2, 3, 0, 1, 4).reshape(-1)
-
-
-def small_block(shards):
+    )(*ins, *patches, angles, table)
+
+
+def small_block(shards, ids):
     w = shards[0]
     t, i, o = w.shape
-    top = jnp.pad(w.reshape(t * i, o), ((0, 64 - t * i), (0, 128 - o)))
+    halves = ids.reshape(2, -1)
+    codes = jnp.stack([halves[0] // 256, halves[0] % 256, halves[1] // 256, halves[1] % 256], axis=1)
+    codes = jnp.pad(codes.astype(BF), ((0, 64 - codes.shape[0]), (0, 32 - 4)))
+    top = jnp.concatenate([jnp.pad(w.reshape(t * i, o), ((0, 64 - t * i), (0, 0))), codes], axis=1)
     rows = jnp.stack([shards[k] for k in VECTORS])
     rows = jnp.pad(rows, ((0, SMALL_ROWS - 64 - rows.shape[0]), (0, 128 - rows.shape[1])))
     return jnp.concatenate([top, rows])
@@ -1230,7 +1259,7 @@
     return p.reshape(ROW_PAD, 256)
 
 
-def gather_weights(shards, patches, angles):
+def gather_weights(shards, patches, angles, ids, table):
     plan, ins, shapes, at = [], [], [], {}
     for i in SQUARE + (1,) + TALL + (15,):
         w = shards[i]
@@ -1249,11 +1278,13 @@
         shapes.append((2, 2, 4, 2) + shards[i].shape)
     at[0, None] = len(plan)
     plan.append((len(ins), SMALL_ROWS, len(shapes), None, "w"))
-    ins.append(small_block(shards))
+    ins.append(small_block(shards, ids))
     shapes.append((2, 2, 4, 2, SMALL_ROWS, 128))
     first = [at[0, None], at[1, 0], at[1, 1], at[1, 2], at[4, None], at[5, None], at[6, None]]
     order = first + [k for k in range(len(plan)) if k not in first]
-    outs = gather_and_stem([plan[k] for k in order], ins, shapes, patches, angles)
+    rows_held = table.shape[0]
+    table = jnp.pad(table, ((0, -rows_held % 384), (0, 0)))
+    outs = gather_and_stem([plan[k] for k in order], ins, shapes, patches, angles, table, 4 * ids.size, rows_held)
     outs, made = outs[: len(plan)], outs[len(plan) :]
     full = [None] * 32
     for i in SQUARE + TALL:
@@ -1264,11 +1295,15 @@
     for i in BROAD:
         full[i] = outs[at[i, None]].reshape(4, D, D)
     t, a, b = shards[0].shape
-    conv1 = outs[at[0, None]][..., : t * a, :b].reshape(2, 2, 4, 2, t, a, b)
+    small = outs[at[0, None]]
+    codes = small[..., : ids.size // 2, 96:100].astype(jnp.int32)
+    all_ids = jnp.stack([codes[..., 2 * h] * 256 + codes[..., 2 * h + 1] for h in (0, 1)], axis=4)
+    all_ids = all_ids.transpose(2, 3, 0, 1, 4, 5).reshape(-1)
+    conv1 = small[..., : t * a, :b].reshape(2, 2, 4, 2, t, a, b)
     full[0] = conv1.transpose(4, 0, 1, 5, 2, 3, 6).reshape(t, 4 * a, 8 * b)
     for k, i in enumerate(VECTORS):
         full[i] = made[13][k]
-    return full, made[:13]
+    return full, made[:13], all_ids, made[14]
 
 
 ORDER = (31, 30, 27, 24, 21, 18, 19, 20, 11, 10, 25, 26, 7, 4, 5, 6, 1)
@@ -1298,7 +1333,7 @@
             shapes.append((2, RB, D))
         elif i == 1:
             for tap, l in enumerate(left):
-                jobs.append((len(items), 0, place(l), place(right), l.shape[0]))
+                jobs.append((len(items), 0, place(l), place(right), right.shape[0]))
                 items.append(("n", BF, len(shapes), tap))
             shapes.append((3, 2, RB, LANES // 2))
         else:
@@ -1306,15 +1341,15 @@
             items.append(("n", F32 if i == EXACT else BF, len(shapes), None))
             shapes.append((2, RB, LANES // 2))
     t, a, b = shards[0].shape
-    conv1 = grads[0].reshape(t, 2, 2, a, 4, 2, b).transpose(1, 2, 4, 5, 0, 3, 6)
+    conv1 = grads[0].reshape(t, 2, 2, a, 4, 2, b).transpose(1, 2, 4, 5, 0, 3, 6).reshape(2, 2, 4, 2, t * a, b)
     n = shards[VECTORS[0]].size
-    vecs = jnp.stack([grads[i] for i in VECTORS]).reshape(-1, 4, 2, 2, 2, n)
-    flat = [conv1.reshape(2, 2, 4, 2, -1), vecs.transpose(3, 4, 1, 2, 0, 5).reshape(2, 2, 4, 2, -1)]
-    size = sum(f.shape[-1] for f in flat)
-    flat.append(jnp.zeros((2, 2, 4, 2, MISC_ROWS * D - size), F32))
-    ins.append(jnp.concatenate(flat, axis=-1).astype(BF).reshape(2, 2, 4, 2, 2, MISC_ROWS // 2, D))
+    vecs = jnp.stack([grads[i] for i in VECTORS]).reshape(-1, 4, 2, 2, 2, n).transpose(3, 4, 1, 2, 0, 5)
+    none = ((0, 0),) * 4
+    conv1 = jnp.pad(conv1.astype(BF), none + ((0, 64 - t * a), (0, 128 - b)))
+    vecs = jnp.pad(vecs.astype(BF), none + ((0, SMALL_ROWS - 64 - len(VECTORS)), (0, 128 - n)))
+    ins.append(jnp.concatenate([conv1, vecs], axis=4).reshape(2, 2, 4, 2, 2, RB, 128))
     items.append(("m", BF, len(shapes), None))
-    shapes.append((2, MISC_ROWS // 2, D))
+    shapes.append((2, RB, 128))
     small = [j for j in jobs if items[j[0]][0] == "n"]
     large = [j for j in jobs if items[j[0]][0] != "n"]
     jobs, large = small[:HEAD_START], list(large)
@@ -1326,12 +1361,10 @@
     out = [None] * 32
     for i, v in zip(ORDER, got):
         out[i] = v.reshape(shards[i].shape)
-    misc = got[-1].reshape(-1)
-    out[0] = misc[: shards[0].size].reshape(shards[0].shape)
-    at = shards[0].size
-    for i in VECTORS:
-        out[i] = misc[at : at + n]
-        at += n
+    small = got[-1].reshape(SMALL_ROWS, 128)
+    out[0] = small[: t * a, :b].reshape(t, a, b)
+    for k, i in enumerate(VECTORS):
+        out[i] = small[64 + k, :n]
     return out
 
 
@@ -1351,15 +1384,6 @@
 
     fast = dps == 8 and seqs == 4
     weights = shards[:14] + [None] + shards[15:]
-    if fast:
-        ids = share_ids(token_ids[0])
-    else:
-        ids = lax.all_gather(token_ids[0], BOTH, axis=0, tiled=True)
-    hot = one_hot(ids, table)
-    looked = mm(hot, table, BF)
-
-    mine = lax.psum_scatter(looked, "dp", scatter_dimension=0, tiled=True)
-
     pairs = extended(mel_frames[0], 2).reshape(frames + 2, -1)
     mels = mel_frames.shape[2]
     n = frames + 1
@@ -1371,12 +1395,9 @@
     odd_keep = (row < n - 1) | (me < seqs - 1)
     if fast:
         patches = [patch_rows(p, mels) for p in (even_in, odd_in, even_in[1:])]
-        patches[0], _ = lax.optimization_barrier((patches[0], looked))
-        full, made = gather_weights(weights, patches, angles)
+        full, made, ids, looked = gather_weights(weights, patches, angles, token_ids[0], table)
         even_pre, odd_pre, even0, odd0, even1, second_pre, stream0, enc_normed, q, k_all, v_all = made[:11]
         enc_mixed, enc_lse = made[11:]
-        even_pre, odd_pre = even_pre[:n], odd_pre[:n]
-        even0, odd0, even1 = even0[:frames], odd0[:frames], even1[:frames]
     else:
         full = gather_plain(weights)
         conv1, conv2 = full[0].reshape(-1, D), full[1]
@@ -1390,6 +1411,10 @@
         q = (mm(enc_normed, full[4]) * SCALE).astype(BF)
         k, v = mm(enc_normed, full[5], BF), mm(enc_normed, full[6], BF)
         enc_mixed, enc_lse, k_all, v_all = clip_attend(q, k, v)
+        ids = lax.all_gather(token_ids[0], BOTH, axis=0, tiled=True)
+        looked = lax.psum_scatter(mm(one_hot(ids, table), table, BF), "dp", scatter_dimension=0, tiled=True)
+        looked = lax.all_gather(looked, "seq", axis=0, tiled=True)
+        looked = looked.reshape(seqs, all_slots, D // seqs).transpose(1, 0, 2).reshape(all_slots, D)
     vec = {i: full[i].astype(F32) for i in range(32) if KINDS[i] == "v"}
     conv1, conv2, position = full[0].reshape(-1, D), full[1], full[15]
     eo = full[7]
@@ -1405,9 +1430,6 @@
     mk = mm(memory, ck_w, BF)
     mv = mm(memory, cv_w, BF)
 
-    mine, enc_mixed = lax.optimization_barrier((mine, enc_mixed))
-    looked = lax.all_gather(mine, "seq", axis=0, tiled=True)
-    looked = looked.reshape(seqs, all_slots, D // seqs).transpose(1, 0, 2).reshape(all_slots, D)
     place = jnp.arange(all_slots)
     embedded = looked.astype(F32) + position.astype(F32)
     dec_normed = norm(embedded, vec[16], vec[17])
@@ -1477,12 +1499,6 @@
     up = inputs_back(18, 16, own(dec_normed), own(embedded), own(dsq), own(dsk), own(dsv), up)
 
     cols = exchange_columns(up.astype(BF))
-    every = lax.all_gather(cols, "dp", axis=0, tiled=True)
-    grad_table = dot(hot, every, 0, 0)
-    per_clip = every.reshape(dps, dps, -1, D // seqs)
-    grad_position = jnp.sum(
-        lax.dynamic_index_in_dim(per_clip, lax.axis_index("dp"), 1, False).astype(F32), axis=0
-    )
 
     grads[25] = (memory, dmk)
     grads[26] = (memory, dmv)
@@ -1497,24 +1513,34 @@
     d_second = (gelu_slope(second_pre) * up).astype(BF)
     grads[1] = ([even0, odd0, even1], d_second)
     rim = extended(d_second, 1)
-    d_even = mm_t(rim[1:], conv2[0]) + mm_t(rim[:n], conv2[2])
+    padded = even_pre.shape[0]
+    rim = jnp.pad(rim, ((0, padded + 1 - rim.shape[0]), (0, 0)))
+    row = jnp.arange(padded)[:, None]
+    even_keep = ((row > 0) | (me > 0)) & (row < n)
+    odd_keep = (row < n - 1) | ((me < seqs - 1) & (row < n))
+    d_even = mm_t(rim[1:], conv2[0]) + mm_t(rim[:padded], conv2[2])
     d_odd = mm_t(rim[1:], conv2[1])
     d_even = jnp.where(even_keep, gelu_slope(even_pre) * low(d_even), 0.0).astype(BF)
     d_odd = jnp.where(odd_keep, gelu_slope(odd_pre) * low(d_odd), 0.0).astype(BF)
-    grads[0] = (outer(odd_in[:frames], d_odd[:frames], F32) + outer(even_in[1:], d_even[1:], F32)).reshape(
+    grads[0] = (outer(odd_in[:frames], d_odd[:frames], F32) + outer(even_in[1:], d_even[1:n], F32)).reshape(
         3, mels, D
     )
     me_g, mo_g = mm_t(d_even, conv1), mm_t(d_odd, conv1)
     mel_grad = jnp.concatenate(
         [
-            me_g[1:, :mels] + me_g[:-1, 2 * mels :] + mo_g[:-1, mels : 2 * mels],
-            me_g[1:, mels : 2 * mels] + mo_g[1:, :mels] + mo_g[:-1, 2 * mels :],
+            me_g[1:n, :mels] + me_g[: n - 1, 2 * mels :] + mo_g[: n - 1, mels : 2 * mels],
+            me_g[1:n, mels : 2 * mels] + mo_g[1:n, :mels] + mo_g[: n - 1, 2 * mels :],
         ],
         axis=1,
     ).reshape(1, 2 * frames, mels)
 
+    every = lax.all_gather(cols, "dp", axis=0, tiled=True)
     done = (reduce_grads if fast else reduce_plain)(grads, shards)
-    done[14], done[15] = grad_table, grad_position
+    done[14] = dot(one_hot(ids, table), every, 0, 0)
+    per_clip = every.reshape(dps, dps, -1, D // seqs)
+    done[15] = jnp.sum(
+        lax.dynamic_index_in_dim(per_clip, lax.axis_index("dp"), 1, False).astype(F32), axis=0
+    )
     return tuple([decoded[None], mel_grad] + done)
 
 

time: 839 us -> 797 us (0.950)
  local copies, waits for them, and re-layouts: 98.7 us -> 83.4 us
  matrix products: 58.3 us -> 47.4 us
  waiting for transfers between devices: 8.68 us -> 19.3 us
  blocking collectives: 36.8 us -> 28.2 us
    pallas_call x1 -> x0, Pallas kernels: 15.3 us -> none  [share_ids(): pl.pallas_call(share_kernel, out_shape=jax.ShapeDtypeStruct((2, 2, 4, 2,...]
    dot_general x30 -> x29, matrix products: 58.3 us -> 47.4 us  [dot(): lax.dot_general(a, b, (((ca,), (cb,)), ((), ())), preferred_element_type=...]
    convert_element_type x4 -> x2, local copies, waits for them, and re-layouts: 10.2 us -> 0.88 us  [reduce_grads(): conv1 = jnp.pad(conv1.astype(BF), none + ((0, 64 - t * a), (0, 128 - b)))]
    all_to_all x2, waiting for transfers between devices: 6.01 us -> 15.1 us  [exchange(): got = lax.all_to_all(v, 'seq', split_axis=0, concat_axis=0, tiled=True)]
    all_gather x1 -> x0, blocking collectives: 8.72 us -> none  [body(): looked = lax.all_gather(mine, 'seq', axis=0, tiled=True)]
    unnamed x277 -> x283, local copies, waits for them, and re-layouts: 41.5 us -> 42 us
  transfers between devices with their start and end apart: 9 -> 8, of which waited for: 3 -> 3; matrix products, arithmetic and copies ran while one was open for 11% -> 5% of each run, Pallas kernels for 57% -> 25%
where the time goes in v3:
time: 797 us; the launch traced here: 791 us
  Pallas kernels  538 us (68%)
  local copies, waits for them, and re-layouts  83.4 us (10%)
  matrix products  47.4 us (6%)
  other arithmetic  34.1 us (4%)
  blocking collectives  28.2 us (4%)
  starting transfers between devices  24.1 us (3%)
  waiting for transfers between devices  19.3 us (2%)
  between operations  16.7 us (2%)
    pallas_call x1, Pallas kernels, gather_and_stem(): pl.pallas_call(functools.partial(stem_kernel, plan, len(ins), len(out_sha...  222 us
    pallas_call x1, Pallas kernels, reduce_fast(): pl.pallas_call(functools.partial(reduce_kernel, items, jobs, len(ins), le...  195 us
    pallas_call x6, Pallas kernels, local_call(): pl.pallas_call(kernel, out_shape=[jax.ShapeDtypeStruct(s, t) for s, t in...  89.2 us
    dot_general x29, matrix products, dot(): lax.dot_general(a, b, (((ca,), (cb,)), ((), ())), preferred_element_type=...  47.4 us
    unnamed x283, local copies, waits for them, and re-layouts  42 us
    pallas_call x4, Pallas kernels, blocks(): pl.pallas_call(kernel, grid=(grid,), out_shape=[jax.ShapeDtypeStruct(s, t...  32.4 us
  transfers between devices with their start and end apart: 8, of which 3 were waited for; matrix products, arithmetic and copies ran while one was open for 5% of the time, Pallas kernels for 25%

profile of v3, /device:TPU:1, one launch (start us, length us, event | category | flops | bytes accessed | tf_op | source)
XLA Modules:
  0.0 791.3 jit_solution(5315589882135840002)
XLA Ops:
  8.1 4.5 collective-permute-start
  36.3 221.5 %shard_map.603 = (bf16[4,2,2,48,768]{4,3,2,1,0:T(8,128)(2,1)}, bf16[4,2,2,48,768]{4,3,2,1,0:T(8,128)(2,1)}, bf16[4,2,2,48,768]{4,3,2,1,0:T(8,128)(2,1)}, bf16[4,...) custom-call(bf16[96,192]{1,0:T(8,128)(2,1)} %refs_0_.3, ...), custom_call_target="tpu_custom_call" | custom-call | tf_op jit(solution)/shard_map/pallas_call | solution.py:1231
  277.0 9.2 %shard_map.604 = (bf16[448,768]{1,0:T(8,128)(2,1)}, f32[12,448]{1,0:T(8,128)}) custom-call(s32[1]{0:T(128)} %copy.424.refs_0_, bf16[448,768]{1,0:T(8,128)(2,1)} %fusion.8.refs_1_, bf16[448,768]{1,0:T(8,128)(2,1)} %convolution_convert_fusion.1.refs_2_, bf16[448,768]{1,0:T(8,128)(2,1)} %convolution_convert_fusion.refs_3_), custom_call_target="tpu_custom_call" | custom-call | flops 1233125376 | bytes 8388608 | tf_op jit(solution)/shard_map/pallas_call | solution.py:784
  294.7 8.9 %shard_map.605 = (bf16[384,768]{1,0:T(8,128)(2,1)S(1)}, f32[4,384,768]{2,1,0:T(8,128)}, bf16[4,384,768]{2,1,0:T(8,128)(2,1)S(1)}, f32[384,768]{1,0:T(8,128)S(1)}) custom-call(f32[384,768]{1,0:T(8,128)S(1)} %convolution_add_fusion.5.stream, f32[1,768]{1,0:T(1,128)S(1)} %get-tuple-element.474.gain, f32[1,768]{1,0:T(1,128)S(1)} %get-tuple-element.483.bias, ...), custom_call_target="tpu_custom_call" | custom-call | flops 3623878656 | bytes 16777216 | tf_op jit(solution)/shard_map/pallas_call | solution.py:873
  310.6 9.0 %shard_map.606 = (bf16[448,768]{1,0:T(8,128)(2,1)}, f32[12,448]{1,0:T(8,128)}) custom-call(bf16[448,768]{1,0:T(8,128)(2,1)} %fusion.9.refs_0_.q, bf16[384,768]{1,0:T(8,128)(2,1)} %convolution_convert_fusion.4.refs_1_.k, bf16[384,768]{1,0:T(8,128)(2,1)} %convolution_convert_fusion.3.refs_2_.v), custom_call_target="tpu_custom_call" | custom-call | flops 1056964608 | bytes 8388608 | tf_op jit(solution)/shard_map/pallas_call | solution.py:784
  322.9 4.3 all-to-all-start
  329.2 9.0 %all-to-all-done = bf16[4,112,896]{2,1,0:T(8,128)(2,1)} async-done(((bf16[4,112,896]{2,1,0:T(8,128)(2,1)}), bf16[4,112,896]{2,1,0:T(8,128)(2,1)}, u32[]{:S(2)}, u32[]{:S(2)}) %all-to-all-start) | async-done | bytes 802848 | tf_op jit(solution)/shard_map/all_to_all | solution.py:122
  350.0 5.6 shard_map.607
  356.5 6.9 shard_map.608
  367.2 8.8 %all_gather.9 = bf16[448,896]{1,0:T(8,128)(2,1)S(1)} all-gather(bf16[112,896]{1,0:T(8,128)(2,1)S(1)} %concatenate.54), channel_id=1, replica_groups=mesh['dp'=8,'seq'=4] {'seq'}, dimensions={0}, use_global_device_ids=true | all-gather | bytes 1003520 | tf_op jit(solution)/shard_map/all_gather | solution.py:1476
  378.8 6.1 shard_map.609
  385.8 10.8 %psum.7 = f32[2,12,448]{2,1,0:T(8,128)S(1)} all-reduce(f32[2,12,448]{2,1,0:T(8,128)S(1)} %pad_maximum_fusion.7), channel_id=1, replica_groups=mesh['dp'=8,'seq'=4] {'seq'}, use_global_device_ids=true, to_apply=%region_9.10 | all-reduce | flops 10752 | bytes 86016 | tf_op jit(solution)/shard_map/psum | solution.py:1478
  397.2 11.1 %shard_map.610 = (f32[448,768]{1,0:T(8,128)}, bf16[384,768]{1,0:T(8,128)(2,1)}, bf16[384,768]{1,0:T(8,128)(2,1)}) custom-call(bf16[448,768]{1,0:T(8,128)(2,1)} %fusion.9.refs_0_.q, bf16[384,768]{1,0:T(8,128)(2,1)} %convolution_convert_fusion.4.refs_1_.k, bf16[384,768]{1,0:T(8,128)(2,1)} %convolution_convert_fusion.3.refs_2_.v, ...), custom_call_target="tpu_custom_call" | custom-call | flops 3170893824 | bytes 8388608 | tf_op jit(solution)/shard_map/pallas_call | solution.py:784
  411.6 11.0 %shard_map.611 = (f32[384,768]{1,0:T(8,128)S(1)}, bf16[384,768]{1,0:T(8,128)(2,1)S(1)}, bf16[4,384,768]{2,1,0:T(8,128)(2,1)}, f32[1,768]{1,0:T(1,128)S(1)}, f32[1,768]{1,0:T(1,128)S(1)}) custom-call(f32[384,768]{1,0:T(8,128)S(1)} %subtract_multiply_fusion.up, f32[384,768]{1,0:T(8,128)S(1)} %convolution_add_fusion.5.stream, ...), custom_call_target="tpu_custom_call" | custom-call | flops 3623878656 | bytes 16777216 | tf_op jit(solution)/shard_map/pallas_call | solution.py:873
  426.9 40.3 %shard_map.612 = (bf16[384,768]{1,0:T(8,128)(2,1)}, bf16[384,768]{1,0:T(8,128)(2,1)}, bf16[384,768]{1,0:T(8,128)(2,1)}) custom-call(bf16[384,768]{1,0:T(8,128)(2,1)} %get-tuple-element.154.q, bf16[1536,768]{1,0:T(8,128)(2,1)} %get-tuple-element.155.k, bf16[1536,768]{1,0:T(8,128)(2,1)} %get-tuple-element.156.v, ...), custom_call_target="tpu_custom_call" | custom-call | flops 10871635968 | bytes 8388608 | tf_op jit(solution)/shard_map/pallas_call | solution.py:784
  477.7 4.3 collective-permute-start.2
  485.5 3.7 all-to-all-start.1
  499.9 6.0 all-to-all-done.1
  510.0 8.6 %all_gather.10.refs_4_ = bf16[448,768]{1,0:T(8,128)(2,1)} all-gather(bf16[112,768]{1,0:T(8,128)(2,1)S(1)} %convolution_convert_fusion.5), channel_id=1, replica_groups=mesh['dp'=8,'seq'=4] {'seq'}, dimensions={0}, use_global_device_ids=true | all-gather | bytes 860160 | tf_op jit(solution)/shard_map/all_gather | solution.py:1487
  518.6 13.5 %shard_map.613 = (bf16[448,768]{1,0:T(8,128)(2,1)}, bf16[448,768]{1,0:T(8,128)(2,1)}, bf16[448,768]{1,0:T(8,128)(2,1)}) custom-call(s32[1]{0:T(128)} %copy.424.refs_0_, bf16[448,768]{1,0:T(8,128)(2,1)} %fusion.8.refs_1_, bf16[448,768]{1,0:T(8,128)(2,1)} %convolution_convert_fusion.1.refs_2_, bf16[448,768]{1,0:T(8,128)(2,1)} %convolution_convert_fusion.refs_3_, ...), custom_call_target="tpu_custom_call" | custom-call | flops 3699376128 | bytes 8388608 | tf_op jit(solution)/shard_map/pallas_call | solution.py:784
  537.1 3.5 all-to-all-start.2
  540.9 4.2 all-to-all-done.2
  552.3 194.9 %shard_map.614 = (f32[2,2,2,48,192]{4,3,2,1,0:T(8,128)}, f32[2,48,768]{2,1,0:T(8,128)}, f32[2,48,192]{2,1,0:T(8,128)}, f32[2,48,192]{2,1,0:T(8,128)}, f32[2,48,1...) custom-call(bf16[4,112,768]{2,1,0:T(8,128)(2,1)} %copy-done.1, ...), custom_call_target="tpu_custom_call" | custom-call | tf_op jit(solution)/shard_map/pallas_call | solution.py:552
  762.8 11.5 %fusion = f32[3264,192]{0,1:T(8,128)} fusion(bf16[3584,192]{0,1:T(8,128)(2,1)S(1)} %copy-done.46, s32[3584]{0:T(1024)S(1)} %copy-done.95), kind=kOutput, calls=%fused_computation.1 | convolution fusion | flops 4503797760 | bytes 3897344 | tf_op jit(solution)/shard_map/dot_general | solution.py:25
  (487 shorter events, 157.3 us)
Async XLA Ops:
  7.2 15.8 %copy-start.72 = (bf16[1,112,768]{2,1,0:T(8,128)(2,1)S(1)}, bf16[1,112,768]{2,1,0:T(8,128)(2,1)}, u32[]{:S(2)}) copy-start(bf16[1,112,768]{2,1,0:T(8,128)(2,1)} %param.71) | copy-start | bytes 516100
  8.1 22.8 %collective-permute-start = (bf16[2,80]{0,1:T(8,128)(2,1)S(1)}, bf16[2,80]{0,1:T(8,128)(2,1)S(1)}, u32[]{:S(2)}, u32[]{:S(2)}) collective-permute-start(bf16[2,80]{0,1:T(8,128)(2,1)S(1)} %get-tuple-element.459), channel_id=1, source_target_pairs={{0,1},{1,2},{2,3},{4,5},{5,6},{6,7},{8,9},{9,10},{10,11},{12,13},{... | collective-permute-start | bytes 968 | tf_op jit(solution)/shard_map/ppermute | solution.py:111
  12.6 18.3 %collective-permute-start.1 = (bf16[2,80]{0,1:T(8,128)(2,1)S(1)}, bf16[2,80]{0,1:T(8,128)(2,1)S(1)}, u32[]{:S(2)}, u32[]{:S(2)}) collective-permute-start(bf16[2,80]{0,1:T(8,128)(2,1)S(1)} %get-tuple-element.460), channel_id=1, source_target_pairs={{1,0},{2,1},{3,2},{5,4},{6,5},{7,6},{9,8},{10,9},{11,10},{13,12},{... | collective-permute-start | bytes 968 | tf_op jit(solution)/shard_map/ppermute | solution.py:111
  262.4 64.8 %copy-start.89 = (f32[384]{0:T(512)}, f32[384]{0:T(512)S(1)}, u32[]{:S(2)}) copy-start(f32[384]{0:T(512)S(1)} %broadcast_multiply_fusion.2) | copy-start | bytes 4612
  263.0 43.3 %copy-start.86 = (f32[768]{0:T(1024)}, f32[768]{0:T(1024)S(1)}, u32[]{:S(2)}) copy-start(f32[768]{0:T(1024)S(1)} %get-tuple-element.480) | copy-start | bytes 9220
  277.0 10.8 %copy-start.12 = (bf16[8,56,768]{2,1,0:T(8,128)(2,1)S(1)}, bf16[8,56,768]{2,1,0:T(8,128)(2,1)}, u32[]{:S(2)}) copy-start(bf16[8,56,768]{2,1,0:T(8,128)(2,1)} %copy-done.11) | copy-start | bytes 2064388
  277.0 10.8 %copy-start.14 = (bf16[448,768]{1,0:T(8,128)(2,1)S(1)}, bf16[448,768]{1,0:T(8,128)(2,1)}, u32[]{:S(2)}) copy-start(bf16[448,768]{1,0:T(8,128)(2,1)} %get-tuple-element.121) | copy-start | bytes 2064388
  277.0 10.8 %copy-start.21 = (bf16[4,2,2,48,768]{4,3,2,1,0:T(8,128)(2,1)S(1)}, bf16[4,2,2,48,768]{4,3,2,1,0:T(8,128)(2,1)}, u32[]{:S(2)}) copy-start(bf16[4,2,2,48,768]{4,3,2,1,0:T(8,128)(2,1)} %get-tuple-element.128) | copy-start | bytes 3538948
  322.9 15.3 %all-to-all-start = ((bf16[4,112,896]{2,1,0:T(8,128)(2,1)}), bf16[4,112,896]{2,1,0:T(8,128)(2,1)}, u32[]{:S(2)}, u32[]{:S(2)}) async-start(bf16[4,112,896]{2,1,0:T(8,128)(2,1)} %bitcast.242), calls=%async_computation | async-start | bytes 1605632 | tf_op jit(solution)/shard_map/all_to_all | solution.py:122
  348.3 7.4 copy-start.43
  356.5 8.4 %copy-start.20 = (bf16[4,2,2,48,768]{4,3,2,1,0:T(8,128)(2,1)S(1)}, bf16[4,2,2,48,768]{4,3,2,1,0:T(8,128)(2,1)}, u32[]{:S(2)}) copy-start(bf16[4,2,2,48,768]{4,3,2,1,0:T(8,128)(2,1)} %get-tuple-element.140) | copy-start | bytes 3538948
  397.2 11.1 %copy-start.64 = (bf16[4,2,2,48,768]{4,3,2,1,0:T(8,128)(2,1)S(1)}, bf16[4,2,2,48,768]{4,3,2,1,0:T(8,128)(2,1)}, u32[]{:S(2)}) copy-start(bf16[4,2,2,48,768]{4,3,2,1,0:T(8,128)(2,1)} %get-tuple-element.136) | copy-start | bytes 3538948
  426.9 42.4 %copy-start.59 = (bf16[4,2,2,48,768]{4,3,2,1,0:T(8,128)(2,1)S(1)}, bf16[4,2,2,48,768]{4,3,2,1,0:T(8,128)(2,1)}, u32[]{:S(2)}) copy-start(bf16[4,2,2,48,768]{4,3,2,1,0:T(8,128)(2,1)} %get-tuple-element.159) | copy-start | bytes 3538948
  477.7 11.5 %collective-permute-start.2 = (bf16[1,768]{1,0:T(2,128)(2,1)S(1)}, bf16[1,768]{1,0:T(2,128)(2,1)S(1)}, u32[]{:S(2)}, u32[]{:S(2)}) collective-permute-start(bf16[1,768]{1,0:T(2,128)(2,1)S(1)} %get-tuple-element.450), channel_id=1, source_target_pairs={{0,1},{1,2},{2,3},{4,5},{5,6},{6,7},{8,9},{9,10},{10,11},{12,13},{... | collective-permute-start | bytes 4616 | tf_op jit(solution)/shard_map/ppermute | solution.py:111
  482.1 7.2 collective-permute-start.3
  485.5 20.4 %all-to-all-start.1 = ((f32[4,112,768]{2,1,0:T(8,128)}), f32[4,112,768]{2,1,0:T(8,128)S(1)}, u32[]{:S(2)}, u32[]{:S(2)}) async-start(f32[4,112,768]{2,1,0:T(8,128)} %bitcast.247), calls=%async_computation.1 | async-start | bytes 2752512 | tf_op jit(solution)/shard_map/all_to_all | solution.py:122
  508.3 10.3 %copy-start.42 = (bf16[112,768]{1,0:T(8,128)(2,1)}, bf16[112,768]{1,0:T(8,128)(2,1)S(1)}, u32[]{:S(2)}) copy-start(bf16[112,768]{1,0:T(8,128)(2,1)S(1)} %get-tuple-element.437.refs_9_) | copy-start | bytes 516100
  518.6 14.6 %copy-start.54 = (bf16[4,2,2,48,768]{4,3,2,1,0:T(8,128)(2,1)S(1)}, bf16[4,2,2,48,768]{4,3,2,1,0:T(8,128)(2,1)}, u32[]{:S(2)}) copy-start(bf16[4,2,2,48,768]{4,3,2,1,0:T(8,128)(2,1)} %get-tuple-element.124) | copy-start | bytes 3538948
  537.1 8.0 %all-to-all-start.2 = ((bf16[4,112,192]{1,2,0:T(8,128)(2,1)}), bf16[4,112,192]{1,2,0:T(8,128)(2,1)S(1)}, u32[]{:S(2)}, u32[]{:S(2)}) async-start(bf16[4,112,192]{1,2,0:T(8,128)(2,1)} %bitcast.83), calls=%async_computation.2 | async-start | bytes 393216 | tf_op jit(solution)/shard_map/all_to_all | solution.py:1551
  540.6 213.2 %all-gather.3.cloned.1.call-start = ((), (), s32[]{:S(2)}) async-start(), calls=%async_computation.3 | async-start | bytes 1769472 | tf_op jit(solution)/shard_map/all_gather | solution.py:1537
  762.8 11.6 %copy-start.71 = (f32[3,2,48,192]{3,2,1,0:T(8,128)S(1)}, f32[3,2,48,192]{3,2,1,0:T(8,128)}, u32[]{:S(2)}) copy-start(f32[3,2,48,192]{3,2,1,0:T(8,128)} %get-tuple-element.191) | copy-start | bytes 663556
  762.8 12.3 %copy-start.85 = (f32[2,48,192]{2,1,0:T(8,128)S(1)}, f32[2,48,192]{2,1,0:T(8,128)}, u32[]{:S(2)}) copy-start(f32[2,48,192]{2,1,0:T(8,128)} %get-tuple-element.192) | copy-start | bytes 221188
  762.8 13.0 %copy-start.84 = (f32[2,48,192]{2,1,0:T(8,128)S(1)}, f32[2,48,192]{2,1,0:T(8,128)}, u32[]{:S(2)}) copy-start(f32[2,48,192]{2,1,0:T(8,128)} %get-tuple-element.193) | copy-start | bytes 221188
  762.8 13.6 %copy-start.83 = (f32[2,48,192]{2,1,0:T(8,128)S(1)}, f32[2,48,192]{2,1,0:T(8,128)}, u32[]{:S(2)}) copy-start(f32[2,48,192]{2,1,0:T(8,128)} %get-tuple-element.194) | copy-start | bytes 221188
  (105 other events, 240.6 us)
Sparse Core Ops, SparseCore 0:
  546.3 54.4 all-gather.2

commit v4 on v3

--- a/solution.py
+++ b/solution.py
@@ -115,12 +115,6 @@
     before = shift(x[-width:], "seq", 1)
     after = shift(x[:width], "seq", -1)
     return jnp.concatenate([before, x, after], axis=0)
-
-
-def exchange(v):
-    n = lax.axis_size("seq")
-    got = lax.all_to_all(v, "seq", split_axis=0, concat_axis=0, tiled=True)
-    return got.reshape(n, v.shape[0] // n, v.shape[1])
 
 
 def sinusoid(first_frame, frame_count):
@@ -632,21 +626,6 @@
     lax.fori_loop(0, HEADS // 2, step, 0)
 
 
-def sums_kernel(q, k, v, up, lse, mass, inner):
-    def step(pair, _):
-        at = lanes_of(pair)
-        q_slab, k_slab, v_slab, u_slab = q[:, at], k[:, at], v[:, at], up[:, at]
-        for half in (0, 1):
-            row = pl.ds(2 * pair + half, 1)
-            p = jnp.exp(tdot(k_slab, one_head(q_slab, half), 1, 1) - lse[row, :])
-            dp = tdot(v_slab, one_head(u_slab, half), 1, 1)
-            mass[row, :] = jnp.sum(p, axis=0, keepdims=True)
-            inner[row, :] = jnp.sum(p * dp, axis=0, keepdims=True)
-        return 0
-
-    lax.fori_loop(0, HEADS // 2, step, 0)
-
-
 def back_kernel(causal, given, *refs):
     count, known = None, None
     if causal:
@@ -771,6 +750,97 @@
     for pair in range(pairs):
         for copy in across(pair) + beside(pair):
             copy.wait_send()
+
+
+def clip_peers():
+    d, s = lax.axis_index("dp"), lax.axis_index("seq")
+    return [(d, lax.rem(s + j, 4)) for j in (1, 2, 3)], s
+
+
+def greet_peers(peers):
+    barrier = pltpu.get_barrier_semaphore()
+    for dev in peers:
+        pl.semaphore_signal(barrier, inc=1, device_id=dev, device_id_type=MESH)
+    pl.semaphore_wait(barrier, 3)
+
+
+def cross_kernel(q, k, v, parts, lses, o, osend, orecv, lsend, lrecv):
+    peers, me = clip_peers()
+    greet_peers(peers)
+    r = parts.shape[1]
+    pairs = HEADS // 2
+    rows = lambda s: pl.ds(pl.multiple_of(s * r, 16), r)
+
+    def tell(j, pair):
+        at = lanes_of(pair)
+        return remote(
+            o.at[rows(peers[j][1]), at], parts.at[j + 1, :, at], osend.at[j, pair], orecv.at[j, pair], peers[j]
+        )
+
+    def step(pair, _):
+        forward_pair(pair, q, k, v, o, lses.at[0], None)
+        for j in range(3):
+            tell(j, pair).start()
+        return 0
+
+    lax.fori_loop(0, pairs, step, 0)
+    sums = [remote(lses.at[0], lses.at[j + 1], lsend.at[j], lrecv.at[j], peers[j]) for j in range(3)]
+    for copy in sums:
+        copy.start()
+    parts[0] = o[rows(me), :]
+    for copy in sums + [tell(j, pair) for j in range(3) for pair in range(pairs)]:
+        copy.wait_recv()
+    for copy in sums + [tell(j, pair) for j in range(3) for pair in range(pairs)]:
+        copy.wait_send()
+
+
+def cross_back_kernel(q, k, v, up, lse, dq, dk, dv, sums, known, mine, theirs, ssend, srecv, dsend, drecv):
+    peers, me = clip_peers()
+    greet_peers(peers)
+    r = dq.shape[0]
+    pairs = HEADS // 2
+    rows = lambda s: pl.ds(pl.multiple_of(s * r, 16), r)
+
+    def first(pair, _):
+        at = lanes_of(pair)
+        q_slab, k_slab, v_slab, u_slab = q[:, at], k[:, at], v[:, at], up[:, at]
+        for half in (0, 1):
+            row = 2 * pair + half
+            p = jnp.exp(tdot(k_slab, one_head(q_slab, half), 1, 1) - lse[pl.ds(row, 1), :])
+            dp = tdot(v_slab, one_head(u_slab, half), 1, 1)
+            sums[0, pl.ds(row, 1), :] = jnp.sum(p, axis=0, keepdims=True)
+            sums[0, pl.ds(16 + row, 1), :] = jnp.sum(p * dp, axis=0, keepdims=True)
+        return 0
+
+    sums[0] = jnp.zeros(sums.shape[1:], F32)
+    lax.fori_loop(0, pairs, first, 0)
+    shared = [remote(sums.at[0], sums.at[j + 1], ssend.at[j], srecv.at[j], peers[j]) for j in range(3)]
+    for copy in shared:
+        copy.start()
+    for copy in shared:
+        copy.wait_recv()
+    total = sums[0] + sums[1] + sums[2] + sums[3]
+    known[...] = total[16 : 16 + HEADS] / total[0:HEADS]
+
+    def tell(j, pair):
+        at = lanes_of(pair)
+        return remote(
+            mine.at[rows(peers[j][1]), at], theirs.at[j, :, at], dsend.at[j, pair], drecv.at[j, pair], peers[j]
+        )
+
+    def second(pair, _):
+        backward_pair(pair, q, k, v, up, lse, mine, dk, dv, None, known)
+        for j in range(3):
+            tell(j, pair).start()
+        return 0
+
+    lax.fori_loop(0, pairs, second, 0)
+    for j in range(3):
+        for pair in range(pairs):
+            tell(j, pair).wait_recv()
+    dq[...] = mine[rows(me), :] + theirs[0] + theirs[1] + theirs[2]
+    for copy in shared + [tell(j, pair) for j in range(3) for pair in range(pairs)]:
+        copy.wait_send()
 
 
 def local_call(kernel, out_shape, args, cost, count=None, scratch=(), barrier=None):
@@ -802,8 +872,22 @@
     return local_call(kernel, shapes, [q, k, v], rows_cost(q, k), count)
 
 
-def attend_sums(q, k, v, up, lse):
-    return local_call(sums_kernel, [(lse.shape, F32)] * 2, [q, k, v, up, lse], rows_cost(q, k))
+def cross_attend(q, k, v):
+    r = q.shape[0] // 4
+    sem = pltpu.SemaphoreType.DMA
+    scratch = [pltpu.VMEM(q.shape, BF)] + [sem((3, HEADS // 2))] * 2 + [sem((3,))] * 2
+    shapes = [((4, r, D), BF), ((4, HEADS, q.shape[0]), F32)]
+    return local_call(cross_kernel, shapes, [q, k, v], rows_cost(q, k), None, scratch, 6)
+
+
+def cross_back(q, k, v, up, lse):
+    slots = q.shape[0]
+    sem = pltpu.SemaphoreType.DMA
+    scratch = [pltpu.VMEM((4, 32, slots), F32), pltpu.VMEM((HEADS, slots), F32)]
+    scratch += [pltpu.VMEM((slots, D), F32), pltpu.VMEM((3, slots // 4, D), F32)]
+    scratch += [sem((3,))] * 2 + [sem((3, HEADS // 2))] * 2
+    shapes = [((slots // 4, D), F32), (k.shape, BF), (k.shape, BF)]
+    return local_call(cross_back_kernel, shapes, [q, k, v, up, lse], 4 * rows_cost(q, k), None, scratch, 7)
 
 
 def attend_back(q, k, v, up, lse, count=None, inner=None, out=BF):
@@ -1441,8 +1525,8 @@
     cross_normed = norm(stream4, vec[22], vec[23])
     xq = (mm(cross_normed, cq_w) * SCALE).astype(BF)
 
-    part, part_lse = attend(xq, mk, mv)
-    parts, lses = unpack(exchange(pack(part, part_lse)))
+    parts, lses = cross_attend(xq, mk, mv)
+    lses = lax.dynamic_slice_in_dim(lses, me * slots, slots, 2).transpose(0, 2, 1)
     top = jnp.max(lses, axis=0)
     share = jnp.exp(lses - top)
     total = jnp.sum(share, axis=0)
@@ -1475,9 +1559,7 @@
     d_mixed = mm_t(d_low, co_w, BF)
     d_mixed, lse_all = unpack(lax.all_gather(pack(d_mixed, cross_lse.T), "seq", axis=0, tiled=True))
     lse_all = lse_all.T
-    sums = lax.psum(jnp.stack(attend_sums(xq, mk, mv, d_mixed, lse_all)), "seq")
-    dxq, dmk, dmv = attend_back(xq, mk, mv, d_mixed, lse_all, inner=sums[1] / sums[0], out=F32)
-    dxq = jnp.sum(exchange(dxq), axis=0)
+    dxq, dmk, dmv = cross_back(xq, mk, mv, d_mixed, lse_all)
     dxq = (low(dxq) * SCALE).astype(BF)
     grads[24] = (own(cross_normed), dxq)
     back, grads[22], grads[23] = norm_back(stream4, vec[22], mm_t(dxq, cq_w))

time: 797 us -> 766 us (0.961)
  Pallas kernels: 538 us -> 558 us
  waiting for transfers between devices: 19.3 us -> 0.05 us
  blocking collectives: 28.2 us -> 17.4 us
    pallas_call x6 -> x5, Pallas kernels: 89.2 us -> 109 us  [local_call(): pl.pallas_call(kernel, out_shape=[jax.ShapeDtypeStruct(s, t) for s, t in...]
    all_to_all x2 -> x0, waiting for transfers between devices: 15.1 us -> none  [exchange(): got = lax.all_to_all(v, 'seq', split_axis=0, concat_axis=0, tiled=True)]
    psum x1 -> x0, blocking collectives: 10.8 us -> none  [body(): sums = lax.psum(jnp.stack(attend_sums(xq, mk, mv, d_mixed, lse_all)), 'seq')]
    unnamed x283 -> x236, local copies, waits for them, and re-layouts: 42 us -> 35.4 us
  transfers between devices with their start and end apart: 8 -> 6, of which waited for: 3 -> 0; matrix products, arithmetic and copies ran while one was open for 5% -> 6% of each run, Pallas kernels for 25% -> 31%
where the time goes in v4:
time: 766 us; the launch traced here: 761 us
  Pallas kernels  558 us (73%)
  local copies, waits for them, and re-layouts  76.1 us (10%)
  matrix products  44.4 us (6%)
  other arithmetic  32.3 us (4%)
  blocking collectives  17.4 us (2%)
  between operations  16.6 us (2%)
  starting transfers between devices  16.4 us (2%)
    pallas_call x1, Pallas kernels, gather_and_stem(): pl.pallas_call(functools.partial(stem_kernel, plan, len(ins), len(out_sha...  222 us
    pallas_call x1, Pallas kernels, reduce_fast(): pl.pallas_call(functools.partial(reduce_kernel, items, jobs, len(ins), le...  195 us
    pallas_call x5, Pallas kernels, local_call(): pl.pallas_call(kernel, out_shape=[jax.ShapeDtypeStruct(s, t) for s, t in...  109 us
    dot_general x29, matrix products, dot(): lax.dot_general(a, b, (((ca,), (cb,)), ((), ())), preferred_element_type=...  44.4 us
    unnamed x236, local copies, waits for them, and re-layouts  35.4 us
    pallas_call x4, Pallas kernels, blocks(): pl.pallas_call(kernel, grid=(grid,), out_shape=[jax.ShapeDtypeStruct(s, t...  32 us
  transfers between devices with their start and end apart: 6, of which 0 were waited for; matrix products, arithmetic and copies ran while one was open for 6% of the time, Pallas kernels for 31%

profile of v4, /device:TPU:1, one launch (start us, length us, event | category | flops | bytes accessed | tf_op | source)
XLA Modules:
  0.0 761.0 jit_solution(899436033726982795)
XLA Ops:
  8.1 4.5 collective-permute-start
  35.5 221.5 %shard_map.603 = (bf16[4,2,2,48,768]{4,3,2,1,0:T(8,128)(2,1)}, bf16[4,2,2,48,768]{4,3,2,1,0:T(8,128)(2,1)}, bf16[4,2,2,48,768]{4,3,2,1,0:T(8,128)(2,1)}, bf16[4,...) custom-call(bf16[96,192]{1,0:T(8,128)(2,1)} %refs_0_.3, ...), custom_call_target="tpu_custom_call" | custom-call | tf_op jit(solution)/shard_map/pallas_call | solution.py:1315
  266.1 9.1 %shard_map.604 = (bf16[448,768]{1,0:T(8,128)(2,1)}, f32[12,448]{1,0:T(8,128)}) custom-call(s32[1]{0:T(128)} %copy.392.refs_0_, bf16[448,768]{1,0:T(8,128)(2,1)} %fusion.7.refs_1_, bf16[448,768]{1,0:T(8,128)(2,1)} %convolution_convert_fusion.1.refs_2_, bf16[448,768]{1,0:T(8,128)(2,1)} %convolution_convert_fusion.refs_3_), custom_call_target="tpu_custom_call" | custom-call | flops 1233125376 | bytes 8388608 | tf_op jit(solution)/shard_map/pallas_call | solution.py:854
  285.1 8.5 %shard_map.605 = (bf16[384,768]{1,0:T(8,128)(2,1)S(1)}, f32[4,384,768]{2,1,0:T(8,128)}, bf16[4,384,768]{2,1,0:T(8,128)(2,1)S(1)}, f32[384,768]{1,0:T(8,128)S(1)}) custom-call(f32[384,768]{1,0:T(8,128)S(1)} %convolution_add_fusion.5.stream, f32[1,768]{1,0:T(1,128)S(1)} %get-tuple-element.470.gain, f32[1,768]{1,0:T(1,128)S(1)} %get-tuple-element.479.bias, ...), custom_call_target="tpu_custom_call" | custom-call | flops 3623878656 | bytes 16777216 | tf_op jit(solution)/shard_map/pallas_call | solution.py:957
  300.7 15.2 %shard_map.606 = (bf16[4,112,768]{2,1,0:T(8,128)(2,1)}, f32[4,12,448]{2,1,0:T(8,128)}) custom-call(bf16[448,768]{1,0:T(8,128)(2,1)} %fusion.8.q, bf16[384,768]{1,0:T(8,128)(2,1)} %convolution_convert_fusion.4.k, bf16[384,768]{1,0:T(8,128)(2,1)} %convolution_convert_fusion.3.v), custom_call_target="tpu_custom_call" | custom-call | flops 1056964608 | bytes 8388608 | tf_op jit(solution)/shard_map/pallas_call | solution.py:854
  320.3 3.0 copy.317
  326.3 5.6 shard_map.607
  332.8 6.9 shard_map.608
  343.5 8.8 %all_gather.9 = bf16[448,896]{1,0:T(8,128)(2,1)S(1)} all-gather(bf16[112,896]{1,0:T(8,128)(2,1)S(1)} %concatenate.50), channel_id=1, replica_groups=mesh['dp'=8,'seq'=4] {'seq'}, dimensions={0}, use_global_device_ids=true | all-gather | bytes 1003520 | tf_op jit(solution)/shard_map/all_gather | solution.py:1560
  354.3 2.6 fusion.30
  361.7 30.2 %shard_map.609 = (f32[112,768]{1,0:T(8,128)}, bf16[384,768]{1,0:T(8,128)(2,1)}, bf16[384,768]{1,0:T(8,128)(2,1)}) custom-call(bf16[448,768]{1,0:T(8,128)(2,1)} %fusion.8.q, bf16[384,768]{1,0:T(8,128)(2,1)} %convolution_convert_fusion.4.k, bf16[384,768]{1,0:T(8,128)(2,1)} %convolution_convert_fusion.3.v, bf16[448,768]{1,0:T(8,128)(2,1)} %slice.263.up, ...), custom_call_target="tpu_custom_call" | custom-call | flops 4227858432 | bytes 8388608 | tf_op jit(solution)/shard_map/pallas_call | solution.py:854
  398.9 11.1 %shard_map.610 = (f32[384,768]{1,0:T(8,128)S(1)}, bf16[384,768]{1,0:T(8,128)(2,1)S(1)}, bf16[4,384,768]{2,1,0:T(8,128)(2,1)}, f32[1,768]{1,0:T(1,128)S(1)}, f32[1,768]{1,0:T(1,128)S(1)}) custom-call(f32[384,768]{1,0:T(8,128)S(1)} %subtract_multiply_fusion.up, f32[384,768]{1,0:T(8,128)S(1)} %convolution_add_fusion.5.stream, ...), custom_call_target="tpu_custom_call" | custom-call | flops 3623878656 | bytes 16777216 | tf_op jit(solution)/shard_map/pallas_call | solution.py:957
  411.4 8.6 %all_gather.10.refs_4_ = bf16[448,768]{1,0:T(8,128)(2,1)} all-gather(bf16[112,768]{1,0:T(8,128)(2,1)S(1)} %convolution_convert_fusion.5), channel_id=1, replica_groups=mesh['dp'=8,'seq'=4] {'seq'}, dimensions={0}, use_global_device_ids=true | all-gather | bytes 860160 | tf_op jit(solution)/shard_map/all_gather | solution.py:1569
  420.0 13.5 %shard_map.612 = (bf16[448,768]{1,0:T(8,128)(2,1)}, bf16[448,768]{1,0:T(8,128)(2,1)}, bf16[448,768]{1,0:T(8,128)(2,1)}) custom-call(s32[1]{0:T(128)} %copy.392.refs_0_, bf16[448,768]{1,0:T(8,128)(2,1)} %fusion.7.refs_1_, bf16[448,768]{1,0:T(8,128)(2,1)} %convolution_convert_fusion.1.refs_2_, bf16[448,768]{1,0:T(8,128)(2,1)} %convolution_convert_fusion.refs_3_, ...), custom_call_target="tpu_custom_call" | custom-call | flops 3699376128 | bytes 8388608 | tf_op jit(solution)/shard_map/pallas_call | solution.py:854
  442.3 4.1 all-to-all-start
  448.1 41.2 %shard_map.611 = (bf16[384,768]{1,0:T(8,128)(2,1)}, bf16[384,768]{1,0:T(8,128)(2,1)}, bf16[384,768]{1,0:T(8,128)(2,1)}) custom-call(bf16[384,768]{1,0:T(8,128)(2,1)} %get-tuple-element.150.q, bf16[1536,768]{1,0:T(8,128)(2,1)} %get-tuple-element.151.k, bf16[1536,768]{1,0:T(8,128)(2,1)} %get-tuple-element.152.v, ...), custom_call_target="tpu_custom_call" | custom-call | flops 10871635968 | bytes 8388608 | tf_op jit(solution)/shard_map/pallas_call | solution.py:854
  496.7 2.2 fusion.28.refs_28_
  499.0 3.9 collective-permute-start.2
  511.1 2.7 fusion.10
  521.9 195.0 %shard_map.613 = (f32[2,2,2,48,192]{4,3,2,1,0:T(8,128)}, f32[2,48,768]{2,1,0:T(8,128)}, f32[2,48,192]{2,1,0:T(8,128)}, f32[2,48,192]{2,1,0:T(8,128)}, f32[2,48,1...) custom-call(bf16[4,112,768]{2,1,0:T(8,128)(2,1)} %copy-done.1, ...), custom_call_target="tpu_custom_call" | custom-call | tf_op jit(solution)/shard_map/pallas_call | solution.py:546
  723.5 2.3 copy.343
  725.8 2.6 reshape.742
  728.5 2.4 copy.344
  732.5 11.6 %fusion = f32[3264,192]{0,1:T(8,128)} fusion(bf16[3584,192]{0,1:T(8,128)(2,1)S(1)} %copy-done.37, s32[3584]{0:T(1024)S(1)} %copy-done.83), kind=kOutput, calls=%fused_computation.1 | convolution fusion | flops 4503797760 | bytes 3897344 | tf_op jit(solution)/shard_map/dot_general | solution.py:25
  (422 shorter events, 127.4 us)
Async XLA Ops:
  7.2 15.2 %copy-start.64 = (bf16[1,112,768]{2,1,0:T(8,128)(2,1)S(1)}, bf16[1,112,768]{2,1,0:T(8,128)(2,1)}, u32[]{:S(2)}) copy-start(bf16[1,112,768]{2,1,0:T(8,128)(2,1)} %param.71) | copy-start | bytes 516100
  8.1 22.0 %collective-permute-start = (bf16[2,80]{0,1:T(8,128)(2,1)S(1)}, bf16[2,80]{0,1:T(8,128)(2,1)S(1)}, u32[]{:S(2)}, u32[]{:S(2)}) collective-permute-start(bf16[2,80]{0,1:T(8,128)(2,1)S(1)} %get-tuple-element.455), channel_id=1, source_target_pairs={{0,1},{1,2},{2,3},{4,5},{5,6},{6,7},{8,9},{9,10},{10,11},{12,13},{... | collective-permute-start | bytes 968 | tf_op jit(solution)/shard_map/ppermute | solution.py:111
  12.6 17.5 %collective-permute-start.1 = (bf16[2,80]{0,1:T(8,128)(2,1)S(1)}, bf16[2,80]{0,1:T(8,128)(2,1)S(1)}, u32[]{:S(2)}, u32[]{:S(2)}) collective-permute-start(bf16[2,80]{0,1:T(8,128)(2,1)S(1)} %get-tuple-element.456), channel_id=1, source_target_pairs={{1,0},{2,1},{3,2},{5,4},{6,5},{7,6},{9,8},{10,9},{11,10},{13,12},{... | collective-permute-start | bytes 968 | tf_op jit(solution)/shard_map/ppermute | solution.py:111
  266.1 10.7 %copy-start.18 = (bf16[4,2,2,48,768]{4,3,2,1,0:T(8,128)(2,1)S(1)}, bf16[4,2,2,48,768]{4,3,2,1,0:T(8,128)(2,1)}, u32[]{:S(2)}) copy-start(bf16[4,2,2,48,768]{4,3,2,1,0:T(8,128)(2,1)} %get-tuple-element.126) | copy-start | bytes 3538948
  332.8 6.9 copy-start.5
  361.6 31.2 %copy-start.56 = (bf16[4,2,2,48,768]{4,3,2,1,0:T(8,128)(2,1)S(1)}, bf16[4,2,2,48,768]{4,3,2,1,0:T(8,128)(2,1)}, u32[]{:S(2)}) copy-start(bf16[4,2,2,48,768]{4,3,2,1,0:T(8,128)(2,1)} %get-tuple-element.134) | copy-start | bytes 3538948
  420.0 14.5 %copy-start.45 = (bf16[4,2,2,48,768]{4,3,2,1,0:T(8,128)(2,1)S(1)}, bf16[4,2,2,48,768]{4,3,2,1,0:T(8,128)(2,1)}, u32[]{:S(2)}) copy-start(bf16[4,2,2,48,768]{4,3,2,1,0:T(8,128)(2,1)} %get-tuple-element.122) | copy-start | bytes 3538948
  442.3 66.8 %all-to-all-start = ((bf16[4,112,192]{1,2,0:T(8,128)(2,1)}), bf16[4,112,192]{1,2,0:T(8,128)(2,1)}, u32[]{:S(2)}, u32[]{:S(2)}) async-start(bf16[4,112,192]{1,2,0:T(8,128)(2,1)} %bitcast.78), calls=%async_computation | async-start | bytes 393216 | tf_op jit(solution)/shard_map/all_to_all | solution.py:1633
  446.5 277.1 %all-gather.3.cloned.1.call-start = ((), (), s32[]{:S(2)}) async-start(), calls=%async_computation.1 | async-start | bytes 1769472 | tf_op jit(solution)/shard_map/all_gather | solution.py:1619
  448.1 43.3 %copy-start.51 = (bf16[4,2,2,48,768]{4,3,2,1,0:T(8,128)(2,1)S(1)}, bf16[4,2,2,48,768]{4,3,2,1,0:T(8,128)(2,1)}, u32[]{:S(2)}) copy-start(bf16[4,2,2,48,768]{4,3,2,1,0:T(8,128)(2,1)} %get-tuple-element.155) | copy-start | bytes 3538948
  496.6 8.5 %copy-start.80 = (bf16[1,4,2,2,2,24]{5,4,3,2,1,0:T(2,128)(2,1)S(1)}, bf16[1,4,2,2,2,24]{5,4,3,2,1,0:T(2,128)(2,1)}, u32[]{:S(2)}) copy-start(bf16[1,4,2,2,2,24]{5,4,3,2,1,0:T(2,128)(2,1)} %stack.111) | copy-start | bytes 4612
  496.6 8.5 %copy-start.79 = (bf16[1,4,2,2,2,24]{5,4,3,2,1,0:T(2,128)(2,1)S(1)}, bf16[1,4,2,2,2,24]{5,4,3,2,1,0:T(2,128)(2,1)}, u32[]{:S(2)}) copy-start(bf16[1,4,2,2,2,24]{5,4,3,2,1,0:T(2,128)(2,1)} %stack.112) | copy-start | bytes 4612
  496.7 8.5 %copy-start.77 = (s32[2,2,4,2,56]{4,3,2,1,0:T(2,128)S(1)}, s32[2,2,4,2,56]{4,3,2,1,0:T(2,128)}, u32[]{:S(2)}) copy-start(s32[2,2,4,2,56]{4,3,2,1,0:T(2,128)} %get-tuple-element.420) | copy-start | bytes 21508
  496.7 8.5 %copy-start.78 = (s32[2,2,4,2,56]{4,3,2,1,0:T(2,128)S(1)}, s32[2,2,4,2,56]{4,3,2,1,0:T(2,128)}, u32[]{:S(2)}) copy-start(s32[2,2,4,2,56]{4,3,2,1,0:T(2,128)} %get-tuple-element.421) | copy-start | bytes 21508
  498.9 9.4 %copy-start.16 = (bf16[384,768]{1,0:T(8,128)(2,1)}, bf16[384,768]{1,0:T(8,128)(2,1)S(1)}, u32[]{:S(2)}) copy-start(bf16[384,768]{1,0:T(8,128)(2,1)S(1)} %fusion.28.refs_28_) | copy-start | bytes 1769476
  499.0 9.3 %collective-permute-start.2 = (bf16[1,768]{1,0:T(2,128)(2,1)S(1)}, bf16[1,768]{1,0:T(2,128)(2,1)S(1)}, u32[]{:S(2)}, u32[]{:S(2)}) collective-permute-start(bf16[1,768]{1,0:T(2,128)(2,1)S(1)} %get-tuple-element.446), channel_id=1, source_target_pairs={{0,1},{1,2},{2,3},{4,5},{5,6},{6,7},{8,9},{9,10},{10,11},{12,13},{... | collective-permute-start | bytes 4616 | tf_op jit(solution)/shard_map/ppermute | solution.py:111
  502.9 5.4 collective-permute-start.3
  732.4 11.6 %copy-start.63 = (f32[3,2,48,192]{3,2,1,0:T(8,128)S(1)}, f32[3,2,48,192]{3,2,1,0:T(8,128)}, u32[]{:S(2)}) copy-start(f32[3,2,48,192]{3,2,1,0:T(8,128)} %get-tuple-element.187) | copy-start | bytes 663556
  732.5 12.3 %copy-start.76 = (f32[2,48,192]{2,1,0:T(8,128)S(1)}, f32[2,48,192]{2,1,0:T(8,128)}, u32[]{:S(2)}) copy-start(f32[2,48,192]{2,1,0:T(8,128)} %get-tuple-element.188) | copy-start | bytes 221188
  732.5 13.0 %copy-start.75 = (f32[2,48,192]{2,1,0:T(8,128)S(1)}, f32[2,48,192]{2,1,0:T(8,128)}, u32[]{:S(2)}) copy-start(f32[2,48,192]{2,1,0:T(8,128)} %get-tuple-element.189) | copy-start | bytes 221188
  732.5 13.6 %copy-start.74 = (f32[2,48,192]{2,1,0:T(8,128)S(1)}, f32[2,48,192]{2,1,0:T(8,128)}, u32[]{:S(2)}) copy-start(f32[2,48,192]{2,1,0:T(8,128)} %get-tuple-element.190) | copy-start | bytes 221188
  744.8 6.5 copy-start.67
  745.4 6.5 copy-start.66
  746.1 6.5 copy-start.65
  (80 other events, 160.6 us)
Sparse Core Ops, SparseCore 0:
  511.2 55.4 all-gather.2

commit v5 on v4

--- a/solution.py
+++ b/solution.py
@@ -626,23 +626,6 @@
     lax.fori_loop(0, HEADS // 2, step, 0)
 
 
-def back_kernel(causal, given, *refs):
-    count, known = None, None
-    if causal:
-        count, refs = refs[0], refs[1:]
-    q, k, v, up, lse = refs[:5]
-    refs = refs[5:]
-    if given:
-        known, refs = refs[0], refs[1:]
-    dq, dk, dv = refs
-
-    def step(pair, _):
-        backward_pair(pair, q, k, v, up, lse, dq, dk, dv, count, known)
-        return 0
-
-    lax.fori_loop(0, HEADS // 2, step, 0)
-
-
 def clip_attend_kernel(q, k, v, o, lse, k_all, v_all, xsend, xrecv, csend, crecv):
     xp, cp = clip_partners()
     r = q.shape[0]
@@ -840,6 +823,32 @@
             tell(j, pair).wait_recv()
     dq[...] = mine[rows(me), :] + theirs[0] + theirs[1] + theirs[2]
     for copy in shared + [tell(j, pair) for j in range(3) for pair in range(pairs)]:
+        copy.wait_send()
+
+
+def clip_rows_back_kernel(count, q, k, v, own, lse, dq, dk, dv, up, send, recv):
+    peers, me = clip_peers()
+    greet_peers(peers)
+    r = own.shape[0]
+    here = pl.ds(pl.multiple_of(me * r, 16), r)
+
+    def tell(j, pair):
+        at = lanes_of(pair)
+        return remote(own.at[:, at], up.at[here, at], send.at[j, pair], recv.at[j, pair], peers[j])
+
+    every = [tell(j, pair) for pair in range(HEADS // 2) for j in range(3)]
+    for copy in every:
+        copy.start()
+    up[here, :] = own[...]
+
+    def step(pair, _):
+        for j in range(3):
+            tell(j, pair).wait_recv()
+        backward_pair(pair, q, k, v, up, lse, dq, dk, dv, count, None)
+        return 0
+
+    lax.fori_loop(0, HEADS // 2, step, 0)
+    for copy in every:
         copy.wait_send()
 
 
@@ -890,11 +899,10 @@
     return local_call(cross_back_kernel, shapes, [q, k, v, up, lse], 4 * rows_cost(q, k), None, scratch, 7)
 
 
-def attend_back(q, k, v, up, lse, count=None, inner=None, out=BF):
-    shapes = [(q.shape, out), (k.shape, BF), (k.shape, BF)]
-    kernel = functools.partial(back_kernel, count is not None, inner is not None)
-    args = [q, k, v, up, lse] + ([] if inner is None else [inner])
-    return local_call(kernel, shapes, args, 3 * rows_cost(q, k), count)
+def clip_rows_back(q, k, v, own, lse, count):
+    scratch = [pltpu.VMEM(q.shape, BF)] + [pltpu.SemaphoreType.DMA((3, HEADS // 2))] * 2
+    args = [q, k, v, own, lse]
+    return local_call(clip_rows_back_kernel, [(q.shape, BF)] * 3, args, 3 * rows_cost(q, k), count, scratch, 8)
 
 
 def clip_attend(q, k, v):
@@ -1566,8 +1574,8 @@
     up = up + back
     d_low = up.astype(BF)
     grads[21] = (own(dec_mixed), d_low)
-    d_mixed = lax.all_gather(mm_t(d_low, do_w, BF), "seq", axis=0, tiled=True)
-    dsq, dsk, dsv = attend_back(sq, sk, sv, d_mixed, dec_lse, token_counts)
+    d_mixed = mm_t(d_low, do_w, BF)
+    dsq, dsk, dsv = clip_rows_back(sq, sk, sv, d_mixed, dec_lse, token_counts)
 
     def inputs_back(first, gain, normed, stream, dq, dk, dv, up):
         dq = (dq.astype(F32) * SCALE).astype(BF)

time: 766 us -> 764 us (level)
  blocking collectives: 17.4 us -> 8.81 us
    all_gather x1 -> x0, blocking collectives: 8.63 us -> none  [body(): d_mixed = lax.all_gather(mm_t(d_low, do_w, BF), 'seq', axis=0, tiled=True)]
    unnamed x236 -> x232, local copies, waits for them, and re-layouts: 35.4 us -> 35.4 us
where the time goes in v5:
time: 764 us; the launch traced here: 759 us
  Pallas kernels  562 us (74%)
  local copies, waits for them, and re-layouts  75.9 us (10%)
  matrix products  46.7 us (6%)
  other arithmetic  32.5 us (4%)
  between operations  16.6 us (2%)
  starting transfers between devices  16.3 us (2%)
  blocking collectives  8.81 us (1%)
    pallas_call x1, Pallas kernels, gather_and_stem(): pl.pallas_call(functools.partial(stem_kernel, plan, len(ins), len(out_sha...  222 us
    pallas_call x1, Pallas kernels, reduce_fast(): pl.pallas_call(functools.partial(reduce_kernel, items, jobs, len(ins), le...  195 us
    pallas_call x5, Pallas kernels, local_call(): pl.pallas_call(kernel, out_shape=[jax.ShapeDtypeStruct(s, t) for s, t in...  114 us
    dot_general x29, matrix products, dot(): lax.dot_general(a, b, (((ca,), (cb,)), ((), ())), preferred_element_type=...  46.7 us
    unnamed x232, local copies, waits for them, and re-layouts  35.4 us
    pallas_call x4, Pallas kernels, blocks(): pl.pallas_call(kernel, grid=(grid,), out_shape=[jax.ShapeDtypeStruct(s, t...  32 us
  transfers between devices with their start and end apart: 6, of which 0 were waited for; matrix products, arithmetic and copies ran while one was open for 6% of the time, Pallas kernels for 31%

profile of v5, /device:TPU:1, one launch (start us, length us, event | category | flops | bytes accessed | tf_op | source)
XLA Modules:
  0.0 758.8 jit_solution(11038236491678398934)
XLA Ops:
  8.1 4.5 collective-permute-start
  22.6 2.1 multiply_sine_fusion
  35.5 221.6 %shard_map.603 = (bf16[4,2,2,48,768]{4,3,2,1,0:T(8,128)(2,1)}, bf16[4,2,2,48,768]{4,3,2,1,0:T(8,128)(2,1)}, bf16[4,2,2,48,768]{4,3,2,1,0:T(8,128)(2,1)}, bf16[4,...) custom-call(bf16[96,192]{1,0:T(8,128)(2,1)} %refs_0_.2, ...), custom_call_target="tpu_custom_call" | custom-call | tf_op jit(solution)/shard_map/pallas_call | solution.py:1323
  266.2 9.1 %shard_map.604 = (bf16[448,768]{1,0:T(8,128)(2,1)}, f32[12,448]{1,0:T(8,128)}) custom-call(s32[1]{0:T(128)} %copy.392.refs_0_.count, bf16[448,768]{1,0:T(8,128)(2,1)} %fusion.7.refs_1_.q, bf16[448,768]{1,0:T(8,128)(2,1)} %convolution_convert_fusion.1.refs_2_.k, bf16[448,768]{1,0:T(8,128)(2,1)} %convolution_convert_fusion.refs_3_.v), custom_call_target="tpu_custom_call" | custom-call | flops 1233125376 | bytes 8388608 | tf_op jit(solution)/shard_map/pallas_call | solution.py:863
  285.2 8.4 %shard_map.605 = (bf16[384,768]{1,0:T(8,128)(2,1)S(1)}, f32[4,384,768]{2,1,0:T(8,128)}, bf16[4,384,768]{2,1,0:T(8,128)(2,1)S(1)}, f32[384,768]{1,0:T(8,128)S(1)}) custom-call(f32[384,768]{1,0:T(8,128)S(1)} %convolution_add_fusion.5.stream, f32[1,768]{1,0:T(1,128)S(1)} %get-tuple-element.470.gain, f32[1,768]{1,0:T(1,128)S(1)} %get-tuple-element.479.bias, ...), custom_call_target="tpu_custom_call" | custom-call | flops 3623878656 | bytes 16777216 | tf_op jit(solution)/shard_map/pallas_call | solution.py:965
  300.7 15.1 %shard_map.606 = (bf16[4,112,768]{2,1,0:T(8,128)(2,1)}, f32[4,12,448]{2,1,0:T(8,128)}) custom-call(bf16[448,768]{1,0:T(8,128)(2,1)} %fusion.8.q, bf16[384,768]{1,0:T(8,128)(2,1)} %convolution_convert_fusion.4.k, bf16[384,768]{1,0:T(8,128)(2,1)} %convolution_convert_fusion.3.v), custom_call_target="tpu_custom_call" | custom-call | flops 1056964608 | bytes 8388608 | tf_op jit(solution)/shard_map/pallas_call | solution.py:863
  320.3 3.0 copy.317
  326.4 5.6 shard_map.607
  332.9 6.8 shard_map.608
  343.5 8.8 %all_gather.6 = bf16[448,896]{1,0:T(8,128)(2,1)S(1)} all-gather(bf16[112,896]{1,0:T(8,128)(2,1)S(1)} %concatenate.50), channel_id=1, replica_groups=mesh['dp'=8,'seq'=4] {'seq'}, dimensions={0}, use_global_device_ids=true | all-gather | bytes 1003520 | tf_op jit(solution)/shard_map/all_gather | solution.py:1568
  354.4 2.6 fusion.30
  361.7 30.2 %shard_map.609 = (f32[112,768]{1,0:T(8,128)}, bf16[384,768]{1,0:T(8,128)(2,1)}, bf16[384,768]{1,0:T(8,128)(2,1)}) custom-call(bf16[448,768]{1,0:T(8,128)(2,1)} %fusion.8.q, bf16[384,768]{1,0:T(8,128)(2,1)} %convolution_convert_fusion.4.k, bf16[384,768]{1,0:T(8,128)(2,1)} %convolution_convert_fusion.3.v, bf16[448,768]{1,0:T(8,128)(2,1)} %slice.263.up, ...), custom_call_target="tpu_custom_call" | custom-call | flops 4227858432 | bytes 8388608 | tf_op jit(solution)/shard_map/pallas_call | solution.py:863
  398.1 18.1 %shard_map.612 = (bf16[448,768]{1,0:T(8,128)(2,1)}, bf16[448,768]{1,0:T(8,128)(2,1)}, bf16[448,768]{1,0:T(8,128)(2,1)}) custom-call(s32[1]{0:T(128)} %copy.392.refs_0_.count, bf16[448,768]{1,0:T(8,128)(2,1)} %fusion.7.refs_1_.q, bf16[448,768]{1,0:T(8,128)(2,1)} %convolution_convert_fusion.1.refs_2_.k, bf16[448,768]{1,0:T(8,128)(2,1)} %convolution_convert_fusion.refs_3_.v, ...), custom_call_target="tpu_custom_call" | custom-call | flops 3699376128 | bytes 8388608 | tf_op jit(solution)/shard_map/pallas_call | solution.py:863
  419.2 11.1 %shard_map.610 = (f32[384,768]{1,0:T(8,128)S(1)}, bf16[384,768]{1,0:T(8,128)(2,1)S(1)}, bf16[4,384,768]{2,1,0:T(8,128)(2,1)}, f32[1,768]{1,0:T(1,128)S(1)}, f32[1,768]{1,0:T(1,128)S(1)}) custom-call(f32[384,768]{1,0:T(8,128)S(1)} %subtract_multiply_fusion.up, f32[384,768]{1,0:T(8,128)S(1)} %convolution_add_fusion.5.stream, ...), custom_call_target="tpu_custom_call" | custom-call | flops 3623878656 | bytes 16777216 | tf_op jit(solution)/shard_map/pallas_call | solution.py:965
  440.5 4.0 all-to-all-start
  446.2 41.1 %shard_map.611 = (bf16[384,768]{1,0:T(8,128)(2,1)}, bf16[384,768]{1,0:T(8,128)(2,1)}, bf16[384,768]{1,0:T(8,128)(2,1)}) custom-call(bf16[384,768]{1,0:T(8,128)(2,1)} %get-tuple-element.150.q, bf16[1536,768]{1,0:T(8,128)(2,1)} %get-tuple-element.151.k, bf16[1536,768]{1,0:T(8,128)(2,1)} %get-tuple-element.152.v, ...), custom_call_target="tpu_custom_call" | custom-call | flops 10871635968 | bytes 8388608 | tf_op jit(solution)/shard_map/pallas_call | solution.py:863
  494.7 2.2 fusion.28.refs_28_
  497.0 3.9 collective-permute-start.2
  509.1 2.7 fusion.10
  519.9 194.9 %shard_map.613 = (f32[2,2,2,48,192]{4,3,2,1,0:T(8,128)}, f32[2,48,768]{2,1,0:T(8,128)}, f32[2,48,192]{2,1,0:T(8,128)}, f32[2,48,192]{2,1,0:T(8,128)}, f32[2,48,1...) custom-call(bf16[4,112,768]{2,1,0:T(8,128)(2,1)} %copy-done.1, ...), custom_call_target="tpu_custom_call" | custom-call | tf_op jit(solution)/shard_map/pallas_call | solution.py:546
  721.4 2.3 copy.343
  723.7 2.6 reshape.742
  726.4 2.4 copy.344
  730.3 11.5 %fusion = f32[3264,192]{0,1:T(8,128)} fusion(bf16[3584,192]{0,1:T(8,128)(2,1)S(1)} %copy-done.37, s32[3584]{0:T(1024)S(1)} %copy-done.81), kind=kOutput, calls=%fused_computation.1 | convolution fusion | flops 4503797760 | bytes 3897344 | tf_op jit(solution)/shard_map/dot_general | solution.py:25
  (417 shorter events, 127.5 us)
Async XLA Ops:
  7.2 15.2 %copy-start.62 = (bf16[1,112,768]{2,1,0:T(8,128)(2,1)S(1)}, bf16[1,112,768]{2,1,0:T(8,128)(2,1)}, u32[]{:S(2)}) copy-start(bf16[1,112,768]{2,1,0:T(8,128)(2,1)} %param.71) | copy-start | bytes 516100
  8.1 22.0 %collective-permute-start = (bf16[2,80]{0,1:T(8,128)(2,1)S(1)}, bf16[2,80]{0,1:T(8,128)(2,1)S(1)}, u32[]{:S(2)}, u32[]{:S(2)}) collective-permute-start(bf16[2,80]{0,1:T(8,128)(2,1)S(1)} %get-tuple-element.455), channel_id=1, source_target_pairs={{0,1},{1,2},{2,3},{4,5},{5,6},{6,7},{8,9},{9,10},{10,11},{12,13},{... | collective-permute-start | bytes 968 | tf_op jit(solution)/shard_map/ppermute | solution.py:111
  12.6 17.5 %collective-permute-start.1 = (bf16[2,80]{0,1:T(8,128)(2,1)S(1)}, bf16[2,80]{0,1:T(8,128)(2,1)S(1)}, u32[]{:S(2)}, u32[]{:S(2)}) collective-permute-start(bf16[2,80]{0,1:T(8,128)(2,1)S(1)} %get-tuple-element.456), channel_id=1, source_target_pairs={{1,0},{2,1},{3,2},{5,4},{6,5},{7,6},{9,8},{10,9},{11,10},{13,12},{... | collective-permute-start | bytes 968 | tf_op jit(solution)/shard_map/ppermute | solution.py:111
  266.2 10.7 %copy-start.18 = (bf16[4,2,2,48,768]{4,3,2,1,0:T(8,128)(2,1)S(1)}, bf16[4,2,2,48,768]{4,3,2,1,0:T(8,128)(2,1)}, u32[]{:S(2)}) copy-start(bf16[4,2,2,48,768]{4,3,2,1,0:T(8,128)(2,1)} %get-tuple-element.126) | copy-start | bytes 3538948
  332.9 6.9 copy-start.5
  361.7 31.2 %copy-start.54 = (bf16[4,2,2,48,768]{4,3,2,1,0:T(8,128)(2,1)S(1)}, bf16[4,2,2,48,768]{4,3,2,1,0:T(8,128)(2,1)}, u32[]{:S(2)}) copy-start(bf16[4,2,2,48,768]{4,3,2,1,0:T(8,128)(2,1)} %get-tuple-element.134) | copy-start | bytes 3538948
  398.1 19.2 %copy-start.43 = (bf16[4,2,2,48,768]{4,3,2,1,0:T(8,128)(2,1)S(1)}, bf16[4,2,2,48,768]{4,3,2,1,0:T(8,128)(2,1)}, u32[]{:S(2)}) copy-start(bf16[4,2,2,48,768]{4,3,2,1,0:T(8,128)(2,1)} %get-tuple-element.122) | copy-start | bytes 3538948
  440.5 66.6 %all-to-all-start = ((bf16[4,112,192]{1,2,0:T(8,128)(2,1)}), bf16[4,112,192]{1,2,0:T(8,128)(2,1)}, u32[]{:S(2)}, u32[]{:S(2)}) async-start(bf16[4,112,192]{1,2,0:T(8,128)(2,1)} %bitcast.78), calls=%async_computation | async-start | bytes 393216 | tf_op jit(solution)/shard_map/all_to_all | solution.py:1641
  444.5 276.9 %all-gather.3.cloned.1.call-start = ((), (), s32[]{:S(2)}) async-start(), calls=%async_computation.1 | async-start | bytes 1769472 | tf_op jit(solution)/shard_map/all_gather | solution.py:1627
  446.1 43.2 %copy-start.49 = (bf16[4,2,2,48,768]{4,3,2,1,0:T(8,128)(2,1)S(1)}, bf16[4,2,2,48,768]{4,3,2,1,0:T(8,128)(2,1)}, u32[]{:S(2)}) copy-start(bf16[4,2,2,48,768]{4,3,2,1,0:T(8,128)(2,1)} %get-tuple-element.155) | copy-start | bytes 3538948
  494.6 8.5 %copy-start.78 = (bf16[1,4,2,2,2,24]{5,4,3,2,1,0:T(2,128)(2,1)S(1)}, bf16[1,4,2,2,2,24]{5,4,3,2,1,0:T(2,128)(2,1)}, u32[]{:S(2)}) copy-start(bf16[1,4,2,2,2,24]{5,4,3,2,1,0:T(2,128)(2,1)} %stack.111) | copy-start | bytes 4612
  494.6 8.5 %copy-start.77 = (bf16[1,4,2,2,2,24]{5,4,3,2,1,0:T(2,128)(2,1)S(1)}, bf16[1,4,2,2,2,24]{5,4,3,2,1,0:T(2,128)(2,1)}, u32[]{:S(2)}) copy-start(bf16[1,4,2,2,2,24]{5,4,3,2,1,0:T(2,128)(2,1)} %stack.112) | copy-start | bytes 4612
  494.6 8.5 %copy-start.75 = (s32[2,2,4,2,56]{4,3,2,1,0:T(2,128)S(1)}, s32[2,2,4,2,56]{4,3,2,1,0:T(2,128)}, u32[]{:S(2)}) copy-start(s32[2,2,4,2,56]{4,3,2,1,0:T(2,128)} %get-tuple-element.420) | copy-start | bytes 21508
  494.6 8.5 %copy-start.76 = (s32[2,2,4,2,56]{4,3,2,1,0:T(2,128)S(1)}, s32[2,2,4,2,56]{4,3,2,1,0:T(2,128)}, u32[]{:S(2)}) copy-start(s32[2,2,4,2,56]{4,3,2,1,0:T(2,128)} %get-tuple-element.421) | copy-start | bytes 21508
  496.9 9.4 %copy-start.16 = (bf16[384,768]{1,0:T(8,128)(2,1)}, bf16[384,768]{1,0:T(8,128)(2,1)S(1)}, u32[]{:S(2)}) copy-start(bf16[384,768]{1,0:T(8,128)(2,1)S(1)} %fusion.28.refs_28_) | copy-start | bytes 1769476
  497.0 9.3 %collective-permute-start.2 = (bf16[1,768]{1,0:T(2,128)(2,1)S(1)}, bf16[1,768]{1,0:T(2,128)(2,1)S(1)}, u32[]{:S(2)}, u32[]{:S(2)}) collective-permute-start(bf16[1,768]{1,0:T(2,128)(2,1)S(1)} %get-tuple-element.446), channel_id=1, source_target_pairs={{0,1},{1,2},{2,3},{4,5},{5,6},{6,7},{8,9},{9,10},{10,11},{12,13},{... | collective-permute-start | bytes 4616 | tf_op jit(solution)/shard_map/ppermute | solution.py:111
  500.9 5.4 collective-permute-start.3
  730.3 11.6 %copy-start.61 = (f32[3,2,48,192]{3,2,1,0:T(8,128)S(1)}, f32[3,2,48,192]{3,2,1,0:T(8,128)}, u32[]{:S(2)}) copy-start(f32[3,2,48,192]{3,2,1,0:T(8,128)} %get-tuple-element.187) | copy-start | bytes 663556
  730.3 12.3 %copy-start.74 = (f32[2,48,192]{2,1,0:T(8,128)S(1)}, f32[2,48,192]{2,1,0:T(8,128)}, u32[]{:S(2)}) copy-start(f32[2,48,192]{2,1,0:T(8,128)} %get-tuple-element.188) | copy-start | bytes 221188
  730.3 13.0 %copy-start.73 = (f32[2,48,192]{2,1,0:T(8,128)S(1)}, f32[2,48,192]{2,1,0:T(8,128)}, u32[]{:S(2)}) copy-start(f32[2,48,192]{2,1,0:T(8,128)} %get-tuple-element.189) | copy-start | bytes 221188
  730.3 13.6 %copy-start.72 = (f32[2,48,192]{2,1,0:T(8,128)S(1)}, f32[2,48,192]{2,1,0:T(8,128)}, u32[]{:S(2)}) copy-start(f32[2,48,192]{2,1,0:T(8,128)} %get-tuple-element.190) | copy-start | bytes 221188
  742.6 6.5 copy-start.65
  743.3 6.5 copy-start.64
  743.9 6.5 copy-start.63
  (78 other events, 153.9 us)
Sparse Core Ops, SparseCore 0:
  509.2 55.4 all-gather.2
